TPU v7x, 256 devices: a whole 4x4x8 slice. The times are simulated.
256 devices in a mesh: row: 16 (over y, z_hi), col: 8 (over x, core), gz: 2 (over z_lo).
Axes of the slice: x: 4, y: 4, z: 8 (z_hi: 4, z_lo: 2; z = z_hi * 2 + z_lo), core: 2. Of those that a mesh axis runs over, the one named last changes fastest.
Arguments:
- source: float32 [2, 4, 1024, 1024], P(None, 'gz', 'row', 'col'), may hold values from -24 to 24
- cell_class: int32 [4, 1024, 1024], P('gz', 'row', 'col'), may hold values from 0 to 7
- coeff_table: float32 [8], replicated, may hold values from 0.5 to 8
- owner_cell: int32 [32768], P(('row', 'col', 'gz')), may hold values from 0 to 16383
- node_pos: float32 [3, 32768], P(None, ('row', 'col', 'gz')), may hold values from 0 to 1
- node_weight: float32 [32768], P(('row', 'col', 'gz')), may hold values from 0.002 to 0.02
Outputs:
- potential: float32 [2, 4, 1024, 1024], P(None, 'gz', 'row', 'col')
- boundary_values: float32 [2, 32768], P(None, ('row', 'col', 'gz'))
Inputs may be any that keep to these rules, and one draw needn't show every extreme that they name: `owner_cell`: each boundary node names a cell of its own device's tile, a flat index over 2 x 64 x 128 cells with the layer slowest.
All inputs are finite; a program needn't handle non-finite values.
Results may differ from a plain program's by a relative error of at most 0.0003.
Values sent between devices are 32-bit elements; how exact they have to be, the bound alone decides.
No kernel may reach another device: no remote copies, remote signals or barrier semaphores. Data moves between devices by JAX's collectives and lax.ppermute only.
A program may use at most 64 MiB of HBM per device.

v0:
```python
import jax
import jax.numpy as jnp
from jax import lax
from jax.sharding import PartitionSpec as P

SWEEPS = 4


OMEGA = 0.8
RELAX = 0.5
SOFTEN = 0.01


def extended(shard, sides, width):
    for axis, dim in sides:
        size, length = (lax.axis_size(axis), shard.shape[dim])
        up = [(i, (i + 1) % size) for i in range(size - 1)]
        down = [(j, i) for i, j in up]
        last = lax.slice_in_dim(shard, length - width, length, axis=dim)
        leading = lax.slice_in_dim(shard, 0, width, axis=dim)
        before = lax.ppermute(last, axis, up)
        after = lax.ppermute(leading, axis, down)
        shard = jnp.concatenate([before, shard, after], axis=dim)
    return shard


def lookup_diagonal(cell_class, coeff_table):
    summed = jnp.zeros(cell_class.shape, jnp.float32)
    for class_level in range(coeff_table.shape[0]):
        summed = summed + jnp.where(
            cell_class == class_level, coeff_table[class_level], jnp.zeros((), coeff_table.dtype)
        )
    return 6.0 + summed


def stencil_update(padded, field, forcing, diagonal):
    beside = padded[:, 2:, 1:-1, 1:-1] + padded[:, :-2, 1:-1, 1:-1]
    beside = beside + padded[:, 1:-1, 2:, 1:-1] + padded[:, 1:-1, :-2, 1:-1]
    beside = beside + padded[:, 1:-1, 1:-1, 2:] + padded[:, 1:-1, 1:-1, :-2]
    return field + OMEGA * (forcing - (diagonal * field - beside)) / diagonal


def sweep_once(field, forcing, diagonal):
    padded = extended(field, (("row", 2), ("col", 3), ("gz", 1)), 1)
    return stencil_update(padded, field, forcing, diagonal)


def on_device(source, cell_class, coeff_table, owner_cell, node_pos, node_weight):
    images, depth, rows_x, cols_y = source.shape
    cell_count = depth * rows_x * cols_y
    node_count = owner_cell.shape[0]
    diagonal = lookup_diagonal(cell_class, coeff_table)

    def relax_all(field, forcing):
        for repeat in range(SWEEPS):
            field = sweep_once(field, forcing, diagonal)
        return field

    target_pos = lax.all_gather(node_pos, ("col", "gz"), axis=1, tiled=True)
    source_meta = lax.all_gather(
        jnp.concatenate([node_pos, node_weight[None, :]], 0), "row", axis=1, tiled=True
    )
    target_count = target_pos.shape[1]
    block_rows = min(512, target_count)
    target_blocks = target_pos.reshape(3, target_count // block_rows, block_rows).transpose(1, 0, 2)

    def kernel_apply(piece_traces):

        def block_sum(target):
            diff_x = target[0][:, None] - source_meta[0][None, :]
            diff_y = target[1][:, None] - source_meta[1][None, :]
            diff_z = target[2][:, None] - source_meta[2][None, :]
            inverse = lax.rsqrt(diff_x * diff_x + diff_y * diff_y + diff_z * diff_z + SOFTEN)
            kernel = source_meta[3][None, :] * diff_z * inverse * inverse * inverse
            return lax.dot_general(
                piece_traces,
                kernel,
                (((1,), (1,)), ((), ())),
                precision=lax.Precision.HIGHEST,
                preferred_element_type=jnp.float32,
            )

        pieces = lax.map(block_sum, target_blocks)
        return pieces.transpose(1, 0, 2).reshape(images, target_count)

    def fk_round(forcing, first, second):
        first = relax_all(first, forcing)
        trace = jnp.take(first.reshape(images, cell_count), owner_cell, axis=1)
        partial_sums = kernel_apply(lax.all_gather(trace, "row", axis=1, tiled=True))
        whole_sums = lax.psum(partial_sums, ("col", "gz"))
        summed = lax.dynamic_slice_in_dim(
            whole_sums, lax.axis_index(("col", "gz")) * node_count, node_count, 1
        )
        values = -0.5 * trace + summed
        spread = (
            jnp.zeros((images, cell_count), jnp.float32)
            .at[:, owner_cell]
            .add(values)
            .reshape(source.shape)
        )
        second = relax_all(second, spread)
        return (first, second, values)

    first = jnp.zeros(source.shape, jnp.float32)
    second = jnp.zeros(source.shape, jnp.float32)
    first, second, values = fk_round(source, first, second)
    forcing = source - RELAX * (first + second)
    first, second, values = fk_round(forcing, first, second)
    return (first + second, values)


def solution(mesh):
    return jax.shard_map(
        on_device,
        mesh=mesh,
        in_specs=(
            P(None, "gz", "row", "col"),
            P("gz", "row", "col"),
            P(),
            P(("row", "col", "gz")),
            P(None, ("row", "col", "gz")),
            P(("row", "col", "gz")),
        ),
        out_specs=(P(None, "gz", "row", "col"), P(None, ("row", "col", "gz"))),
        check_vma=False,
    )
```

profile of v0, /device:TPU:8, one launch (start us, length us, event | category | flops | bytes accessed | tf_op | source)
XLA Modules:
  0.0 788.1 jit_solution(11103989547739344262)
XLA Ops:
  26.6 6.0 broadcast_multiply_fusion
  33.8 6.0 collective-permute-start.6
  67.0 5.5 collective-permute-start.13
  89.3 38.5 %all_gather.12 = f32[4,2048]{1,0:T(4,128)S(1)} all-gather(f32[4,128]{1,0:T(4,128)S(1)} %pad_maximum_fusion.298), channel_id=1, replica_groups=mesh['row'=16,'col'=8,'gz'=2] {'row'}, dimensions={1}, use_global_device_ids=true | all-gather | bytes 34816 | tf_op jit(solution)/shard_map/all_gather | solution.py:60
  130.0 6.9 collective-permute-start.19
  137.0 26.3 %all_gather.13 = f32[3,2048]{1,0:T(4,128)S(1)} all-gather(f32[3,128]{1,0:T(4,128)S(1)} %copy-done.1), channel_id=1, replica_groups=mesh['row'=16,'col'=8,'gz'=2] {'col','gz'}, dimensions={1}, use_global_device_ids=true | all-gather | bytes 26112 | tf_op jit(solution)/shard_map/all_gather | solution.py:59
  186.0 44.9 %all_gather.14 = f32[2,2048]{0,1:T(8,128)S(1)} all-gather(f32[2,128]{0,1:T(8,128)S(1)} %select_bitcast_fusion.1), channel_id=1, replica_groups=mesh['row'=16,'col'=8,'gz'=2] {'row'}, dimensions={1}, use_global_device_ids=true | all-gather | bytes 17408 | tf_op jit(solution)/shard_map/all_gather | solution.py:89
  231.2 22.4 %while.20 = (s32[]{:T(128)}, f32[4,2,512]{2,1,0:T(2,128)S(1)}, f32[4,2048]{1,0:T(4,128)S(1)}, f32[4,3,512]{2,1,0:T(4,128)S(1)}, f32[2,2048]{1,0:T(2,128)S(1)}, /*index=5*/s32[]{:T(128)}, s32[]{:T(128)}, s32[]{}, s32[]{}) while((s32[]{:T(128)}, f32[4,2,512]{2,1,0:T(2,128)S(1)}, f32[4,2048]{1,0:T(4,128)S(1)}, f32[4,3,512]{2,1,0:T(4,128)S(1)}, ...), condition=%wide.region_1.3_spmd, body=%wide.region_0.2_spmd.sunk | while | flops 38797316 | bytes 137349 | solution.py:83
  231.3 5.5 fusion.246
  236.9 5.5 fusion.246
  242.5 5.5 fusion.246
  248.1 5.5 fusion.246
  254.0 83.4 %psum.14 = f32[2,2048]{0,1:T(8,128)S(1)} all-reduce(f32[2,2048]{0,1:T(8,128)S(1)} %bitcast.103), channel_id=1, replica_groups=mesh['row'=16,'col'=8,'gz'=2] {'col','gz'}, use_global_device_ids=true, to_apply=%region_2.4 | all-reduce | flops 4096 | bytes 32768 | tf_op jit(solution)/shard_map/psum | solution.py:90
  352.6 7.5 collective-permute-start.25
  377.8 6.9 collective-permute-start.31
  386.7 6.9 collective-permute-start.43
  414.2 6.9 collective-permute-start.37
  442.9 6.9 collective-permute-start.49
  455.4 6.8 collective-permute-done.51
  473.9 6.4 collective-permute-start.55
  506.7 6.8 collective-permute-start.61
  518.3 6.6 collective-permute-start.62
  550.5 44.2 %all_gather.15 = f32[2,2048]{0,1:T(8,128)S(1)} all-gather(f32[2,128]{0,1:T(8,128)S(1)} %select_bitcast_fusion), channel_id=1, replica_groups=mesh['row'=16,'col'=8,'gz'=2] {'row'}, dimensions={1}, use_global_device_ids=true | all-gather | bytes 17408 | tf_op jit(solution)/shard_map/all_gather | solution.py:89
  595.0 22.4 %while.21 = (s32[]{:T(128)}, f32[4,2,512]{2,1,0:T(2,128)S(1)}, f32[4,2048]{1,0:T(4,128)S(1)}, f32[4,3,512]{2,1,0:T(4,128)S(1)}, f32[2,2048]{1,0:T(2,128)S(1)}, /*index=5*/s32[]{:T(128)}, s32[]{:T(128)}, s32[]{}, s32[]{}) while((s32[]{:T(128)}, f32[4,2,512]{2,1,0:T(2,128)S(1)}, f32[4,2048]{1,0:T(4,128)S(1)}, f32[4,3,512]{2,1,0:T(4,128)S(1)}, ...), condition=%wide.region_5.7_spmd, body=%wide.region_4.6_spmd.sunk | while | flops 38797316 | bytes 137349 | solution.py:83
  595.1 5.5 fusion.249
  600.7 5.5 fusion.249
  606.3 5.5 fusion.249
  611.9 5.5 fusion.249
  617.8 77.3 %psum.15 = f32[2,2048]{0,1:T(8,128)S(1)} all-reduce(f32[2,2048]{0,1:T(8,128)S(1)} %bitcast.104), channel_id=1, replica_groups=mesh['row'=16,'col'=8,'gz'=2] {'col','gz'}, use_global_device_ids=true, to_apply=%region_6.8 | all-reduce | flops 4096 | bytes 32768 | tf_op jit(solution)/shard_map/psum | solution.py:90
  705.6 5.5 collective-permute-start.72
  735.2 5.4 collective-permute-start.79
  756.6 5.9 collective-permute-start.84
  (303 shorter events, 323.5 us)
Async XLA Ops:
  0.7 10.2 %collective-permute-start = (f32[2,2,1,128]{3,2,1,0:T(1,128)S(1)}, f32[2,2,1,128]{3,2,1,0:T(1,128)S(1)}, u32[]{:S(2)}, u32[]{:S(2)}) collective-permute-start(f32[2,2,1,128]{3,2,1,0:T(1,128)S(1)} %broadcast.39), channel_id=1, source_target_pairs={{0,16},{16,32},{32,48},{48,64},{64,80},{80,96},{96,112},{112,128},... | collective-permute-start | bytes 6152 | tf_op jit(solution)/shard_map/ppermute | solution.py:21
  20.8 11.8 %collective-permute-start.4 = (f32[2,1,66,130]{3,2,1,0:T(8,128)S(1)}, f32[2,1,66,130]{3,2,1,0:T(8,128)S(1)}, u32[]{:S(2)}, u32[]{:S(2)}) collective-permute-start(f32[2,1,66,130]{3,2,1,0:T(8,128)S(1)} %get-tuple-element.140), channel_id=1, source_target_pairs={{1,0},{3,2},{5,4},{7,6},{9,8},{11,10},{13,12},{15,14},{17,16},{19,... | collective-permute-start | bytes 205928 | tf_op jit(solution)/shard_map/ppermute | solution.py:22
  22.1 10.6 %collective-permute-start.5 = (f32[2,1,66,130]{3,2,1,0:T(8,128)S(1)}, f32[2,1,66,130]{3,2,1,0:T(8,128)S(1)}, u32[]{:S(2)}, u32[]{:S(2)}) collective-permute-start(f32[2,1,66,130]{3,2,1,0:T(8,128)S(1)} %get-tuple-element.141), channel_id=1, source_target_pairs={{0,1},{2,3},{4,5},{6,7},{8,9},{10,11},{12,13},{14,15},{16,17},{18,... | collective-permute-start | bytes 205928 | tf_op jit(solution)/shard_map/ppermute | solution.py:21
  83.4 44.4 %collective-permute-start.16 = (f32[2,1,66,130]{3,2,1,0:T(8,128)S(1)}, f32[2,1,66,130]{3,2,1,0:T(8,128)S(1)}, u32[]{:S(2)}, u32[]{:S(2)}) collective-permute-start(f32[2,1,66,130]{3,2,1,0:T(8,128)S(1)} %get-tuple-element.136), channel_id=1, source_target_pairs={{1,0},{3,2},{5,4},{7,6},{9,8},{11,10},{13,12},{15,14},{17,16},{19,... | collective-permute-start | bytes 205928 | tf_op jit(solution)/shard_map/ppermute | solution.py:22
  84.7 43.2 %collective-permute-start.17 = (f32[2,1,66,130]{3,2,1,0:T(8,128)S(1)}, f32[2,1,66,130]{3,2,1,0:T(8,128)S(1)}, u32[]{:S(2)}, u32[]{:S(2)}) collective-permute-start(f32[2,1,66,130]{3,2,1,0:T(8,128)S(1)} %get-tuple-element.137), channel_id=1, source_target_pairs={{0,1},{2,3},{4,5},{6,7},{8,9},{10,11},{12,13},{14,15},{16,17},{18,... | collective-permute-start | bytes 205928 | tf_op jit(solution)/shard_map/ppermute | solution.py:21
  128.1 35.2 %collective-permute-start.18 = (f32[2,2,1,128]{3,2,1,0:T(1,128)S(1)}, f32[2,2,1,128]{3,2,1,0:T(1,128)S(1)}, u32[]{:S(2)}, u32[]{:S(2)}) collective-permute-start(f32[2,2,1,128]{3,2,1,0:T(1,128)S(1)} %get-tuple-element.194), channel_id=1, source_target_pairs={{0,16},{16,32},{32,48},{48,64},{64,80},{80,96},{96,112},{112,128},... | collective-permute-start | bytes 6152 | tf_op jit(solution)/shard_map/ppermute | solution.py:21
  130.0 33.2 %collective-permute-start.19 = (f32[2,2,1,128]{3,2,1,0:T(1,128)S(1)}, f32[2,2,1,128]{3,2,1,0:T(1,128)S(1)}, u32[]{:S(2)}, u32[]{:S(2)}) collective-permute-start(f32[2,2,1,128]{3,2,1,0:T(1,128)S(1)} %get-tuple-element.195), channel_id=1, source_target_pairs={{16,0},{32,16},{48,32},{64,48},{80,64},{96,80},{112,96},{128,112},... | collective-permute-start | bytes 6152 | tf_op jit(solution)/shard_map/ppermute | solution.py:22
  347.6 12.5 %collective-permute-start.24 = (f32[2,2,1,128]{3,2,1,0:T(1,128)S(1)}, f32[2,2,1,128]{3,2,1,0:T(1,128)S(1)}, u32[]{:S(2)}, u32[]{:S(2)}) collective-permute-start(f32[2,2,1,128]{3,2,1,0:T(1,128)S(1)} %get-tuple-element.190), channel_id=1, source_target_pairs={{0,16},{16,32},{32,48},{48,64},{64,80},{80,96},{96,112},{112,128},... | collective-permute-start | bytes 6152 | tf_op jit(solution)/shard_map/ppermute | solution.py:21
  375.9 17.8 %collective-permute-start.30 = (f32[2,2,1,128]{3,2,1,0:T(1,128)S(1)}, f32[2,2,1,128]{3,2,1,0:T(1,128)S(1)}, u32[]{:S(2)}, u32[]{:S(2)}) collective-permute-start(f32[2,2,1,128]{3,2,1,0:T(1,128)S(1)} %get-tuple-element.188), channel_id=1, source_target_pairs={{0,16},{16,32},{32,48},{48,64},{64,80},{80,96},{96,112},{112,128},... | collective-permute-start | bytes 6152 | tf_op jit(solution)/shard_map/ppermute | solution.py:21
  377.8 15.8 %collective-permute-start.31 = (f32[2,2,1,128]{3,2,1,0:T(1,128)S(1)}, f32[2,2,1,128]{3,2,1,0:T(1,128)S(1)}, u32[]{:S(2)}, u32[]{:S(2)}) collective-permute-start(f32[2,2,1,128]{3,2,1,0:T(1,128)S(1)} %get-tuple-element.189), channel_id=1, source_target_pairs={{16,0},{32,16},{48,32},{64,48},{80,64},{96,80},{112,96},{128,112},... | collective-permute-start | bytes 6152 | tf_op jit(solution)/shard_map/ppermute | solution.py:22
  384.8 11.6 %collective-permute-start.42 = (f32[2,2,1,128]{3,2,1,0:T(1,128)S(1)}, f32[2,2,1,128]{3,2,1,0:T(1,128)S(1)}, u32[]{:S(2)}, u32[]{:S(2)}) collective-permute-start(f32[2,2,1,128]{3,2,1,0:T(1,128)S(1)} %get-tuple-element.192), channel_id=1, source_target_pairs={{0,16},{16,32},{32,48},{48,64},{64,80},{80,96},{96,112},{112,128},... | collective-permute-start | bytes 6152 | tf_op jit(solution)/shard_map/ppermute | solution.py:21
  386.7 9.7 %collective-permute-start.43 = (f32[2,2,1,128]{3,2,1,0:T(1,128)S(1)}, f32[2,2,1,128]{3,2,1,0:T(1,128)S(1)}, u32[]{:S(2)}, u32[]{:S(2)}) collective-permute-start(f32[2,2,1,128]{3,2,1,0:T(1,128)S(1)} %get-tuple-element.193), channel_id=1, source_target_pairs={{16,0},{32,16},{48,32},{64,48},{80,64},{96,80},{112,96},{128,112},... | collective-permute-start | bytes 6152 | tf_op jit(solution)/shard_map/ppermute | solution.py:22
  399.5 12.4 %collective-permute-start.34 = (f32[2,1,66,130]{3,2,1,0:T(8,128)S(1)}, f32[2,1,66,130]{3,2,1,0:T(8,128)S(1)}, u32[]{:S(2)}, u32[]{:S(2)}) collective-permute-start(f32[2,1,66,130]{3,2,1,0:T(8,128)S(1)} %get-tuple-element.128), channel_id=1, source_target_pairs={{1,0},{3,2},{5,4},{7,6},{9,8},{11,10},{13,12},{15,14},{17,16},{19,... | collective-permute-start | bytes 205928 | tf_op jit(solution)/shard_map/ppermute | solution.py:22
  400.8 11.2 %collective-permute-start.35 = (f32[2,1,66,130]{3,2,1,0:T(8,128)S(1)}, f32[2,1,66,130]{3,2,1,0:T(8,128)S(1)}, u32[]{:S(2)}, u32[]{:S(2)}) collective-permute-start(f32[2,1,66,130]{3,2,1,0:T(8,128)S(1)} %get-tuple-element.129), channel_id=1, source_target_pairs={{0,1},{2,3},{4,5},{6,7},{8,9},{10,11},{12,13},{14,15},{16,17},{18,... | collective-permute-start | bytes 205928 | tf_op jit(solution)/shard_map/ppermute | solution.py:21
  405.5 15.6 %collective-permute-start.44 = (f32[2,2,66,1]{3,2,1,0:T(8,128)S(1)}, f32[2,2,66,1]{3,2,1,0:T(8,128)S(1)}, u32[]{:S(2)}, u32[]{:S(2)}) collective-permute-start(f32[2,2,66,1]{3,2,1,0:T(8,128)S(1)} %get-tuple-element.163), channel_id=1, source_target_pairs={{0,2},{2,4},{4,6},{6,8},{8,10},{10,12},{12,14},{1,3},{3,5},{5,7},{... | collective-permute-start | bytes 3176 | tf_op jit(solution)/shard_map/ppermute | solution.py:21
  410.7 10.5 %collective-permute-start.45 = (f32[2,2,66,1]{3,2,1,0:T(8,128)S(1)}, f32[2,2,66,1]{3,2,1,0:T(8,128)S(1)}, u32[]{:S(2)}, u32[]{:S(2)}) collective-permute-start(f32[2,2,66,1]{3,2,1,0:T(8,128)S(1)} %get-tuple-element.162), channel_id=1, source_target_pairs={{2,0},{4,2},{6,4},{8,6},{10,8},{12,10},{14,12},{3,1},{5,3},{7,5},{... | collective-permute-start | bytes 3176 | tf_op jit(solution)/shard_map/ppermute | solution.py:22
  425.8 12.0 %collective-permute-start.46 = (f32[2,1,66,130]{3,2,1,0:T(8,128)S(1)}, f32[2,1,66,130]{3,2,1,0:T(8,128)S(1)}, u32[]{:S(2)}, u32[]{:S(2)}) collective-permute-start(f32[2,1,66,130]{3,2,1,0:T(8,128)S(1)} %get-tuple-element.132), channel_id=1, source_target_pairs={{1,0},{3,2},{5,4},{7,6},{9,8},{11,10},{13,12},{15,14},{17,16},{19,... | collective-permute-start | bytes 205928 | tf_op jit(solution)/shard_map/ppermute | solution.py:22
  427.1 10.7 %collective-permute-start.47 = (f32[2,1,66,130]{3,2,1,0:T(8,128)S(1)}, f32[2,1,66,130]{3,2,1,0:T(8,128)S(1)}, u32[]{:S(2)}, u32[]{:S(2)}) collective-permute-start(f32[2,1,66,130]{3,2,1,0:T(8,128)S(1)} %get-tuple-element.133), channel_id=1, source_target_pairs={{0,1},{2,3},{4,5},{6,7},{8,9},{10,11},{12,13},{14,15},{16,17},{18,... | collective-permute-start | bytes 205928 | tf_op jit(solution)/shard_map/ppermute | solution.py:21
  471.2 9.1 %collective-permute-start.54 = (f32[2,2,1,128]{3,2,1,0:T(1,128)S(1)}, f32[2,2,1,128]{3,2,1,0:T(1,128)S(1)}, u32[]{:S(2)}, u32[]{:S(2)}) collective-permute-start(f32[2,2,1,128]{3,2,1,0:T(1,128)S(1)} %get-tuple-element.182), channel_id=1, source_target_pairs={{0,16},{16,32},{32,48},{48,64},{64,80},{80,96},{96,112},{112,128},... | collective-permute-start | bytes 6152 | tf_op jit(solution)/shard_map/ppermute | solution.py:21
  481.7 13.9 %collective-permute-start.56 = (f32[2,2,66,1]{3,2,1,0:T(8,128)S(1)}, f32[2,2,66,1]{3,2,1,0:T(8,128)S(1)}, u32[]{:S(2)}, u32[]{:S(2)}) collective-permute-start(f32[2,2,66,1]{3,2,1,0:T(8,128)S(1)} %get-tuple-element.153), channel_id=1, source_target_pairs={{0,2},{2,4},{4,6},{6,8},{8,10},{10,12},{12,14},{1,3},{3,5},{5,7},{... | collective-permute-start | bytes 3176 | tf_op jit(solution)/shard_map/ppermute | solution.py:21
  485.5 10.2 %collective-permute-start.57 = (f32[2,2,66,1]{3,2,1,0:T(8,128)S(1)}, f32[2,2,66,1]{3,2,1,0:T(8,128)S(1)}, u32[]{:S(2)}, u32[]{:S(2)}) collective-permute-start(f32[2,2,66,1]{3,2,1,0:T(8,128)S(1)} %get-tuple-element.152), channel_id=1, source_target_pairs={{2,0},{4,2},{6,4},{8,6},{10,8},{12,10},{14,12},{3,1},{5,3},{7,5},{... | collective-permute-start | bytes 3176 | tf_op jit(solution)/shard_map/ppermute | solution.py:22
  486.8 15.0 %collective-permute-start.66 = (f32[2,2,1,128]{3,2,1,0:T(1,128)S(1)}, f32[2,2,1,128]{3,2,1,0:T(1,128)S(1)}, u32[]{:S(2)}, u32[]{:S(2)}) collective-permute-start(f32[2,2,1,128]{3,2,1,0:T(1,128)S(1)} %get-tuple-element.178), channel_id=1, source_target_pairs={{0,16},{16,32},{32,48},{48,64},{64,80},{80,96},{96,112},{112,128},... | collective-permute-start | bytes 6152 | tf_op jit(solution)/shard_map/ppermute | solution.py:21
  490.9 10.8 %collective-permute-start.67 = (f32[2,2,1,128]{3,2,1,0:T(1,128)S(1)}, f32[2,2,1,128]{3,2,1,0:T(1,128)S(1)}, u32[]{:S(2)}, u32[]{:S(2)}) collective-permute-start(f32[2,2,1,128]{3,2,1,0:T(1,128)S(1)} %get-tuple-element.179), channel_id=1, source_target_pairs={{16,0},{32,16},{48,32},{64,48},{80,64},{96,80},{112,96},{128,112},... | collective-permute-start | bytes 6152 | tf_op jit(solution)/shard_map/ppermute | solution.py:22
  504.7 13.5 %collective-permute-start.60 = (f32[2,2,1,128]{3,2,1,0:T(1,128)S(1)}, f32[2,2,1,128]{3,2,1,0:T(1,128)S(1)}, u32[]{:S(2)}, u32[]{:S(2)}) collective-permute-start(f32[2,2,1,128]{3,2,1,0:T(1,128)S(1)} %get-tuple-element.180), channel_id=1, source_target_pairs={{0,16},{16,32},{32,48},{48,64},{64,80},{80,96},{96,112},{112,128},... | collective-permute-start | bytes 6152 | tf_op jit(solution)/shard_map/ppermute | solution.py:21
  506.7 11.4 %collective-permute-start.61 = (f32[2,2,1,128]{3,2,1,0:T(1,128)S(1)}, f32[2,2,1,128]{3,2,1,0:T(1,128)S(1)}, u32[]{:S(2)}, u32[]{:S(2)}) collective-permute-start(f32[2,2,1,128]{3,2,1,0:T(1,128)S(1)} %get-tuple-element.181), channel_id=1, source_target_pairs={{16,0},{32,16},{48,32},{64,48},{80,64},{96,80},{112,96},{128,112},... | collective-permute-start | bytes 6152 | tf_op jit(solution)/shard_map/ppermute | solution.py:22
  513.7 12.6 %collective-permute-start.68 = (f32[2,2,66,1]{3,2,1,0:T(8,128)S(1)}, f32[2,2,66,1]{3,2,1,0:T(8,128)S(1)}, u32[]{:S(2)}, u32[]{:S(2)}) collective-permute-start(f32[2,2,66,1]{3,2,1,0:T(8,128)S(1)} %get-tuple-element.149), channel_id=1, source_target_pairs={{0,2},{2,4},{4,6},{6,8},{8,10},{10,12},{12,14},{1,3},{3,5},{5,7},{... | collective-permute-start | bytes 3176 | tf_op jit(solution)/shard_map/ppermute | solution.py:21
  516.9 9.4 %collective-permute-start.69 = (f32[2,2,66,1]{3,2,1,0:T(8,128)S(1)}, f32[2,2,66,1]{3,2,1,0:T(8,128)S(1)}, u32[]{:S(2)}, u32[]{:S(2)}) collective-permute-start(f32[2,2,66,1]{3,2,1,0:T(8,128)S(1)} %get-tuple-element.148), channel_id=1, source_target_pairs={{2,0},{4,2},{6,4},{8,6},{10,8},{12,10},{14,12},{3,1},{5,3},{7,5},{... | collective-permute-start | bytes 3176 | tf_op jit(solution)/shard_map/ppermute | solution.py:22
  529.7 11.8 %collective-permute-start.64 = (f32[2,1,66,130]{3,2,1,0:T(8,128)S(1)}, f32[2,1,66,130]{3,2,1,0:T(8,128)S(1)}, u32[]{:S(2)}, u32[]{:S(2)}) collective-permute-start(f32[2,1,66,130]{3,2,1,0:T(8,128)S(1)} %get-tuple-element.120), channel_id=1, source_target_pairs={{1,0},{3,2},{5,4},{7,6},{9,8},{11,10},{13,12},{15,14},{17,16},{19,... | collective-permute-start | bytes 205928 | tf_op jit(solution)/shard_map/ppermute | solution.py:22
  531.0 10.5 %collective-permute-start.65 = (f32[2,1,66,130]{3,2,1,0:T(8,128)S(1)}, f32[2,1,66,130]{3,2,1,0:T(8,128)S(1)}, u32[]{:S(2)}, u32[]{:S(2)}) collective-permute-start(f32[2,1,66,130]{3,2,1,0:T(8,128)S(1)} %get-tuple-element.121), channel_id=1, source_target_pairs={{0,1},{2,3},{4,5},{6,7},{8,9},{10,11},{12,13},{14,15},{16,17},{18,... | collective-permute-start | bytes 205928 | tf_op jit(solution)/shard_map/ppermute | solution.py:21
  535.5 169.8 %collective-permute-start.70 = (f32[2,1,66,130]{3,2,1,0:T(8,128)S(1)}, f32[2,1,66,130]{3,2,1,0:T(8,128)S(1)}, u32[]{:S(2)}, u32[]{:S(2)}) collective-permute-start(f32[2,1,66,130]{3,2,1,0:T(8,128)S(1)} %get-tuple-element.118), channel_id=1, source_target_pairs={{1,0},{3,2},{5,4},{7,6},{9,8},{11,10},{13,12},{15,14},{17,16},{19,... | collective-permute-start | bytes 205928 | tf_op jit(solution)/shard_map/ppermute | solution.py:22
  536.8 168.5 %collective-permute-start.71 = (f32[2,1,66,130]{3,2,1,0:T(8,128)S(1)}, f32[2,1,66,130]{3,2,1,0:T(8,128)S(1)}, u32[]{:S(2)}, u32[]{:S(2)}) collective-permute-start(f32[2,1,66,130]{3,2,1,0:T(8,128)S(1)} %get-tuple-element.119), channel_id=1, source_target_pairs={{0,1},{2,3},{4,5},{6,7},{8,9},{10,11},{12,13},{14,15},{16,17},{18,... | collective-permute-start | bytes 205928 | tf_op jit(solution)/shard_map/ppermute | solution.py:21
  756.6 9.1 %collective-permute-start.84 = (f32[2,2,1,128]{3,2,1,0:T(1,128)S(1)}, f32[2,2,1,128]{3,2,1,0:T(1,128)S(1)}, u32[]{:S(2)}, u32[]{:S(2)}) collective-permute-start(f32[2,2,1,128]{3,2,1,0:T(1,128)S(1)} %get-tuple-element.172), channel_id=1, source_target_pairs={{0,16},{16,32},{32,48},{48,64},{64,80},{80,96},{96,112},{112,128},... | collective-permute-start | bytes 6152 | tf_op jit(solution)/shard_map/ppermute | solution.py:21
  (62 other events, 656.3 us)
where the time goes:
time: 797 us; the launch traced here: 788 us
  blocking collectives  315 us (40%)
  starting transfers between devices  287 us (36%)
  waiting for transfers between devices  81 us (10%)
  matrix products  44.2 us (6%)
  local copies, waits for them, and re-layouts  33.9 us (4%)
  other arithmetic  24.6 us (3%)
    ppermute x45, starting transfers between devices, extended(): before = lax.ppermute(last, axis, up)  163 us
    psum x2, blocking collectives, fk_round(): whole_sums = lax.psum(partial_sums, ('col', 'gz'))  161 us
    ppermute x45, starting transfers between devices, extended(): after = lax.ppermute(leading, axis, down)  124 us
    all_gather x2, blocking collectives, fk_round(): lax.all_gather(trace, 'row', axis=1, tiled=True)  89.1 us
    ppermute x45, waiting for transfers between devices, extended(): after = lax.ppermute(leading, axis, down)  67.9 us
    dot_general x8, matrix products, block_sum(): lax.dot_general(piece_traces, kernel, (((1,), (1,)), ((), ())), precision...  44.2 us
    all_gather x1, blocking collectives, on_device(): lax.all_gather(jnp.concatenate([node_pos, node_weight[None, :]], 0), 'row...  38.5 us
    all_gather x1, blocking collectives, on_device(): target_pos = lax.all_gather(node_pos, ('col', 'gz'), axis=1, tiled=True)  26.3 us
  transfers between devices with their start and end apart: 90, of which 39 were waited for; matrix products, arithmetic and copies ran while one was open for 7% of the time, Pallas kernels for 0%

commit v1 on v0

v1 whole, which is shorter than its diff:
```python
import functools

import jax
import jax.numpy as jnp
from jax import lax
from jax.experimental import pallas as pl
from jax.experimental.pallas import tpu as pltpu
from jax.sharding import PartitionSpec as P

SWEEPS = 4
OMEGA = 0.8
RELAX = 0.5
SOFTEN = 0.01
H = 8
HIGH = lax.Precision.HIGHEST
F32 = jnp.float32


def iota(shape, axis):
    return lax.broadcasted_iota(jnp.int32, shape, axis)


def pick(flag, shape, yes, no):
    return jnp.where(jnp.full(shape, flag, jnp.int32) == 1, yes, no)


def place(me_ref, n_col):
    me = me_ref[0]
    gz = lax.rem(me, 2)
    col = lax.rem(me // 2, n_col)
    row = me // (2 * n_col)
    return row, col, gz


def layer_of(own_ref, other_ref, kind, z, gz, shape):
    mine = pick(gz, shape, 1, 0) == z // 2
    return jnp.where(mine, own_ref[kind, z % 2], other_ref[kind, z % 2])


def col_pack(n_col, me_ref, own_ref, other_ref, a_ref, b_ref):
    _, col, gz = place(me_ref, n_col)
    shape = own_ref.shape[2:]
    lane = iota(shape, 1)
    left = jnp.zeros(shape, F32)
    right = jnp.zeros(shape, F32)
    for s in range(12):
        cell = layer_of(own_ref, other_ref, s // 4, s % 4, gz, shape)
        here = (lane >= 8 * s) & (lane < 8 * s + 8)
        low = pltpu.roll(cell, 8 * s, 1) if s else cell
        left = jnp.where(here, low, left)
        right = jnp.where(here, pltpu.roll(cell, 8 * s + 8, 1), right)
    odd = lax.rem(col, 2)
    a_ref[...] = pick(odd, shape, left, right)
    b_ref[...] = pick(odd, shape, right, left)


def row_pack(n_col, me_ref, own_ref, other_ref, a_in, b_in, ext_ref, a_ref, b_ref):
    row, col, gz = place(me_ref, n_col)
    shape = own_ref.shape[2:]
    rows, lanes = shape
    lane = iota(shape, 1)
    odd_col = lax.rem(col, 2)
    from_right = pick(odd_col, shape, b_in[...], a_in[...])
    from_left = pick(odd_col, shape, a_in[...], b_in[...])
    odd = lax.rem(row, 2)
    edge = (H, 2 * lanes)
    for s in range(12):
        cell = layer_of(own_ref, other_ref, s // 4, s % 4, gz, shape)
        low = pltpu.roll(from_right, lanes - 8 * s, 1) if s else from_right
        high = pltpu.roll(from_left, lanes - 8 - 8 * s, 1)
        side = jnp.where(lane < 8, low, jnp.where(lane >= lanes - 8, high, 0.0))
        ext_ref[s, :, 0:lanes] = cell
        ext_ref[s, :, lanes : 2 * lanes] = side
        top = ext_ref[s, 0:H, :]
        bottom = ext_ref[s, rows - H : rows, :]
        a_ref[s] = pick(odd, edge, top, bottom)
        b_ref[s] = pick(odd, edge, bottom, top)


def sweep(now_ref, next_ref, force_ref, weight_ref):
    rows, lanes = now_ref.shape[2:]

    def image(m, carry):
        for z in range(4):
            cell = now_ref[m, z]
            beside = pltpu.roll(cell, 1, 0) + pltpu.roll(cell, rows - 1, 0)
            beside = beside + (pltpu.roll(cell, 1, 1) + pltpu.roll(cell, lanes - 1, 1))
            if z > 0:
                beside = beside + now_ref[m, z - 1]
            if z < 3:
                beside = beside + now_ref[m, z + 1]
            next_ref[m, z] = (1.0 - OMEGA) * cell + (force_ref[m, z] + weight_ref[z] * beside)
        return carry

    lax.fori_loop(0, now_ref.shape[0], image, 0)


def read_trace(field_ref, owner_ref, node_ref, gz, t_ref, u_ref):
    owner = owner_ref[...]
    nodes = owner.shape[1]
    shape = (128, nodes)
    at_row = jnp.where(iota(shape, 0) == owner // 128, 1.0, 0.0).astype(F32)
    at_lane = iota(shape, 0) == lax.rem(owner, 128)
    for m in range(2):
        field = jnp.concatenate([field_ref[m, 2 * gz + k, H : H + 64, 0:128] for k in range(2)], 0)
        found = lax.dot_general(
            field, at_row, (((0,), (0,)), ((), ())), precision=HIGH, preferred_element_type=F32
        )
        trace = jnp.sum(jnp.where(at_lane, found, 0.0), axis=0, keepdims=True)
        t_ref[m : m + 1, :] = trace
        u_ref[m : m + 1, :] = trace * node_ref[...]


def first_relax(
    n_col, me_ref, ext_ref, a_in, b_in, owner_ref, node_ref, full_ref, first_ref, t_ref, u_ref, force, spare
):
    row, _, gz = place(me_ref, n_col)
    odd = lax.rem(row, 2)
    edge = a_in.shape[1:]
    for s in range(12):
        full_ref[s // 4, s % 4, 0:H, :] = pick(odd, edge, a_in[s], b_in[s])
        full_ref[s // 4, s % 4, H : H + 64, :] = ext_ref[s]
        full_ref[s // 4, s % 4, H + 64 : 2 * H + 64, :] = pick(odd, edge, b_in[s], a_in[s])
    weight = full_ref.at[2]
    for m in range(2):
        for z in range(4):
            force[m, z] = full_ref[m, z] * weight[z]
    sweep(force, first_ref, force, weight)
    sweep(first_ref, spare, force, weight)
    sweep(spare, first_ref, force, weight)
    read_trace(first_ref, owner_ref, node_ref, gz, t_ref, u_ref)


def load_spread(odd, spread_ref, a_in, b_in, weight, force):
    edge = a_in.shape[1:]
    for s in range(8):
        m, z = s // 4, s % 4
        force[m, z, 0:H, :] = pick(odd, edge, a_in[s], b_in[s]) * weight[z, 0:H]
        force[m, z, H : H + 64, :] = spread_ref[s] * weight[z, H : H + 64]
        force[m, z, H + 64 : 2 * H + 64, :] = pick(odd, edge, b_in[s], a_in[s]) * weight[z, H + 64 : 2 * H + 64]


def second_round(
    n_col, me_ref, full_ref, first_ref, spread_ref, a_in, b_in, owner_ref, node_ref,
    second_ref, keep_ref, t_ref, u_ref, force, spare, other,
):
    row, _, gz = place(me_ref, n_col)
    weight = full_ref.at[2]
    load_spread(lax.rem(row, 2), spread_ref, a_in, b_in, weight, force)
    sweep(force, second_ref, force, weight)
    sweep(second_ref, spare, force, weight)
    sweep(spare, second_ref, force, weight)
    for m in range(2):
        for z in range(4):
            force[m, z] = (full_ref[m, z] - RELAX * (first_ref[m, z] + second_ref[m, z])) * weight[z]
    sweep(first_ref, spare, force, weight)
    sweep(spare, other, force, weight)
    sweep(other, spare, force, weight)
    sweep(spare, other, force, weight)
    for m in range(2):
        for k in range(2):
            keep_ref[m, k] = other[m, 2 * gz + k, H : H + 64, 0:128]
    read_trace(other, owner_ref, node_ref, gz, t_ref, u_ref)


def last_relax(
    n_col, me_ref, full_ref, second_ref, spread_ref, a_in, b_in, keep_ref, out_ref, force, spare, other
):
    row, _, gz = place(me_ref, n_col)
    weight = full_ref.at[2]
    load_spread(lax.rem(row, 2), spread_ref, a_in, b_in, weight, force)
    sweep(second_ref, spare, force, weight)
    sweep(spare, other, force, weight)
    sweep(other, spare, force, weight)
    sweep(spare, other, force, weight)
    for m in range(2):
        for k in range(2):
            out_ref[m, k] = keep_ref[m, k] + other[m, 2 * gz + k, H : H + 64, 0:128]


def pair_kernel(source_ref, target_ref, out_ref):
    nodes = source_ref.shape[2]
    square = (nodes, nodes)
    at = [jnp.broadcast_to(source_ref[0, k : k + 1, :], square).T for k in range(3)]
    for t in range(target_ref.shape[0]):
        dx = target_ref[t, 0:1, :] - at[0]
        dy = target_ref[t, 1:2, :] - at[1]
        dz = target_ref[t, 2:3, :] - at[2]
        inverse = lax.rsqrt(dx * dx + dy * dy + (dz * dz + SOFTEN))
        out_ref[0, :, t * nodes : (t + 1) * nodes] = dz * inverse * (inverse * inverse)


def apply_kernel(n_col, steps, me_ref, u_ref, pair_ref, t_ref, out_ref, acc, lined):
    step = pl.program_id(0)
    _, col, gz = place(me_ref, n_col)
    nodes = u_ref.shape[2]
    square = (nodes, nodes)
    blocks = 2 * n_col

    @pl.when(step == 0)
    def _():
        acc[...] = jnp.zeros_like(acc)

    for k in range(pair_ref.shape[0]):
        at = [jnp.broadcast_to(u_ref[k, m : m + 1, :], square).T for m in range(2)]
        for t in range(blocks):
            pair = pair_ref[k, :, t * nodes : (t + 1) * nodes]
            for m in range(2):
                part = jnp.sum((pair * at[m]).reshape(nodes // 8, 8, nodes), axis=0)
                acc[m, t] = acc[m, t] + part

    @pl.when(step == steps - 1)
    def _():
        lined[...] = jnp.zeros_like(lined)
        for t in range(blocks):
            mine = jnp.where(2 * col + gz == t, -0.5, 0.0).astype(F32)
            for m in range(2):
                whole = jnp.sum(acc[m, t], axis=0, keepdims=True)
                lined[m, t + 2 : t + 3, :] = whole + mine * t_ref[m : m + 1, :]
        for c in range(n_col):
            for m in range(2):
                near = lined[m, 2 * c : 2 * c + 8, :]
                out_ref[2 * c, 8 * m : 8 * m + 8, :] = near
                out_ref[2 * c + 1, 8 * m : 8 * m + 8, :] = near


def spread_nodes(n_col, me_ref, part_ref, target_ref, spread_ref, a_ref, b_ref, value_ref):
    row, col, gz = place(me_ref, n_col)
    nodes = part_ref.shape[2]
    blocks = 2 * n_col
    value = part_ref[0]
    for k in range(1, blocks):
        value = value + part_ref[k]
    shape = (128, nodes)
    down = iota(shape, 0)
    weighted, lanes = [], []
    for b in range(6):
        at = jnp.clip(2 * col - 2 + b, 0, blocks - 1)
        owner = target_ref[at, 3:4, :].astype(jnp.int32)
        hit = down == owner // 128
        weighted.append(
            jnp.concatenate([jnp.where(hit, value[8 * m + b : 8 * m + b + 1, :], 0.0) for m in range(2)], 0)
        )
        lane = down == lax.rem(owner, 128)
        if b < 2:
            lane = lane & (down >= 128 - H)
        if b > 3:
            lane = lane & (down < H)
        lanes.append(jnp.where(lane, 1.0, 0.0).astype(F32))

    def product(a, b):
        return lax.dot_general(a, b, (((1,), (1,)), ((), ())), precision=HIGH, preferred_element_type=F32)

    for g in range(2):
        own = product(weighted[2 + g], lanes[2 + g])
        side = product(
            jnp.concatenate([weighted[g], weighted[4 + g]], 1), jnp.concatenate([lanes[g], lanes[4 + g]], 1)
        )
        for m in range(2):
            for k in range(2):
                start = 128 * m + 64 * k
                spread_ref[4 * m + 2 * g + k, :, 0:128] = own[start : start + 64]
                spread_ref[4 * m + 2 * g + k, :, 128:256] = side[start : start + 64]
    odd = lax.rem(row, 2)
    edge = (H, 256)
    for s in range(8):
        top = spread_ref[s, 0:H, :]
        bottom = spread_ref[s, 64 - H : 64, :]
        a_ref[s] = pick(odd, edge, top, bottom)
        b_ref[s] = pick(odd, edge, bottom, top)
    for m in range(2):
        value_ref[m : m + 1, :] = pick(
            gz, (1, nodes), value[8 * m + 3 : 8 * m + 4, :], value[8 * m + 2 : 8 * m + 3, :]
        )


SMEM = pl.BlockSpec(memory_space=pltpu.SMEM)
VMEM = pl.BlockSpec(memory_space=pltpu.VMEM)


def run(body, name, outs, args, scratch=(), flops=0):
    moved = sum(a.size * 4 for a in args) + sum(4 * functools.reduce(lambda a, b: a * b, o) for o in outs)
    return pl.pallas_call(
        body,
        name=name,
        out_shape=[jax.ShapeDtypeStruct(o, F32) for o in outs],
        in_specs=[SMEM] + [VMEM] * (len(args) - 1),
        out_specs=[VMEM] * len(outs),
        scratch_shapes=[pltpu.VMEM(s, F32) for s in scratch],
        compiler_params=pltpu.CompilerParams(vmem_limit_bytes=24 << 20),
        cost_estimate=pl.CostEstimate(flops=flops, bytes_accessed=moved, transcendentals=0),
    )(*args)


def on_device(
    n_row, n_col, source, cell_class, coeff_table, owner_cell, node_pos, node_weight
):
    everything = ("row", "col", "gz")
    nodes = owner_cell.shape[0]
    me = lax.axis_index(everything).reshape(1)

    def swaps(axis, size, a, b):
        first = [(i, i ^ 1) for i in range(size)]
        second = [(i + 1, i + 2) for i in range(0, size - 2, 2)]
        second = second + [(j, i) for i, j in second]
        return lax.ppermute(a, axis, first), lax.ppermute(b, axis, second)

    def gathered(x, axes, count):
        return lax.all_to_all(jnp.broadcast_to(x[None], (count,) + x.shape), axes, 0, 0)

    summed = jnp.zeros(cell_class.shape, F32)
    for level in range(coeff_table.shape[0]):
        summed = summed + jnp.where(cell_class == level, coeff_table[level], 0.0)
    packed = jnp.concatenate([source, (OMEGA / (6.0 + summed))[None]], 0)
    other = lax.ppermute(packed, "gz", [(0, 1), (1, 0)])
    owner = owner_cell[None, :]
    weight = node_weight[None, :]
    target = gathered(
        jnp.concatenate([node_pos, owner.astype(F32)], 0), ("col", "gz"), 2 * n_col
    )
    origin = gathered(node_pos, "row", n_row)

    a, b = run(functools.partial(col_pack, n_col), "col_pack", [(64, 128)] * 2, [me, packed, other])
    a, b = swaps("col", n_col, a, b)
    ext, a, b = run(
        functools.partial(row_pack, n_col),
        "row_pack",
        [(12, 64, 256), (12, H, 256), (12, H, 256)],
        [me, packed, other, a, b],
    )
    a, b = swaps("row", n_row, a, b)

    blocks = 2 * n_col
    pairs = pl.pallas_call(
        pair_kernel,
        name="pair_kernel",
        grid=(n_row,),
        out_shape=jax.ShapeDtypeStruct((n_row, nodes, blocks * nodes), F32),
        in_specs=[
            pl.BlockSpec((1, 3, nodes), lambda i: (i, 0, 0)),
            pl.BlockSpec((blocks, 4, nodes), lambda i: (0, 0, 0)),
        ],
        out_specs=pl.BlockSpec((1, nodes, blocks * nodes), lambda i: (i, 0, 0)),
        compiler_params=pltpu.CompilerParams(vmem_limit_bytes=16 << 20),
        cost_estimate=pl.CostEstimate(
            flops=14 * n_row * blocks * nodes * nodes,
            bytes_accessed=4 * n_row * blocks * nodes * nodes,
            transcendentals=n_row * blocks * nodes * nodes,
        ),
    )(origin, target)

    field = (2, 4, 64 + 2 * H, 256)
    full, first, trace, sent = run(
        functools.partial(first_relax, n_col),
        "first_relax",
        [(3, 4, 64 + 2 * H, 256), field, (2, nodes), (2, nodes)],
        [me, ext, a, b, owner, weight],
        [field] * 2,
    )

    group = 2

    def values_of(trace, sent):
        heard = gathered(sent, "row", n_row)
        partial = pl.pallas_call(
            functools.partial(apply_kernel, n_col, n_row // group),
            name="apply_kernel",
            grid=(n_row // group,),
            out_shape=jax.ShapeDtypeStruct((blocks, 16, nodes), F32),
            in_specs=[
                SMEM,
                pl.BlockSpec((group, 2, nodes), lambda i: (i, 0, 0)),
                pl.BlockSpec((group, nodes, blocks * nodes), lambda i: (i, 0, 0)),
                pl.BlockSpec((2, nodes), lambda i: (0, 0)),
            ],
            out_specs=pl.BlockSpec((blocks, 16, nodes), lambda i: (0, 0, 0)),
            scratch_shapes=[
                pltpu.VMEM((2, blocks, 8, nodes), F32),
                pltpu.VMEM((2, blocks + 8, nodes), F32),
            ],
            compiler_params=pltpu.CompilerParams(vmem_limit_bytes=24 << 20),
            cost_estimate=pl.CostEstimate(
                flops=4 * n_row * blocks * nodes * nodes,
                bytes_accessed=4 * n_row * blocks * nodes * nodes,
                transcendentals=0,
            ),
        )(me, heard, pairs, trace)
        partial = lax.all_to_all(partial, ("col", "gz"), 0, 0)
        spread, a, b, values = run(
            functools.partial(spread_nodes, n_col),
            "spread_nodes",
            [(8, 64, 256), (8, H, 256), (8, H, 256), (2, nodes)],
            [me, partial, target],
        )
        a, b = swaps("row", n_row, a, b)
        return spread, a, b, values

    spread, a, b, _ = values_of(trace, sent)
    second, keep, trace, sent = run(
        functools.partial(second_round, n_col),
        "second_round",
        [field, (2, 2, 64, 128), (2, nodes), (2, nodes)],
        [me, full, first, spread, a, b, owner, weight],
        [field] * 3,
    )
    spread, a, b, values = values_of(trace, sent)
    (potential,) = run(
        functools.partial(last_relax, n_col),
        "last_relax",
        [(2, 2, 64, 128)],
        [me, full, second, spread, a, b, keep],
        [field] * 3,
    )
    return potential, values


def solution(mesh):
    return jax.shard_map(
        functools.partial(on_device, mesh.shape["row"], mesh.shape["col"]),
        mesh=mesh,
        in_specs=(
            P(None, "gz", "row", "col"),
            P("gz", "row", "col"),
            P(),
            P(("row", "col", "gz")),
            P(None, ("row", "col", "gz")),
            P(("row", "col", "gz")),
        ),
        out_specs=(P(None, "gz", "row", "col"), P(None, ("row", "col", "gz"))),
        check_vma=False,
    )
```

time: 797 us -> 152 us (0.19)
  blocking collectives: 315 us -> 37.3 us
  starting transfers between devices: 287 us -> 47.4 us
  waiting for transfers between devices: 81 us -> 12.2 us
  matrix products: 44.2 us -> 0 us
  Pallas kernels: 0 us -> 27.8 us
  local copies, waits for them, and re-layouts: 33.9 us -> 17 us
  other arithmetic: 24.6 us -> 8.29 us
    ppermute x90 -> x9, starting transfers between devices: 287 us -> 22.5 us  [the longest x8 20.5 us: swaps(): return (lax.ppermute(a, axis, first), lax.ppermute(b, axis, second))]
    psum x2 -> x0, blocking collectives: 161 us -> none  [fk_round(): whole_sums = lax.psum(partial_sums, ('col', 'gz'))]
    all_gather x4 -> x0, blocking collectives: 154 us -> none  [the longest x2 89.1 us: fk_round(): lax.all_gather(trace, 'row', axis=1, tiled=True)]
    ppermute x90 -> x9, waiting for transfers between devices: 81 us -> 9.41 us  [the longest x8 9.41 us: swaps(): return (lax.ppermute(a, axis, first), lax.ppermute(b, axis, second))]
    dot_general x8 -> x0, matrix products: 44.2 us -> none  [block_sum(): lax.dot_general(piece_traces, kernel, (((1,), (1,)), ((), ())), precision...]
    all_to_all x0 -> x3, blocking collectives: none -> 37.3 us  [the longest x2 20.1 us: values_of(): partial = lax.all_to_all(partial, ('col', 'gz'), 0, 0)]
    pallas_call x0 -> x10, Pallas kernels: none -> 27.8 us  [the longest x7 12 us: run(): pl.pallas_call(body, name=name, out_shape=[jax.ShapeDtypeStruct(o, F32) f...]
    all_to_all x0 -> x3, starting transfers between devices: none -> 24.8 us  [gathered(): lax.all_to_all(jnp.broadcast_to(x[None], (count,) + x.shape), axes, 0, 0)]
  transfers between devices with their start and end apart: 90 -> 12, of which waited for: 39 -> 4; matrix products, arithmetic and copies ran while one was open for 7% -> 2% of each run, Pallas kernels for 0% -> 7%
where the time goes in v1:
time: 152 us; the launch traced here: 151 us
  starting transfers between devices  47.4 us (31%)
  blocking collectives  37.3 us (25%)
  Pallas kernels  27.8 us (18%)
  local copies, waits for them, and re-layouts  17 us (11%)
  waiting for transfers between devices  12.2 us (8%)
  other arithmetic  8.29 us (5%)
    all_to_all x3, starting transfers between devices, gathered(): lax.all_to_all(jnp.broadcast_to(x[None], (count,) + x.shape), axes, 0, 0)  24.8 us
    ppermute x8, starting transfers between devices, swaps(): return (lax.ppermute(a, axis, first), lax.ppermute(b, axis, second))  20.5 us
    all_to_all x2, blocking collectives, values_of(): partial = lax.all_to_all(partial, ('col', 'gz'), 0, 0)  20.1 us
    all_to_all x1, blocking collectives, gathered(): lax.all_to_all(jnp.broadcast_to(x[None], (count,) + x.shape), axes, 0, 0)  17.2 us
    unnamed x14, local copies, waits for them, and re-layouts  12.8 us
    pallas_call x7, Pallas kernels, run(): pl.pallas_call(body, name=name, out_shape=[jax.ShapeDtypeStruct(o, F32) f...  12 us
    ppermute x8, waiting for transfers between devices, swaps(): return (lax.ppermute(a, axis, first), lax.ppermute(b, axis, second))  9.41 us
    pallas_call x1, Pallas kernels, on_device(): pl.pallas_call(pair_kernel, name='pair_kernel', grid=(n_row,), out_shape=...  8.61 us
  transfers between devices with their start and end apart: 12, of which 4 were waited for; matrix products, arithmetic and copies ran while one was open for 2% of the time, Pallas kernels for 7%

profile of v1, /device:TPU:8, one launch (start us, length us, event | category | flops | bytes accessed | tf_op | source)
XLA Modules:
  0.0 150.7 jit_solution(14706555446599759366)
XLA Ops:
  0.6 1.6 %fusion = (f32[1]{0:T(128)}, f32[1]{0:T(128)}, f32[1]{0:T(128)}, f32[1]{0:T(128)}, f32[1]{0:T(128)}, /*index=5*/f32[1]{0:T(128)}, f32[1]{0:T(128)}, f32[1]{0:T(128)}) fusion(f32[8]{0:T(128)} %param.8), kind=kLoop, calls=%fused_computation.4 | loop fusion | bytes 64 | tf_op jit(solution)/shard_map/slice | solution.py:313
  2.3 6.0 %divide_bitcast_fusion = f32[1,2,64,128]{3,2,1,0:T(8,128)S(1)} fusion(s32[2,64,128]{2,1,0:T(8,128)} %param.7, f32[]{:T(128)} %bitcast.8, f32[]{:T(128)} %bitcast.7, f32[]{:T(128)} %bitcast.6, f32[]{:T(128)} %bitcast.5, f32[]{:T(128)} %bitcast.4, f32[]{:T(128)} %bitcast.3, f32[]{:T(128)} %bitcast.2, f32[]{:T(128)} %bitcast.1), kind=kLoop, calls=%fused_computation.1 | loop fusion | flops 409600 | bytes 131104 | tf_op jit(solution)/shard_map/broadcast_in_dim | solution.py:314
  8.3 0.9 pad_maximum_fusion.own_ref
  9.2 2.0 %collective-permute-start = (f32[3,2,64,128]{3,2,1,0:T(8,128)S(1)}, f32[3,2,64,128]{3,2,1,0:T(8,128)S(1)}, u32[]{:S(2)}, u32[]{:S(2)}) collective-permute-start(f32[3,2,64,128]{3,2,1,0:T(8,128)S(1)} %pad_maximum_fusion.own_ref), channel_id=1, source_target_pairs={{0,1},{1,0},{2,3},{3,2},{4,5},{5,4},{6,7},{7,6},{8,9},{9,8},{10,11... | collective-permute-start | bytes 589832 | tf_op jit(solution)/shard_map/ppermute | solution.py:315
  11.2 1.3 broadcast_in_dim.82
  12.5 10.7 %all-to-all-start.1 = ((f32[16,3,128]{2,1,0:T(4,128)}), f32[16,3,128]{2,1,0:T(4,128)S(1)}, u32[]{:S(2)}, u32[]{:S(2)}) async-start(f32[16,3,128]{2,1,0:T(4,128)} %broadcast_in_dim.82), calls=%async_computation.1 | async-start | bytes 65536 | tf_op jit(solution)/shard_map/all_to_all | solution.py:309
  23.5 0.7 collective-permute-start.2
  25.2 2.4 %collective-permute-start.3 = (f32[12,8,256]{2,1,0:T(8,128)S(1)}, f32[12,8,256]{2,1,0:T(8,128)S(1)}, u32[]{:S(2)}, u32[]{:S(2)}) collective-permute-start(f32[12,8,256]{2,1,0:T(8,128)S(1)} %get-tuple-element.25), channel_id=1, source_target_pairs={{0,16},{16,0},{32,48},{48,32},{64,80},{80,64},{96,112},{112,96},{1... | collective-permute-start | bytes 294920 | tf_op jit(solution)/shard_map/ppermute | solution.py:306
  27.6 5.5 %collective-permute-start.4 = (f32[12,8,256]{2,1,0:T(8,128)S(1)}, f32[12,8,256]{2,1,0:T(8,128)S(1)}, u32[]{:S(2)}, u32[]{:S(2)}) collective-permute-start(f32[12,8,256]{2,1,0:T(8,128)S(1)} %get-tuple-element.26), channel_id=1, source_target_pairs={{16,32},{48,64},{80,96},{112,128},{144,160},{176,192},{208,224},{3... | collective-permute-start | bytes 294920 | tf_op jit(solution)/shard_map/ppermute | solution.py:306
  33.1 0.7 pad_maximum_fusion.1
  34.4 8.7 %all-to-all-start.2 = ((f32[16,4,128]{2,1,0:T(4,128)}), f32[16,4,128]{2,1,0:T(4,128)S(1)}, u32[]{:S(2)}, u32[]{:S(2)}) async-start(f32[16,4,128]{2,1,0:T(4,128)} %broadcast_in_dim.83), calls=%async_computation.2 | async-start | bytes 65536 | tf_op jit(solution)/shard_map/all_to_all | solution.py:309
  44.5 2.0 %first_relax.1 = (f32[3,4,80,256]{3,2,1,0:T(8,128)S(1)}, f32[2,4,80,256]{3,2,1,0:T(8,128)S(1)}, f32[2,128]{1,0:T(2,128)S(1)}, f32[2,128]{1,0:T(2,128)S(1)}) custom-call(s32[1]{0:T(128)} %bitcast.me_ref, f32[12,64,256]{2,1,0:T(8,128)S(1)} %get-tuple-element.24.ext_ref, f32[12,8,256]{2,1,0:T(8,128)S(1)} %collective-permute-done.3.a_in, ...), custom_call_target="tpu_custom_call" | custom-call | bytes 2624516 | tf_op jit(solution)/shard_map/first_relax/pallas_call | solution.py:283
  46.5 2.8 %all-to-all-done.2.target_ref = f32[16,4,128]{2,1,0:T(4,128)S(1)} async-done(((f32[16,4,128]{2,1,0:T(4,128)}), f32[16,4,128]{2,1,0:T(4,128)S(1)}, u32[]{:S(2)}, u32[]{:S(2)}) %all-to-all-start.2) | async-done | bytes 32800 | tf_op jit(solution)/shard_map/all_to_all | solution.py:309
  49.9 5.4 %all-to-all-start = ((f32[16,2,128]{2,1,0:T(2,128)}), f32[16,2,128]{2,1,0:T(2,128)S(1)}, u32[]{:S(2)}, u32[]{:S(2)}) async-start(f32[16,2,128]{2,1,0:T(2,128)} %broadcast_in_dim.81), calls=%async_computation | async-start | bytes 32768 | tf_op jit(solution)/shard_map/all_to_all | solution.py:309
  55.4 8.6 %pair_kernel.1.pair_ref = f32[16,128,2048]{2,1,0:T(8,128)S(1)} custom-call(f32[16,3,128]{2,1,0:T(4,128)S(1)} %all-to-all-done.1.source_ref, f32[16,4,128]{2,1,0:T(4,128)S(1)} %all-to-all-done.2.target_ref), custom_call_target="tpu_custom_call" | custom-call | flops 58720256 | bytes 16777216 | tf_op jit(solution)/shard_map/pair_kernel/pallas_call | solution.py:334
  64.0 5.7 %copy-done = f32[16,128,2048]{2,1,0:T(8,128)} copy-done((f32[16,128,2048]{2,1,0:T(8,128)}, f32[16,128,2048]{2,1,0:T(8,128)S(1)}, u32[]{:S(2)}) %copy-start) | copy-done | bytes 16777240
  69.7 5.8 %copy-done.1 = f32[16,128,2048]{2,1,0:T(8,128)S(1)} copy-done((f32[16,128,2048]{2,1,0:T(8,128)S(1)}, f32[16,128,2048]{2,1,0:T(8,128)}, u32[]{:S(2)}) %copy-start.1) | copy-done | bytes 16777240
  75.5 3.6 %apply_kernel.2 = f32[16,16,128]{2,1,0:T(8,128)S(1)} custom-call(s32[1]{0:T(128)} %bitcast.me_ref, f32[16,2,128]{2,1,0:T(2,128)S(1)} %all-to-all-done.u_ref, f32[16,128,2048]{2,1,0:T(8,128)S(1)} %copy-done.1, f32[2,128]{1,0:T(2,128)S(1)} %get-tuple-element.30.t_ref), custom_call_target="tpu_custom_call" | custom-call | flops 16777216 | bytes 16777216 | tf_op jit(solution)/shard_map/apply_kernel/pallas_call | solution.py:365
  79.1 10.9 %all_to_all.30.part_ref = f32[16,16,128]{2,1,0:T(8,128)S(1)} all-to-all(f32[16,16,128]{2,1,0:T(8,128)S(1)} %apply_kernel.2), channel_id=1, replica_groups=mesh['row'=16,'col'=8,'gz'=2] {'col','gz'}, dimensions={0} | all-to-all | bytes 262144 | tf_op jit(solution)/shard_map/all_to_all | solution.py:388
  90.0 1.3 spread_nodes.2
  91.3 2.4 %collective-permute-start.5 = (f32[8,8,256]{2,1,0:T(8,128)S(1)}, f32[8,8,256]{2,1,0:T(8,128)S(1)}, u32[]{:S(2)}, u32[]{:S(2)}) collective-permute-start(f32[8,8,256]{2,1,0:T(8,128)S(1)} %get-tuple-element.32), channel_id=1, source_target_pairs={{0,16},{16,0},{32,48},{48,32},{64,80},{80,64},{96,112},{112,96},{1... | collective-permute-start | bytes 196616 | tf_op jit(solution)/shard_map/ppermute | solution.py:306
  93.6 5.5 %collective-permute-start.6 = (f32[8,8,256]{2,1,0:T(8,128)S(1)}, f32[8,8,256]{2,1,0:T(8,128)S(1)}, u32[]{:S(2)}, u32[]{:S(2)}) collective-permute-start(f32[8,8,256]{2,1,0:T(8,128)S(1)} %get-tuple-element.33), channel_id=1, source_target_pairs={{16,32},{48,64},{80,96},{112,128},{144,160},{176,192},{208,224},{3... | collective-permute-start | bytes 196616 | tf_op jit(solution)/shard_map/ppermute | solution.py:306
  99.1 3.7 %collective-permute-done.6.b_in = f32[8,8,256]{2,1,0:T(8,128)S(1)} collective-permute-done((f32[8,8,256]{2,1,0:T(8,128)S(1)}, f32[8,8,256]{2,1,0:T(8,128)S(1)}, u32[]{:S(2)}, u32[]{:S(2)}) %collective-permute-start.6) | collective-permute-done | bytes 65568 | tf_op jit(solution)/shard_map/ppermute | solution.py:306
  102.8 4.1 %second_round.1 = (f32[2,4,80,256]{3,2,1,0:T(8,128)S(1)}, f32[2,2,64,128]{3,2,1,0:T(8,128)S(1)}, f32[2,128]{1,0:T(2,128)S(1)}, f32[2,128]{1,0:T(2,128)S(1)}) custom-call(s32[1]{0:T(128)} %bitcast.me_ref, f32[3,4,80,256]{3,2,1,0:T(8,128)S(1)} %get-tuple-element.27.full_ref, f32[2,4,80,256]{3,2,1,0:T(8,128)S(1)} %get-tuple-element.28.first_ref, ...), custom_call_target="tpu_custom_call" | custom-call | bytes 3083268 | tf_op jit(solution)/shard_map/second_round/pallas_call | solution.py:283
  106.9 17.2 %all_to_all.31.u_ref = f32[16,2,128]{2,1,0:T(2,128)S(1)} all-to-all(f32[16,2,128]{2,1,0:T(2,128)S(1)} %broadcast_in_dim.84), channel_id=1, replica_groups=mesh['row'=16,'col'=8,'gz'=2] {'row'}, dimensions={0} | all-to-all | bytes 32768 | tf_op jit(solution)/shard_map/all_to_all | solution.py:309
  124.2 3.6 %apply_kernel.3 = f32[16,16,128]{2,1,0:T(8,128)S(1)} custom-call(s32[1]{0:T(128)} %bitcast.me_ref, f32[16,2,128]{2,1,0:T(2,128)S(1)} %all_to_all.31.u_ref, f32[16,128,2048]{2,1,0:T(8,128)S(1)} %copy-done.2, f32[2,128]{1,0:T(2,128)S(1)} %get-tuple-element.36.t_ref), custom_call_target="tpu_custom_call" | custom-call | flops 16777216 | bytes 16777216 | tf_op jit(solution)/shard_map/apply_kernel/pallas_call | solution.py:365
  127.7 9.1 %all_to_all.32.part_ref = f32[16,16,128]{2,1,0:T(8,128)S(1)} all-to-all(f32[16,16,128]{2,1,0:T(8,128)S(1)} %apply_kernel.3), channel_id=1, replica_groups=mesh['row'=16,'col'=8,'gz'=2] {'col','gz'}, dimensions={0} | all-to-all | bytes 262144 | tf_op jit(solution)/shard_map/all_to_all | solution.py:388
  136.9 1.3 spread_nodes.3
  138.7 3.4 %collective-permute-start.8 = (f32[8,8,256]{2,1,0:T(8,128)S(1)}, f32[8,8,256]{2,1,0:T(8,128)S(1)}, u32[]{:S(2)}, u32[]{:S(2)}) collective-permute-start(f32[8,8,256]{2,1,0:T(8,128)S(1)} %get-tuple-element.39), channel_id=1, source_target_pairs={{16,32},{48,64},{80,96},{112,128},{144,160},{176,192},{208,224},{3... | collective-permute-start | bytes 196616 | tf_op jit(solution)/shard_map/ppermute | solution.py:306
  142.1 2.5 %collective-permute-done.7.a_in = f32[8,8,256]{2,1,0:T(8,128)S(1)} collective-permute-done((f32[8,8,256]{2,1,0:T(8,128)S(1)}, f32[8,8,256]{2,1,0:T(8,128)S(1)}, u32[]{:S(2)}, u32[]{:S(2)}) %collective-permute-start.7) | collective-permute-done | bytes 65568 | tf_op jit(solution)/shard_map/ppermute | solution.py:306
  144.6 3.2 %collective-permute-done.8.b_in = f32[8,8,256]{2,1,0:T(8,128)S(1)} collective-permute-done((f32[8,8,256]{2,1,0:T(8,128)S(1)}, f32[8,8,256]{2,1,0:T(8,128)S(1)}, u32[]{:S(2)}, u32[]{:S(2)}) %collective-permute-start.8) | collective-permute-done | bytes 65568 | tf_op jit(solution)/shard_map/ppermute | solution.py:306
  147.9 2.8 %last_relax.1 = f32[2,2,64,128]{3,2,1,0:T(8,128)} custom-call(s32[1]{0:T(128)} %bitcast.me_ref, f32[3,4,80,256]{3,2,1,0:T(8,128)S(1)} %get-tuple-element.27.full_ref, f32[2,4,80,256]{3,2,1,0:T(8,128)S(1)} %get-tuple-element.34.second_ref, f32[8,64,256]{2,1,0:T(8,128)S(1)} %get-tuple-element.37.spread_ref, f32[8,8,256]{2,1,0:T(8,128)S(1)} %collective-permute-done.7.a_in, ...), custom_call_target="tpu_custom_call" | custom-call | bytes 2555908 | tf_op jit(solution)/shard_map/last_relax/pallas_call | solution.py:283
  (28 shorter events, 4.5 us)
Async XLA Ops:
  9.2 14.0 %collective-permute-start = (f32[3,2,64,128]{3,2,1,0:T(8,128)S(1)}, f32[3,2,64,128]{3,2,1,0:T(8,128)S(1)}, u32[]{:S(2)}, u32[]{:S(2)}) collective-permute-start(f32[3,2,64,128]{3,2,1,0:T(8,128)S(1)} %pad_maximum_fusion.own_ref), channel_id=1, source_target_pairs={{0,1},{1,0},{2,3},{3,2},{4,5},{5,4},{6,7},{7,6},{8,9},{9,8},{10,11... | collective-permute-start | bytes 589832 | tf_op jit(solution)/shard_map/ppermute | solution.py:315
  12.5 21.3 %all-to-all-start.1 = ((f32[16,3,128]{2,1,0:T(4,128)}), f32[16,3,128]{2,1,0:T(4,128)S(1)}, u32[]{:S(2)}, u32[]{:S(2)}) async-start(f32[16,3,128]{2,1,0:T(4,128)} %broadcast_in_dim.82), calls=%async_computation.1 | async-start | bytes 65536 | tf_op jit(solution)/shard_map/all_to_all | solution.py:309
  23.4 1.4 collective-permute-start.1
  23.5 1.3 collective-permute-start.2
  25.2 18.0 %collective-permute-start.3 = (f32[12,8,256]{2,1,0:T(8,128)S(1)}, f32[12,8,256]{2,1,0:T(8,128)S(1)}, u32[]{:S(2)}, u32[]{:S(2)}) collective-permute-start(f32[12,8,256]{2,1,0:T(8,128)S(1)} %get-tuple-element.25), channel_id=1, source_target_pairs={{0,16},{16,0},{32,48},{48,32},{64,80},{80,64},{96,112},{112,96},{1... | collective-permute-start | bytes 294920 | tf_op jit(solution)/shard_map/ppermute | solution.py:306
  27.6 15.6 %collective-permute-start.4 = (f32[12,8,256]{2,1,0:T(8,128)S(1)}, f32[12,8,256]{2,1,0:T(8,128)S(1)}, u32[]{:S(2)}, u32[]{:S(2)}) collective-permute-start(f32[12,8,256]{2,1,0:T(8,128)S(1)} %get-tuple-element.26), channel_id=1, source_target_pairs={{16,32},{48,64},{80,96},{112,128},{144,160},{176,192},{208,224},{3... | collective-permute-start | bytes 294920 | tf_op jit(solution)/shard_map/ppermute | solution.py:306
  34.4 14.9 %all-to-all-start.2 = ((f32[16,4,128]{2,1,0:T(4,128)}), f32[16,4,128]{2,1,0:T(4,128)S(1)}, u32[]{:S(2)}, u32[]{:S(2)}) async-start(f32[16,4,128]{2,1,0:T(4,128)} %broadcast_in_dim.83), calls=%async_computation.2 | async-start | bytes 65536 | tf_op jit(solution)/shard_map/all_to_all | solution.py:309
  43.2 0.7 copy-start.3
  43.8 0.7 copy-start.5
  49.9 19.8 %all-to-all-start = ((f32[16,2,128]{2,1,0:T(2,128)}), f32[16,2,128]{2,1,0:T(2,128)S(1)}, u32[]{:S(2)}, u32[]{:S(2)}) async-start(f32[16,2,128]{2,1,0:T(2,128)} %broadcast_in_dim.81), calls=%async_computation | async-start | bytes 32768 | tf_op jit(solution)/shard_map/all_to_all | solution.py:309
  55.4 47.4 %copy-start.4 = (s32[128]{0:T(128)S(1)}, s32[128]{0:T(128)}, u32[]{:S(2)}) copy-start(s32[128]{0:T(128)} %param.9) | copy-start | bytes 1540
  55.4 47.4 %copy-start.6 = (f32[128]{0:T(128)S(1)}, f32[128]{0:T(128)}, u32[]{:S(2)}) copy-start(f32[128]{0:T(128)} %param.11) | copy-start | bytes 1540
  64.0 5.7 %copy-start = (f32[16,128,2048]{2,1,0:T(8,128)}, f32[16,128,2048]{2,1,0:T(8,128)S(1)}, u32[]{:S(2)}) copy-start(f32[16,128,2048]{2,1,0:T(8,128)S(1)} %pair_kernel.1.pair_ref) | copy-start | bytes 50331652
  69.7 5.8 %copy-start.1 = (f32[16,128,2048]{2,1,0:T(8,128)S(1)}, f32[16,128,2048]{2,1,0:T(8,128)}, u32[]{:S(2)}) copy-start(f32[16,128,2048]{2,1,0:T(8,128)} %copy-done) | copy-start | bytes 50331652
  75.5 48.7 %copy-start.2 = (f32[16,128,2048]{2,1,0:T(8,128)S(1)}, f32[16,128,2048]{2,1,0:T(8,128)}, u32[]{:S(2)}) copy-start(f32[16,128,2048]{2,1,0:T(8,128)} %copy-done) | copy-start | bytes 50331652
  91.3 7.8 %collective-permute-start.5 = (f32[8,8,256]{2,1,0:T(8,128)S(1)}, f32[8,8,256]{2,1,0:T(8,128)S(1)}, u32[]{:S(2)}, u32[]{:S(2)}) collective-permute-start(f32[8,8,256]{2,1,0:T(8,128)S(1)} %get-tuple-element.32), channel_id=1, source_target_pairs={{0,16},{16,0},{32,48},{48,32},{64,80},{80,64},{96,112},{112,96},{1... | collective-permute-start | bytes 196616 | tf_op jit(solution)/shard_map/ppermute | solution.py:306
  93.6 9.2 %collective-permute-start.6 = (f32[8,8,256]{2,1,0:T(8,128)S(1)}, f32[8,8,256]{2,1,0:T(8,128)S(1)}, u32[]{:S(2)}, u32[]{:S(2)}) collective-permute-start(f32[8,8,256]{2,1,0:T(8,128)S(1)} %get-tuple-element.33), channel_id=1, source_target_pairs={{16,32},{48,64},{80,96},{112,128},{144,160},{176,192},{208,224},{3... | collective-permute-start | bytes 196616 | tf_op jit(solution)/shard_map/ppermute | solution.py:306
  138.1 6.5 %collective-permute-start.7 = (f32[8,8,256]{2,1,0:T(8,128)S(1)}, f32[8,8,256]{2,1,0:T(8,128)S(1)}, u32[]{:S(2)}, u32[]{:S(2)}) collective-permute-start(f32[8,8,256]{2,1,0:T(8,128)S(1)} %get-tuple-element.38), channel_id=1, source_target_pairs={{0,16},{16,0},{32,48},{48,32},{64,80},{80,64},{96,112},{112,96},{1... | collective-permute-start | bytes 196616 | tf_op jit(solution)/shard_map/ppermute | solution.py:306
  138.7 9.2 %collective-permute-start.8 = (f32[8,8,256]{2,1,0:T(8,128)S(1)}, f32[8,8,256]{2,1,0:T(8,128)S(1)}, u32[]{:S(2)}, u32[]{:S(2)}) collective-permute-start(f32[8,8,256]{2,1,0:T(8,128)S(1)} %get-tuple-element.39), channel_id=1, source_target_pairs={{16,32},{48,64},{80,96},{112,128},{144,160},{176,192},{208,224},{3... | collective-permute-start | bytes 196616 | tf_op jit(solution)/shard_map/ppermute | solution.py:306

commit v2 on v1

v2 whole, which is shorter than its diff:
```python
import functools

import jax
import jax.numpy as jnp
from jax import lax
from jax.experimental import pallas as pl
from jax.experimental.pallas import tpu as pltpu
from jax.sharding import PartitionSpec as P

SWEEPS = 4
OMEGA = 0.8
RELAX = 0.5
SOFTEN = 0.01
H = 8
HIGH = lax.Precision.HIGHEST
F32 = jnp.float32


def iota(shape, axis):
    return lax.broadcasted_iota(jnp.int32, shape, axis)


def pick(flag, shape, yes, no):
    return jnp.where(jnp.full(shape, flag, jnp.int32) == 1, yes, no)


def place(me_ref, n_col):
    me = me_ref[0]
    gz = lax.rem(me, 2)
    col = lax.rem(me // 2, n_col)
    row = me // (2 * n_col)
    return row, col, gz


def layer_of(own_ref, other_ref, kind, z, gz, shape):
    mine = pick(gz, shape, 1, 0) == z // 2
    return jnp.where(mine, own_ref[kind, z % 2], other_ref[kind, z % 2])


def col_pack(n_col, me_ref, own_ref, other_ref, a_ref, b_ref):
    _, col, gz = place(me_ref, n_col)
    shape = own_ref.shape[2:]
    lane = iota(shape, 1)
    left = jnp.zeros(shape, F32)
    right = jnp.zeros(shape, F32)
    for s in range(12):
        cell = layer_of(own_ref, other_ref, s // 4, s % 4, gz, shape)
        here = (lane >= 8 * s) & (lane < 8 * s + 8)
        low = pltpu.roll(cell, 8 * s, 1) if s else cell
        left = jnp.where(here, low, left)
        right = jnp.where(here, pltpu.roll(cell, 8 * s + 8, 1), right)
    odd = lax.rem(col, 2)
    a_ref[...] = pick(odd, shape, left, right)
    b_ref[...] = pick(odd, shape, right, left)


def row_pack(n_col, me_ref, own_ref, other_ref, a_in, b_in, info_ref, ext_ref, a_ref, b_ref, told_ref):
    row, col, gz = place(me_ref, n_col)
    shape = own_ref.shape[2:]
    rows, lanes = shape
    lane = iota(shape, 1)
    odd_col = lax.rem(col, 2)
    from_right = pick(odd_col, shape, b_in[...], a_in[...])
    from_left = pick(odd_col, shape, a_in[...], b_in[...])
    odd = lax.rem(row, 2)
    edge = (H, 2 * lanes)
    for s in range(12):
        cell = layer_of(own_ref, other_ref, s // 4, s % 4, gz, shape)
        low = pltpu.roll(from_right, lanes - 8 * s, 1) if s else from_right
        high = pltpu.roll(from_left, lanes - 8 - 8 * s, 1)
        side = jnp.where(lane < 8, low, jnp.where(lane >= lanes - 8, high, 0.0))
        ext_ref[s, :, 0:lanes] = cell
        ext_ref[s, :, lanes : 2 * lanes] = side
        top = ext_ref[s, 0:H, :]
        bottom = ext_ref[s, rows - H : rows, :]
        a_ref[s] = pick(odd, edge, top, bottom)
        b_ref[s] = pick(odd, edge, bottom, top)
    for k in range(told_ref.shape[0]):
        told_ref[k] = info_ref[...]


def sweep(now_ref, next_ref, force_ref, weight_ref):
    rows, lanes = now_ref.shape[2:]

    def image(m, carry):
        for z in range(4):
            cell = now_ref[m, z]
            beside = pltpu.roll(cell, 1, 0) + pltpu.roll(cell, rows - 1, 0)
            beside = beside + (pltpu.roll(cell, 1, 1) + pltpu.roll(cell, lanes - 1, 1))
            if z > 0:
                beside = beside + now_ref[m, z - 1]
            if z < 3:
                beside = beside + now_ref[m, z + 1]
            next_ref[m, z] = (1.0 - OMEGA) * cell + (force_ref[m, z] + weight_ref[z] * beside)
        return carry

    lax.fori_loop(0, now_ref.shape[0], image, 0)


def trace_of(rows, owner, first_row):
    span = rows.shape[0] // 2
    nodes = owner.shape[1]
    line = iota((2 * span, nodes), 0)
    line = line + first_row + jnp.where(line >= span, 64 - span, 0)
    at_row = jnp.where(line == owner // 128, 1.0, 0.0).astype(F32)
    at_lane = iota((128, nodes), 0) == lax.rem(owner, 128)
    found = lax.dot_general(rows, at_row, (((0,), (0,)), ((), ())), precision=HIGH, preferred_element_type=F32)
    return jnp.sum(jnp.where(at_lane, found, 0.0), axis=0, keepdims=True)


def two_layers(field_ref, m, gz, start, size):
    return jnp.concatenate([field_ref[m, 2 * gz + k, start : start + size, 0:128] for k in range(2)], 0)


def prepare(me_ref, table_ref, source_ref, class_ref, owner_ref, pos_ref, node_ref, pack_ref, info_ref):
    for k in range(2):
        level = class_ref[k]
        found = jnp.zeros(level.shape, F32)
        for n in range(table_ref.shape[0]):
            found = jnp.where(level == n, table_ref[n], found)
        pack_ref[2, k] = OMEGA / (6.0 + found)
        for m in range(2):
            pack_ref[m, k] = source_ref[m, k]
    info_ref[...] = jnp.zeros_like(info_ref)
    info_ref[2:5, :] = pos_ref[...]
    info_ref[5:6, :] = owner_ref[...].astype(F32)
    info_ref[6:7, :] = node_ref[...]


def first_relax(n_col, me_ref, ext_ref, a_in, b_in, info_ref, full_ref, first_ref, sent_ref, force, spare):
    row, _, gz = place(me_ref, n_col)
    odd = lax.rem(row, 2)
    edge = a_in.shape[1:]
    for s in range(12):
        full_ref[s // 4, s % 4, 0:H, :] = pick(odd, edge, a_in[s], b_in[s])
        full_ref[s // 4, s % 4, H : H + 64, :] = ext_ref[s]
        full_ref[s // 4, s % 4, H + 64 : 2 * H + 64, :] = pick(odd, edge, b_in[s], a_in[s])
    weight = full_ref.at[2]
    for m in range(2):
        for z in range(4):
            force[m, z] = full_ref[m, z] * weight[z]
    sweep(force, first_ref, force, weight)
    sweep(first_ref, spare, force, weight)
    sweep(spare, first_ref, force, weight)
    owner = info_ref[5:6, :].astype(jnp.int32)
    line = iota(info_ref.shape, 0)
    info = info_ref[...]
    for m in range(2):
        info = jnp.where(line == m, trace_of(two_layers(first_ref, m, gz, H, 64), owner, 0), info)
    for k in range(sent_ref.shape[0]):
        sent_ref[k] = info


def carry_relax(n_col, me_ref, full_ref, first_ref, info_ref, keep_ref, trace_ref, force, spare, other):
    _, _, gz = place(me_ref, n_col)
    weight = full_ref.at[2]
    for m in range(2):
        for z in range(4):
            force[m, z] = (full_ref[m, z] - RELAX * first_ref[m, z]) * weight[z]
    sweep(first_ref, spare, force, weight)
    sweep(spare, other, force, weight)
    sweep(other, spare, force, weight)
    sweep(spare, other, force, weight)
    owner = info_ref[5:6, :].astype(jnp.int32)
    for m in range(2):
        for k in range(2):
            keep_ref[m, k] = other[m, 2 * gz + k, H : H + 64, 0:128]
        trace_ref[m : m + 1, :] = trace_of(two_layers(other, m, gz, H, 64), owner, 0)


def columns(rows, count):
    nodes = rows.shape[1]
    return [jnp.broadcast_to(rows[k : k + 1, :], (nodes, nodes)).T for k in range(count)]


def finish_apply(n_col, col, gz, acc, lined, own, out_ref):
    lined[...] = jnp.zeros_like(lined)
    for t in range(2 * n_col):
        mine = jnp.where(2 * col + gz == t, -0.5, 0.0).astype(F32)
        for m in range(2):
            whole = jnp.sum(acc[m, t], axis=0, keepdims=True)
            lined[m, t + 2 : t + 3, :] = whole + mine * own[m : m + 1, :]
    for c in range(n_col):
        for m in range(2):
            near = lined[m, 2 * c : 2 * c + 8, :]
            out_ref[2 * c, 8 * m : 8 * m + 8, :] = near
            out_ref[2 * c + 1, 8 * m : 8 * m + 8, :] = near


def build_apply(n_col, n_row, me_ref, heard_ref, target_ref, pair_ref, out_ref, acc, lined):
    step = pl.program_id(0)
    row, col, gz = place(me_ref, n_col)
    nodes = heard_ref.shape[2]

    @pl.when(step == 0)
    def _():
        acc[...] = jnp.zeros_like(acc)

    heard = heard_ref[step]
    at = columns(heard[2:5, :], 3)
    by = columns(heard[0:2, :] * heard[6:7, :], 2)
    for t in range(target_ref.shape[0]):
        dx = target_ref[t, 2:3, :] - at[0]
        dy = target_ref[t, 3:4, :] - at[1]
        dz = target_ref[t, 4:5, :] - at[2]
        inverse = lax.rsqrt(dx * dx + dy * dy + (dz * dz + SOFTEN))
        pair = dz * inverse * (inverse * inverse)
        pair_ref[0, :, t * nodes : (t + 1) * nodes] = pair
        for m in range(2):
            acc[m, t] = acc[m, t] + jnp.sum((pair * by[m]).reshape(nodes // 8, 8, nodes), axis=0)

    @pl.when(step == n_row - 1)
    def _():
        finish_apply(n_col, col, gz, acc, lined, heard_ref[row], out_ref)


def reapply(n_col, steps, me_ref, heard_ref, info_ref, pair_ref, out_ref, acc, lined, trace):
    step = pl.program_id(0)
    row, col, gz = place(me_ref, n_col)
    nodes = heard_ref.shape[2]
    n_row = heard_ref.shape[0]

    @pl.when(step == 0)
    def _():
        acc[...] = jnp.zeros_like(acc)
        for k in range(n_row):
            whole = heard_ref[k, 0:2, :]
            if k + 1 < n_row:
                whole = whole + heard_ref[k + 1, 2:4, :]
            if k > 0:
                whole = whole + heard_ref[k - 1, 4:6, :]
            trace[k, 0:2, :] = whole
            trace[k, 2:4, :] = whole * info_ref[k, 6:7, :]

    for k in range(pair_ref.shape[0]):
        by = columns(trace[step * pair_ref.shape[0] + k, 2:4, :], 2)
        for t in range(2 * n_col):
            pair = pair_ref[k, :, t * nodes : (t + 1) * nodes]
            for m in range(2):
                acc[m, t] = acc[m, t] + jnp.sum((pair * by[m]).reshape(nodes // 8, 8, nodes), axis=0)

    @pl.when(step == steps - 1)
    def _():
        finish_apply(n_col, col, gz, acc, lined, trace[row], out_ref)


def spread_nodes(n_col, col, part_ref, target_ref, spread_ref):
    nodes = part_ref.shape[2]
    blocks = 2 * n_col
    value = part_ref[0]
    for k in range(1, blocks):
        value = value + part_ref[k]
    shape = (128, nodes)
    down = iota(shape, 0)
    weighted, lanes = [], []
    for b in range(6):
        at = jnp.clip(2 * col - 2 + b, 0, blocks - 1)
        owner = target_ref[at, 5:6, :].astype(jnp.int32)
        hit = down == owner // 128
        weighted.append(
            jnp.concatenate([jnp.where(hit, value[8 * m + b : 8 * m + b + 1, :], 0.0) for m in range(2)], 0)
        )
        lane = down == lax.rem(owner, 128)
        if b < 2:
            lane = lane & (down >= 128 - H)
        if b > 3:
            lane = lane & (down < H)
        lanes.append(jnp.where(lane, 1.0, 0.0).astype(F32))

    def product(a, b):
        return lax.dot_general(a, b, (((1,), (1,)), ((), ())), precision=HIGH, preferred_element_type=F32)

    for g in range(2):
        own = product(weighted[2 + g], lanes[2 + g])
        side = product(
            jnp.concatenate([weighted[g], weighted[4 + g]], 1), jnp.concatenate([lanes[g], lanes[4 + g]], 1)
        )
        for m in range(2):
            for k in range(2):
                start = 128 * m + 64 * k
                spread_ref[4 * m + 2 * g + k, :, 0:128] = own[start : start + 64]
                spread_ref[4 * m + 2 * g + k, :, 128:256] = side[start : start + 64]
    return value


def respond(
    n_col, n_row, me_ref, part_ref, target_ref, full_ref, heard_ref, kept_ref,
    spread_ref, sent_ref, force, spare, other,
):
    row, col, gz = place(me_ref, n_col)
    weight = full_ref.at[2]
    spread_nodes(n_col, col, part_ref, target_ref, spread_ref)
    empty = jnp.zeros((H, 256), F32)
    for m in range(2):
        for z in range(4):
            force[m, z, 0:H, :] = empty
            force[m, z, H : H + 64, :] = spread_ref[4 * m + z] * weight[z, H : H + 64]
            force[m, z, H + 64 : 2 * H + 64, :] = empty
    sweep(force, spare, force, weight)
    sweep(spare, other, force, weight)
    sweep(other, spare, force, weight)
    for m in range(2):
        for z in range(4):
            force[m, z] = (-RELAX * spare[m, z]) * weight[z]
    sweep(force, other, force, weight)
    sweep(other, spare, force, weight)
    sweep(spare, other, force, weight)
    own = heard_ref[row, 5:6, :].astype(jnp.int32)
    above = heard_ref[jnp.maximum(row - 1, 0), 5:6, :].astype(jnp.int32)
    below = heard_ref[jnp.minimum(row + 1, n_row - 1), 5:6, :].astype(jnp.int32)
    line = iota((8, own.shape[1]), 0)
    sent = jnp.zeros((8, own.shape[1]), F32)
    for m in range(2):
        here = trace_of(two_layers(other, m, gz, H, 64), own, 0) + kept_ref[m : m + 1, :]
        sent = jnp.where(line == m, here, sent)
        sent = jnp.where(line == 2 + m, trace_of(two_layers(other, m, gz, 0, H), above, 64 - H), sent)
        sent = jnp.where(line == 4 + m, trace_of(two_layers(other, m, gz, H + 64, H), below, 0), sent)
    for k in range(sent_ref.shape[0]):
        sent_ref[k] = sent


def last_spread(n_col, me_ref, part_ref, target_ref, before_ref, spread_ref, a_ref, b_ref, value_ref):
    row, col, gz = place(me_ref, n_col)
    value = spread_nodes(n_col, col, part_ref, target_ref, spread_ref)
    odd = lax.rem(row, 2)
    edge = (H, 256)
    for s in range(16):
        from_ref = before_ref if s < 8 else spread_ref
        top = from_ref[s % 8, 0:H, :]
        bottom = from_ref[s % 8, 64 - H : 64, :]
        a_ref[s] = pick(odd, edge, top, bottom)
        b_ref[s] = pick(odd, edge, bottom, top)
    for m in range(2):
        value_ref[m : m + 1, :] = pick(
            gz, (1, value.shape[1]), value[8 * m + 3 : 8 * m + 4, :], value[8 * m + 2 : 8 * m + 3, :]
        )


def last_relax(
    n_col, me_ref, full_ref, before_ref, spread_ref, a_in, b_in, keep_ref, out_ref, force, spare, other, later
):
    row, _, gz = place(me_ref, n_col)
    odd = lax.rem(row, 2)
    weight = full_ref.at[2]
    edge = (H, 256)
    for s in range(16):
        m, z = s % 8 // 4, s % 4
        into, own = (force, before_ref) if s < 8 else (later, spread_ref)
        into[m, z, 0:H, :] = pick(odd, edge, a_in[s], b_in[s]) * weight[z, 0:H]
        into[m, z, H : H + 64, :] = own[4 * m + z] * weight[z, H : H + 64]
        into[m, z, H + 64 : 2 * H + 64, :] = pick(odd, edge, b_in[s], a_in[s]) * weight[z, H + 64 : 2 * H + 64]
    sweep(force, spare, force, weight)
    sweep(spare, other, force, weight)
    sweep(other, spare, force, weight)
    for m in range(2):
        for z in range(4):
            later[m, z] = later[m, z] - (RELAX * spare[m, z]) * weight[z]
    sweep(spare, other, later, weight)
    sweep(other, spare, later, weight)
    sweep(spare, other, later, weight)
    sweep(other, spare, later, weight)
    for m in range(2):
        for k in range(2):
            out_ref[m, k] = keep_ref[m, k] + spare[m, 2 * gz + k, H : H + 64, 0:128]


SMEM = pl.BlockSpec(memory_space=pltpu.SMEM)
VMEM = pl.BlockSpec(memory_space=pltpu.VMEM)


def size_of(shape):
    return functools.reduce(lambda a, b: a * b, shape)


def run(body, name, outs, args, scratch=(), flops=0, scalars=1):
    moved = sum(a.size * 4 for a in args) + sum(4 * size_of(o) for o in outs)
    return pl.pallas_call(
        body,
        name=name,
        out_shape=[jax.ShapeDtypeStruct(o, F32) for o in outs],
        in_specs=[SMEM] * scalars + [VMEM] * (len(args) - scalars),
        out_specs=[VMEM] * len(outs),
        scratch_shapes=[pltpu.VMEM(s, F32) for s in scratch],
        compiler_params=pltpu.CompilerParams(vmem_limit_bytes=20 << 20),
        cost_estimate=pl.CostEstimate(flops=flops, bytes_accessed=moved, transcendentals=0),
    )(*args)


def on_device(n_row, n_col, source, cell_class, coeff_table, owner_cell, node_pos, node_weight):
    nodes = owner_cell.shape[0]
    blocks = 2 * n_col
    me = lax.axis_index(("row", "col", "gz")).reshape(1)

    def swaps(axis, size, a, b):
        first = [(i, i ^ 1) for i in range(size)]
        second = [(i + 1, i + 2) for i in range(0, size - 2, 2)]
        second = second + [(j, i) for i, j in second]
        return lax.ppermute(a, axis, first), lax.ppermute(b, axis, second)

    packed, info = run(
        prepare,
        "prepare",
        [(3, 2, 64, 128), (8, nodes)],
        [me, coeff_table, source, cell_class, owner_cell[None, :], node_pos, node_weight[None, :]],
        scalars=2,
    )
    other = lax.ppermute(packed, "gz", [(0, 1), (1, 0)])
    a, b = run(functools.partial(col_pack, n_col), "col_pack", [(64, 128)] * 2, [me, packed, other])
    a, b = swaps("col", n_col, a, b)
    ext, a, b, told = run(
        functools.partial(row_pack, n_col),
        "row_pack",
        [(12, 64, 256), (12, H, 256), (12, H, 256), (blocks, 8, nodes)],
        [me, packed, other, a, b, info],
    )
    a, b = swaps("row", n_row, a, b)
    target = lax.all_to_all(told, ("col", "gz"), 0, 0)

    field = (2, 4, 64 + 2 * H, 256)
    full, first, sent = run(
        functools.partial(first_relax, n_col),
        "first_relax",
        [(3, 4, 64 + 2 * H, 256), field, (n_row, 8, nodes)],
        [me, ext, a, b, info],
        [field] * 2,
    )
    heard = lax.all_to_all(sent, "row", 0, 0)
    keep, kept = run(
        functools.partial(carry_relax, n_col),
        "carry_relax",
        [(2, 2, 64, 128), (2, nodes)],
        [me, full, first, info],
        [field] * 3,
        flops=40 * size_of(field),
    )

    everything = lambda shape: pl.BlockSpec(shape, lambda i: (0,) * len(shape))
    work = n_row * blocks * nodes * nodes
    sums = [pltpu.VMEM((2, blocks, 8, nodes), F32), pltpu.VMEM((2, blocks + 8, nodes), F32)]
    pairs, partial = pl.pallas_call(
        functools.partial(build_apply, n_col, n_row),
        name="build_apply",
        grid=(n_row,),
        out_shape=[
            jax.ShapeDtypeStruct((n_row, nodes, blocks * nodes), F32),
            jax.ShapeDtypeStruct((blocks, 16, nodes), F32),
        ],
        in_specs=[SMEM, everything((n_row, 8, nodes)), everything((blocks, 8, nodes))],
        out_specs=[
            pl.BlockSpec((1, nodes, blocks * nodes), lambda i: (i, 0, 0)),
            everything((blocks, 16, nodes)),
        ],
        scratch_shapes=sums,
        compiler_params=pltpu.CompilerParams(vmem_limit_bytes=16 << 20),
        cost_estimate=pl.CostEstimate(flops=18 * work, bytes_accessed=4 * work, transcendentals=work),
    )(me, heard, target)
    partial = lax.all_to_all(partial, ("col", "gz"), 0, 0)
    before, sent = run(
        functools.partial(respond, n_col, n_row),
        "respond",
        [(8, 64, 256), (n_row, 8, nodes)],
        [me, partial, target, full, heard, kept],
        [field] * 3,
    )
    again = lax.all_to_all(sent, "row", 0, 0)
    group = 2
    partial = pl.pallas_call(
        functools.partial(reapply, n_col, n_row // group),
        name="reapply",
        grid=(n_row // group,),
        out_shape=jax.ShapeDtypeStruct((blocks, 16, nodes), F32),
        in_specs=[
            SMEM,
            everything((n_row, 8, nodes)),
            everything((n_row, 8, nodes)),
            pl.BlockSpec((group, nodes, blocks * nodes), lambda i: (i, 0, 0)),
        ],
        out_specs=everything((blocks, 16, nodes)),
        scratch_shapes=sums + [pltpu.VMEM((n_row, 8, nodes), F32)],
        compiler_params=pltpu.CompilerParams(vmem_limit_bytes=20 << 20),
        cost_estimate=pl.CostEstimate(flops=4 * work, bytes_accessed=4 * work, transcendentals=0),
    )(me, again, heard, pairs)
    partial = lax.all_to_all(partial, ("col", "gz"), 0, 0)
    spread, a, b, values = run(
        functools.partial(last_spread, n_col),
        "last_spread",
        [(8, 64, 256), (16, H, 256), (16, H, 256), (2, nodes)],
        [me, partial, target, before],
    )
    a, b = swaps("row", n_row, a, b)
    (potential,) = run(
        functools.partial(last_relax, n_col),
        "last_relax",
        [(2, 2, 64, 128)],
        [me, full, before, spread, a, b, keep],
        [field] * 4,
    )
    return potential, values


def solution(mesh):
    return jax.shard_map(
        functools.partial(on_device, mesh.shape["row"], mesh.shape["col"]),
        mesh=mesh,
        in_specs=(
            P(None, "gz", "row", "col"),
            P("gz", "row", "col"),
            P(),
            P(("row", "col", "gz")),
            P(None, ("row", "col", "gz")),
            P(("row", "col", "gz")),
        ),
        out_specs=(P(None, "gz", "row", "col"), P(None, ("row", "col", "gz"))),
        check_vma=False,
    )
```

time: 152 us -> 143 us (0.941)
  starting transfers between devices: 47.4 us -> 31 us
  waiting for transfers between devices: 12.2 us -> 24.1 us
  other arithmetic: 8.29 us -> 0 us
  Pallas kernels: 27.8 us -> 32.4 us
    all_to_all x3 -> x2, starting transfers between devices: 24.8 us -> 15.1 us  [the longest x1 9.71 us: on_device(): target = lax.all_to_all(told, ('col', 'gz'), 0, 0)]
    ppermute x8 -> x6, starting transfers between devices: 20.5 us -> 13.8 us  [swaps(): return (lax.ppermute(a, axis, first), lax.ppermute(b, axis, second))]
    broadcast_in_dim x1 -> x0, other arithmetic: 6.02 us -> none  [on_device(): packed = jnp.concatenate([source, (OMEGA / (6.0 + summed))[None]], 0)]
    ppermute x8 -> x6, waiting for transfers between devices: 9.41 us -> 15.2 us  [swaps(): return (lax.ppermute(a, axis, first), lax.ppermute(b, axis, second))]
    ppermute x1, waiting for transfers between devices: 0.01 us -> 4.9 us  [on_device(): other = lax.ppermute(packed, 'gz', [(0, 1), (1, 0)])]
    pallas_call x7 -> x8, Pallas kernels: 12 us -> 16.9 us  [run(): pl.pallas_call(body, name=name, out_shape=[jax.ShapeDtypeStruct(o, F32) f...]
    unnamed x14 -> x16, local copies, waits for them, and re-layouts: 12.8 us -> 15.9 us
    broadcast_in_dim x4 -> x0, local copies, waits for them, and re-layouts: 2.54 us -> none  [gathered(): jnp.broadcast_to(x[None], (count,) + x.shape)]
  transfers between devices with their start and end apart: 12 -> 9, of which waited for: 4 -> 6; matrix products, arithmetic and copies ran while one was open for 2% -> 0% of each run, Pallas kernels for 7% -> 3%
where the time goes in v2:
time: 143 us
  blocking collectives  38.5 us (27%)
  Pallas kernels  32.4 us (23%)
  starting transfers between devices  31 us (22%)
  waiting for transfers between devices  24.1 us (17%)
  local copies, waits for them, and re-layouts  15.9 us (11%)
    pallas_call x8, Pallas kernels, run(): pl.pallas_call(body, name=name, out_shape=[jax.ShapeDtypeStruct(o, F32) f...  16.9 us
    all_to_all x1, blocking collectives, on_device(): heard = lax.all_to_all(sent, 'row', 0, 0)  16.5 us
    unnamed x16, local copies, waits for them, and re-layouts  15.9 us
    ppermute x6, waiting for transfers between devices, swaps(): return (lax.ppermute(a, axis, first), lax.ppermute(b, axis, second))  15.2 us
    ppermute x6, starting transfers between devices, swaps(): return (lax.ppermute(a, axis, first), lax.ppermute(b, axis, second))  13.8 us
    all_to_all x1, blocking collectives, on_device(): again = lax.all_to_all(sent, 'row', 0, 0)  12.9 us
    pallas_call x1, Pallas kernels, on_device(): pl.pallas_call(functools.partial(build_apply, n_col, n_row), name='build_...  12 us
    all_to_all x1, starting transfers between devices, on_device(): target = lax.all_to_all(told, ('col', 'gz'), 0, 0)  9.71 us
  transfers between devices with their start and end apart: 9, of which 6 were waited for; matrix products, arithmetic and copies ran while one was open for 0% of the time, Pallas kernels for 3%

profile of v2, /device:TPU:8, one launch (start us, length us, event | category | flops | bytes accessed | tf_op | source)
XLA Modules:
  0.0 142.6 jit_solution(4802409671452221935)
XLA Ops:
  0.6 0.9 copy-done.2
  1.5 0.8 copy-done.3
  2.4 0.7 copy-done.4
  3.1 0.7 copy-done.5
  3.7 0.7 copy-done.6
  4.4 0.7 copy-done.7
  5.6 2.0 %collective-permute-start = (f32[3,2,64,128]{3,2,1,0:T(8,128)S(1)}, f32[3,2,64,128]{3,2,1,0:T(8,128)S(1)}, u32[]{:S(2)}, u32[]{:S(2)}) collective-permute-start(f32[3,2,64,128]{3,2,1,0:T(8,128)S(1)} %get-tuple-element.23.own_ref), channel_id=1, source_target_pairs={{0,1},{1,0},{2,3},{3,2},{4,5},{5,4},{6,7},{7,6},{8,9},{9,8},{10,11... | collective-permute-start | bytes 589832 | tf_op jit(solution)/shard_map/ppermute | solution.py:407
  7.6 4.9 %collective-permute-done.other_ref = f32[3,2,64,128]{3,2,1,0:T(8,128)S(1)} collective-permute-done((f32[3,2,64,128]{3,2,1,0:T(8,128)S(1)}, f32[3,2,64,128]{3,2,1,0:T(8,128)S(1)}, u32[]{:S(2)}, u32[]{:S(2)}) %collective-permute-start) | collective-permute-done | bytes 196640 | tf_op jit(solution)/shard_map/ppermute | solution.py:407
  12.9 0.7 collective-permute-start.2
  14.1 0.9 row_pack.1
  15.0 9.7 %all-to-all-start.1 = ((f32[16,8,128]{2,1,0:T(8,128)}), f32[16,8,128]{2,1,0:T(8,128)S(1)}, u32[]{:S(2)}, u32[]{:S(2)}) async-start(f32[16,8,128]{2,1,0:T(8,128)} %get-tuple-element.32), calls=%async_computation.1 | async-start | bytes 131072 | tf_op jit(solution)/shard_map/all_to_all | solution.py:417
  24.7 3.4 %collective-permute-start.3 = (f32[12,8,256]{2,1,0:T(8,128)S(1)}, f32[12,8,256]{2,1,0:T(8,128)S(1)}, u32[]{:S(2)}, u32[]{:S(2)}) collective-permute-start(f32[12,8,256]{2,1,0:T(8,128)S(1)} %get-tuple-element.28), channel_id=1, source_target_pairs={{0,16},{16,0},{32,48},{48,32},{64,80},{80,64},{96,112},{112,96},{1... | collective-permute-start | bytes 294920 | tf_op jit(solution)/shard_map/ppermute | solution.py:398
  28.0 5.4 %collective-permute-start.4 = (f32[12,8,256]{2,1,0:T(8,128)S(1)}, f32[12,8,256]{2,1,0:T(8,128)S(1)}, u32[]{:S(2)}, u32[]{:S(2)}) collective-permute-start(f32[12,8,256]{2,1,0:T(8,128)S(1)} %get-tuple-element.29), channel_id=1, source_target_pairs={{16,32},{48,64},{80,96},{112,128},{144,160},{176,192},{208,224},{3... | collective-permute-start | bytes 294920 | tf_op jit(solution)/shard_map/ppermute | solution.py:398
  33.4 6.3 %collective-permute-done.4.b_in = f32[12,8,256]{2,1,0:T(8,128)S(1)} collective-permute-done((f32[12,8,256]{2,1,0:T(8,128)S(1)}, f32[12,8,256]{2,1,0:T(8,128)S(1)}, u32[]{:S(2)}, u32[]{:S(2)}) %collective-permute-start.4) | collective-permute-done | bytes 98336 | tf_op jit(solution)/shard_map/ppermute | solution.py:398
  39.7 2.0 %first_relax.1 = (f32[3,4,80,256]{3,2,1,0:T(8,128)S(1)}, f32[2,4,80,256]{3,2,1,0:T(8,128)S(1)}, f32[16,8,128]{2,1,0:T(8,128)S(1)}) custom-call(s32[1]{0:T(128)} %bitcast.me_ref, f32[12,64,256]{2,1,0:T(8,128)S(1)} %get-tuple-element.27.ext_ref, f32[12,8,256]{2,1,0:T(8,128)S(1)} %collective-permute-done.3.a_in, f32[12,8,256]{2,1,0:T(8,128)S(1)} %collective-permute-done.4.b_in, ...), custom_call_target="tpu_custom_call" | custom-call | bytes 2691076 | tf_op jit(solution)/shard_map/first_relax/pallas_call | solution.py:377
  41.8 16.5 %all_to_all.25.heard_ref.info_ref = f32[16,8,128]{2,1,0:T(8,128)S(1)} all-to-all(f32[16,8,128]{2,1,0:T(8,128)S(1)} %get-tuple-element.31), channel_id=1, replica_groups=mesh['row'=16,'col'=8,'gz'=2] {'row'}, dimensions={0} | all-to-all | bytes 131072 | tf_op jit(solution)/shard_map/all_to_all | solution.py:427
  58.2 12.0 %build_apply.1 = (f32[16,128,2048]{2,1,0:T(8,128)S(1)}, f32[16,16,128]{2,1,0:T(8,128)}) custom-call(s32[1]{0:T(128)} %bitcast.me_ref, f32[16,8,128]{2,1,0:T(8,128)S(1)} %all_to_all.25.heard_ref.info_ref, f32[16,8,128]{2,1,0:T(8,128)S(1)} %all-to-all-done.1.target_ref), custom_call_target="tpu_custom_call" | custom-call | flops 75497472 | bytes 16777216 | tf_op jit(solution)/shard_map/build_apply/pallas_call | solution.py:440
  70.2 5.7 %copy-done = f32[16,128,2048]{2,1,0:T(8,128)} copy-done((f32[16,128,2048]{2,1,0:T(8,128)}, f32[16,128,2048]{2,1,0:T(8,128)S(1)}, u32[]{:S(2)}) %copy-start) | copy-done | bytes 16777240
  75.9 5.4 %all-to-all-start.2 = ((f32[16,16,128]{2,1,0:T(8,128)}), f32[16,16,128]{2,1,0:T(8,128)S(1)}, u32[]{:S(2)}, u32[]{:S(2)}) async-start(f32[16,16,128]{2,1,0:T(8,128)} %get-tuple-element.33), calls=%async_computation.2 | async-start | bytes 262144 | tf_op jit(solution)/shard_map/all_to_all | solution.py:457
  81.3 2.5 %carry_relax.1 = (f32[2,2,64,128]{3,2,1,0:T(8,128)S(1)}, f32[2,128]{1,0:T(2,128)S(1)}) custom-call(s32[1]{0:T(128)} %bitcast.me_ref, f32[3,4,80,256]{3,2,1,0:T(8,128)S(1)} %get-tuple-element.30.full_ref, f32[2,4,80,256]{3,2,1,0:T(8,128)S(1)} %get-tuple-element.34.first_ref, f32[8,128]{1,0:T(8,128)S(1)} %get-tuple-element.26.info_ref), custom_call_target="tpu_custom_call" | custom-call | flops 6553600 | bytes 1774596 | tf_op jit(solution)/shard_map/carry_relax/pallas_call | solution.py:377
  83.8 4.0 %all-to-all-done.2.part_ref = f32[16,16,128]{2,1,0:T(8,128)S(1)} async-done(((f32[16,16,128]{2,1,0:T(8,128)}), f32[16,16,128]{2,1,0:T(8,128)S(1)}, u32[]{:S(2)}, u32[]{:S(2)}) %all-to-all-start.2) | async-done | bytes 131104 | tf_op jit(solution)/shard_map/all_to_all | solution.py:457
  87.9 4.9 %respond.1 = (f32[8,64,256]{2,1,0:T(8,128)S(1)}, f32[16,8,128]{2,1,0:T(8,128)S(1)}) custom-call(s32[1]{0:T(128)} %bitcast.me_ref, f32[16,16,128]{2,1,0:T(8,128)S(1)} %all-to-all-done.2.part_ref, f32[16,8,128]{2,1,0:T(8,128)S(1)} %all-to-all-done.1.target_ref, f32[3,4,80,256]{3,2,1,0:T(8,128)S(1)} %get-tuple-element.30.full_ref, ...), custom_call_target="tpu_custom_call" | custom-call | bytes 1836036 | tf_op jit(solution)/shard_map/respond/pallas_call | solution.py:377
  92.7 12.9 %all_to_all.26.heard_ref = f32[16,8,128]{2,1,0:T(8,128)S(1)} all-to-all(f32[16,8,128]{2,1,0:T(8,128)S(1)} %get-tuple-element.37), channel_id=1, replica_groups=mesh['row'=16,'col'=8,'gz'=2] {'row'}, dimensions={0} | all-to-all | bytes 131072 | tf_op jit(solution)/shard_map/all_to_all | solution.py:465
  105.6 5.8 %copy-done.1 = f32[16,128,2048]{2,1,0:T(8,128)S(1)} copy-done((f32[16,128,2048]{2,1,0:T(8,128)S(1)}, f32[16,128,2048]{2,1,0:T(8,128)}, u32[]{:S(2)}) %copy-start.1) | copy-done | bytes 16777240
  111.4 3.5 %reapply.1 = f32[16,16,128]{2,1,0:T(8,128)S(1)} custom-call(s32[1]{0:T(128)} %bitcast.me_ref, f32[16,8,128]{2,1,0:T(8,128)S(1)} %all_to_all.26.heard_ref, f32[16,8,128]{2,1,0:T(8,128)S(1)} %all_to_all.25.heard_ref.info_ref, f32[16,128,2048]{2,1,0:T(8,128)S(1)} %copy-done.1), custom_call_target="tpu_custom_call" | custom-call | flops 16777216 | bytes 16777216 | tf_op jit(solution)/shard_map/reapply/pallas_call | solution.py:467
  114.9 9.2 %all_to_all.27.part_ref = f32[16,16,128]{2,1,0:T(8,128)S(1)} all-to-all(f32[16,16,128]{2,1,0:T(8,128)S(1)} %reapply.1), channel_id=1, replica_groups=mesh['row'=16,'col'=8,'gz'=2] {'col','gz'}, dimensions={0} | all-to-all | bytes 262144 | tf_op jit(solution)/shard_map/all_to_all | solution.py:483
  124.1 1.3 last_spread.1
  125.4 0.9 collective-permute-start.5
  126.2 3.5 %collective-permute-start.6 = (f32[16,8,256]{2,1,0:T(8,128)S(1)}, f32[16,8,256]{2,1,0:T(8,128)S(1)}, u32[]{:S(2)}, u32[]{:S(2)}) collective-permute-start(f32[16,8,256]{2,1,0:T(8,128)S(1)} %get-tuple-element.41), channel_id=1, source_target_pairs={{16,32},{48,64},{80,96},{112,128},{144,160},{176,192},{208,224},{3... | collective-permute-start | bytes 393224 | tf_op jit(solution)/shard_map/ppermute | solution.py:398
  129.7 5.0 %collective-permute-done.5.a_in = f32[16,8,256]{2,1,0:T(8,128)S(1)} collective-permute-done((f32[16,8,256]{2,1,0:T(8,128)S(1)}, f32[16,8,256]{2,1,0:T(8,128)S(1)}, u32[]{:S(2)}, u32[]{:S(2)}) %collective-permute-start.5) | collective-permute-done | bytes 131104 | tf_op jit(solution)/shard_map/ppermute | solution.py:398
  134.7 3.4 %collective-permute-done.6.b_in = f32[16,8,256]{2,1,0:T(8,128)S(1)} collective-permute-done((f32[16,8,256]{2,1,0:T(8,128)S(1)}, f32[16,8,256]{2,1,0:T(8,128)S(1)}, u32[]{:S(2)}, u32[]{:S(2)}) %collective-permute-start.6) | collective-permute-done | bytes 131104 | tf_op jit(solution)/shard_map/ppermute | solution.py:398
  138.0 4.5 %last_relax.1 = f32[2,2,64,128]{3,2,1,0:T(8,128)} custom-call(s32[1]{0:T(128)} %bitcast.me_ref, f32[3,4,80,256]{3,2,1,0:T(8,128)S(1)} %get-tuple-element.30.full_ref, f32[8,64,256]{2,1,0:T(8,128)S(1)} %get-tuple-element.36.before_ref, f32[8,64,256]{2,1,0:T(8,128)S(1)} %get-tuple-element.39.spread_ref, f32[16,8,256]{2,1,0:T(8,128)S(1)} %collective-permute-done.5.a_in, ...), custom_call_target="tpu_custom_call" | custom-call | bytes 2555908 | tf_op jit(solution)/shard_map/last_relax/pallas_call | solution.py:377
  (15 shorter events, 1.5 us)
Async XLA Ops:
  0.6 0.9 copy-start.2
  1.5 0.8 copy-start.3
  2.4 0.7 copy-start.4
  3.1 0.7 copy-start.5
  3.7 0.7 copy-start.6
  4.4 0.7 copy-start.7
  5.6 6.9 %collective-permute-start = (f32[3,2,64,128]{3,2,1,0:T(8,128)S(1)}, f32[3,2,64,128]{3,2,1,0:T(8,128)S(1)}, u32[]{:S(2)}, u32[]{:S(2)}) collective-permute-start(f32[3,2,64,128]{3,2,1,0:T(8,128)S(1)} %get-tuple-element.23.own_ref), channel_id=1, source_target_pairs={{0,1},{1,0},{2,3},{3,2},{4,5},{5,4},{6,7},{7,6},{8,9},{9,8},{10,11... | collective-permute-start | bytes 589832 | tf_op jit(solution)/shard_map/ppermute | solution.py:407
  12.8 1.3 collective-permute-start.1
  12.9 1.2 collective-permute-start.2
  15.0 26.8 %all-to-all-start.1 = ((f32[16,8,128]{2,1,0:T(8,128)}), f32[16,8,128]{2,1,0:T(8,128)S(1)}, u32[]{:S(2)}, u32[]{:S(2)}) async-start(f32[16,8,128]{2,1,0:T(8,128)} %get-tuple-element.32), calls=%async_computation.1 | async-start | bytes 131072 | tf_op jit(solution)/shard_map/all_to_all | solution.py:417
  24.7 8.7 %collective-permute-start.3 = (f32[12,8,256]{2,1,0:T(8,128)S(1)}, f32[12,8,256]{2,1,0:T(8,128)S(1)}, u32[]{:S(2)}, u32[]{:S(2)}) collective-permute-start(f32[12,8,256]{2,1,0:T(8,128)S(1)} %get-tuple-element.28), channel_id=1, source_target_pairs={{0,16},{16,0},{32,48},{48,32},{64,80},{80,64},{96,112},{112,96},{1... | collective-permute-start | bytes 294920 | tf_op jit(solution)/shard_map/ppermute | solution.py:398
  28.0 11.7 %collective-permute-start.4 = (f32[12,8,256]{2,1,0:T(8,128)S(1)}, f32[12,8,256]{2,1,0:T(8,128)S(1)}, u32[]{:S(2)}, u32[]{:S(2)}) collective-permute-start(f32[12,8,256]{2,1,0:T(8,128)S(1)} %get-tuple-element.29), channel_id=1, source_target_pairs={{16,32},{48,64},{80,96},{112,128},{144,160},{176,192},{208,224},{3... | collective-permute-start | bytes 294920 | tf_op jit(solution)/shard_map/ppermute | solution.py:398
  70.2 5.7 %copy-start = (f32[16,128,2048]{2,1,0:T(8,128)}, f32[16,128,2048]{2,1,0:T(8,128)S(1)}, u32[]{:S(2)}) copy-start(f32[16,128,2048]{2,1,0:T(8,128)S(1)} %get-tuple-element.38.pair_ref) | copy-start | bytes 50331652
  75.9 12.0 %all-to-all-start.2 = ((f32[16,16,128]{2,1,0:T(8,128)}), f32[16,16,128]{2,1,0:T(8,128)S(1)}, u32[]{:S(2)}, u32[]{:S(2)}) async-start(f32[16,16,128]{2,1,0:T(8,128)} %get-tuple-element.33), calls=%async_computation.2 | async-start | bytes 262144 | tf_op jit(solution)/shard_map/all_to_all | solution.py:457
  105.6 5.8 %copy-start.1 = (f32[16,128,2048]{2,1,0:T(8,128)S(1)}, f32[16,128,2048]{2,1,0:T(8,128)}, u32[]{:S(2)}) copy-start(f32[16,128,2048]{2,1,0:T(8,128)} %copy-done) | copy-start | bytes 50331652
  125.4 9.3 %collective-permute-start.5 = (f32[16,8,256]{2,1,0:T(8,128)S(1)}, f32[16,8,256]{2,1,0:T(8,128)S(1)}, u32[]{:S(2)}, u32[]{:S(2)}) collective-permute-start(f32[16,8,256]{2,1,0:T(8,128)S(1)} %get-tuple-element.40), channel_id=1, source_target_pairs={{0,16},{16,0},{32,48},{48,32},{64,80},{80,64},{96,112},{112,96},{1... | collective-permute-start | bytes 393224 | tf_op jit(solution)/shard_map/ppermute | solution.py:398
  126.2 11.8 %collective-permute-start.6 = (f32[16,8,256]{2,1,0:T(8,128)S(1)}, f32[16,8,256]{2,1,0:T(8,128)S(1)}, u32[]{:S(2)}, u32[]{:S(2)}) collective-permute-start(f32[16,8,256]{2,1,0:T(8,128)S(1)} %get-tuple-element.41), channel_id=1, source_target_pairs={{16,32},{48,64},{80,96},{112,128},{144,160},{176,192},{208,224},{3... | collective-permute-start | bytes 393224 | tf_op jit(solution)/shard_map/ppermute | solution.py:398

commit v3 on v2

--- a/solution.py
+++ b/solution.py
@@ -54,16 +54,24 @@
     b_ref[...] = pick(odd, shape, right, left)
 
 
-def row_pack(n_col, me_ref, own_ref, other_ref, a_in, b_in, info_ref, ext_ref, a_ref, b_ref, told_ref):
-    row, col, gz = place(me_ref, n_col)
+def edge_row(from_ref, s, gz):
+    rows, lanes = from_ref.shape[1:]
+    return pick(gz, (H, lanes), from_ref[s, rows - H : rows, :], from_ref[s, 0:H, :])
+
+
+def halo_rows(came_ref, handed_ref, s, gz):
+    came, handed = came_ref[s], handed_ref[s]
+    return pick(gz, came.shape, handed, came), pick(gz, came.shape, came, handed)
+
+
+def row_pack(n_col, me_ref, own_ref, other_ref, a_in, b_in, ext_ref, edge_ref):
+    _, col, gz = place(me_ref, n_col)
     shape = own_ref.shape[2:]
     rows, lanes = shape
     lane = iota(shape, 1)
     odd_col = lax.rem(col, 2)
     from_right = pick(odd_col, shape, b_in[...], a_in[...])
     from_left = pick(odd_col, shape, a_in[...], b_in[...])
-    odd = lax.rem(row, 2)
-    edge = (H, 2 * lanes)
     for s in range(12):
         cell = layer_of(own_ref, other_ref, s // 4, s % 4, gz, shape)
         low = pltpu.roll(from_right, lanes - 8 * s, 1) if s else from_right
@@ -71,12 +79,7 @@
         side = jnp.where(lane < 8, low, jnp.where(lane >= lanes - 8, high, 0.0))
         ext_ref[s, :, 0:lanes] = cell
         ext_ref[s, :, lanes : 2 * lanes] = side
-        top = ext_ref[s, 0:H, :]
-        bottom = ext_ref[s, rows - H : rows, :]
-        a_ref[s] = pick(odd, edge, top, bottom)
-        b_ref[s] = pick(odd, edge, bottom, top)
-    for k in range(told_ref.shape[0]):
-        told_ref[k] = info_ref[...]
+        edge_ref[s] = edge_row(ext_ref, s, gz)
 
 
 def sweep(now_ref, next_ref, force_ref, weight_ref):
@@ -112,29 +115,48 @@
     return jnp.concatenate([field_ref[m, 2 * gz + k, start : start + size, 0:128] for k in range(2)], 0)
 
 
-def prepare(me_ref, table_ref, source_ref, class_ref, owner_ref, pos_ref, node_ref, pack_ref, info_ref):
+def prepare(
+    table_hbm, source_hbm, class_hbm, owner_hbm, pos_hbm, node_hbm, pack_ref, told_ref,
+    table, level_ref, owner_ref, pos_ref, node_ref, sems,
+):
+    moves = [
+        (class_hbm, level_ref),
+        (table_hbm, table),
+        (owner_hbm, owner_ref),
+        (pos_hbm, pos_ref),
+        (node_hbm, node_ref),
+        (source_hbm, pack_ref.at[0:2]),
+    ]
+    copies = [pltpu.make_async_copy(a, b, sems.at[k]) for k, (a, b) in enumerate(moves)]
+    for copy in copies:
+        copy.start()
+    for copy in copies:
+        copy.wait()
     for k in range(2):
-        level = class_ref[k]
+        level = level_ref[k]
         found = jnp.zeros(level.shape, F32)
-        for n in range(table_ref.shape[0]):
-            found = jnp.where(level == n, table_ref[n], found)
+        for n in range(table.shape[0]):
+            found = jnp.where(level == n, table[n], found)
         pack_ref[2, k] = OMEGA / (6.0 + found)
-        for m in range(2):
-            pack_ref[m, k] = source_ref[m, k]
-    info_ref[...] = jnp.zeros_like(info_ref)
-    info_ref[2:5, :] = pos_ref[...]
-    info_ref[5:6, :] = owner_ref[...].astype(F32)
-    info_ref[6:7, :] = node_ref[...]
-
-
-def first_relax(n_col, me_ref, ext_ref, a_in, b_in, info_ref, full_ref, first_ref, sent_ref, force, spare):
-    row, _, gz = place(me_ref, n_col)
-    odd = lax.rem(row, 2)
-    edge = a_in.shape[1:]
+    told_ref[0] = jnp.zeros(told_ref.shape[1:], F32)
+    told_ref[0, 2:5, :] = pos_ref[...]
+    told_ref[0, 5:6, :] = owner_ref[...].astype(F32)
+    told_ref[0, 6:7, :] = node_ref[...]
+    for k in range(1, told_ref.shape[0]):
+        told_ref[k] = told_ref[0]
+
+
+def stage(own_ref, out_ref):
+    out_ref[...] = own_ref[...]
+
+
+def first_relax(n_col, me_ref, ext_ref, a_in, b_in, target_ref, full_ref, first_ref, sent_ref, force, spare):
+    _, col, gz = place(me_ref, n_col)
     for s in range(12):
-        full_ref[s // 4, s % 4, 0:H, :] = pick(odd, edge, a_in[s], b_in[s])
+        top, bottom = halo_rows(a_in, b_in, s, gz)
+        full_ref[s // 4, s % 4, 0:H, :] = top
         full_ref[s // 4, s % 4, H : H + 64, :] = ext_ref[s]
-        full_ref[s // 4, s % 4, H + 64 : 2 * H + 64, :] = pick(odd, edge, b_in[s], a_in[s])
+        full_ref[s // 4, s % 4, H + 64 : 2 * H + 64, :] = bottom
     weight = full_ref.at[2]
     for m in range(2):
         for z in range(4):
@@ -142,17 +164,17 @@
     sweep(force, first_ref, force, weight)
     sweep(first_ref, spare, force, weight)
     sweep(spare, first_ref, force, weight)
-    owner = info_ref[5:6, :].astype(jnp.int32)
-    line = iota(info_ref.shape, 0)
-    info = info_ref[...]
+    info = target_ref[2 * col + gz]
+    owner = info[5:6, :].astype(jnp.int32)
+    line = iota(info.shape, 0)
     for m in range(2):
         info = jnp.where(line == m, trace_of(two_layers(first_ref, m, gz, H, 64), owner, 0), info)
     for k in range(sent_ref.shape[0]):
         sent_ref[k] = info
 
 
-def carry_relax(n_col, me_ref, full_ref, first_ref, info_ref, keep_ref, trace_ref, force, spare, other):
-    _, _, gz = place(me_ref, n_col)
+def carry_relax(n_col, me_ref, full_ref, first_ref, target_ref, keep_ref, trace_ref, force, spare, other):
+    _, col, gz = place(me_ref, n_col)
     weight = full_ref.at[2]
     for m in range(2):
         for z in range(4):
@@ -161,7 +183,7 @@
     sweep(spare, other, force, weight)
     sweep(other, spare, force, weight)
     sweep(spare, other, force, weight)
-    owner = info_ref[5:6, :].astype(jnp.int32)
+    owner = target_ref[2 * col + gz, 5:6, :].astype(jnp.int32)
     for m in range(2):
         for k in range(2):
             keep_ref[m, k] = other[m, 2 * gz + k, H : H + 64, 0:128]
@@ -187,7 +209,7 @@
             out_ref[2 * c + 1, 8 * m : 8 * m + 8, :] = near
 
 
-def build_apply(n_col, n_row, me_ref, heard_ref, target_ref, pair_ref, out_ref, acc, lined):
+def build_apply(n_col, n_row, me_ref, heard_ref, target_ref, _, pair_ref, out_ref, acc, lined):
     step = pl.program_id(0)
     row, col, gz = place(me_ref, n_col)
     nodes = heard_ref.shape[2]
@@ -319,17 +341,11 @@
         sent_ref[k] = sent
 
 
-def last_spread(n_col, me_ref, part_ref, target_ref, before_ref, spread_ref, a_ref, b_ref, value_ref):
-    row, col, gz = place(me_ref, n_col)
+def last_spread(n_col, me_ref, part_ref, target_ref, before_ref, spread_ref, edge_ref, value_ref):
+    _, col, gz = place(me_ref, n_col)
     value = spread_nodes(n_col, col, part_ref, target_ref, spread_ref)
-    odd = lax.rem(row, 2)
-    edge = (H, 256)
     for s in range(16):
-        from_ref = before_ref if s < 8 else spread_ref
-        top = from_ref[s % 8, 0:H, :]
-        bottom = from_ref[s % 8, 64 - H : 64, :]
-        a_ref[s] = pick(odd, edge, top, bottom)
-        b_ref[s] = pick(odd, edge, bottom, top)
+        edge_ref[s] = edge_row(before_ref if s < 8 else spread_ref, s % 8, gz)
     for m in range(2):
         value_ref[m : m + 1, :] = pick(
             gz, (1, value.shape[1]), value[8 * m + 3 : 8 * m + 4, :], value[8 * m + 2 : 8 * m + 3, :]
@@ -339,16 +355,15 @@
 def last_relax(
     n_col, me_ref, full_ref, before_ref, spread_ref, a_in, b_in, keep_ref, out_ref, force, spare, other, later
 ):
-    row, _, gz = place(me_ref, n_col)
-    odd = lax.rem(row, 2)
+    _, _, gz = place(me_ref, n_col)
     weight = full_ref.at[2]
-    edge = (H, 256)
     for s in range(16):
         m, z = s % 8 // 4, s % 4
         into, own = (force, before_ref) if s < 8 else (later, spread_ref)
-        into[m, z, 0:H, :] = pick(odd, edge, a_in[s], b_in[s]) * weight[z, 0:H]
+        top, bottom = halo_rows(a_in, b_in, s, gz)
+        into[m, z, 0:H, :] = top * weight[z, 0:H]
         into[m, z, H : H + 64, :] = own[4 * m + z] * weight[z, H : H + 64]
-        into[m, z, H + 64 : 2 * H + 64, :] = pick(odd, edge, b_in[s], a_in[s]) * weight[z, H + 64 : 2 * H + 64]
+        into[m, z, H + 64 : 2 * H + 64, :] = bottom * weight[z, H + 64 : 2 * H + 64]
     sweep(force, spare, force, weight)
     sweep(spare, other, force, weight)
     sweep(other, spare, force, weight)
@@ -397,31 +412,46 @@
         second = second + [(j, i) for i, j in second]
         return lax.ppermute(a, axis, first), lax.ppermute(b, axis, second)
 
-    packed, info = run(
+    def beside(edge):
+        came = [(2 * i + 1, 2 * i + 2) for i in range(n_row - 1)]
+        came = lax.ppermute(edge, ("row", "gz"), came + [(j, i) for i, j in came])
+        return came, lax.ppermute(came, "gz", [(0, 1), (1, 0)])
+
+    packed, told = pl.pallas_call(
         prepare,
-        "prepare",
-        [(3, 2, 64, 128), (8, nodes)],
-        [me, coeff_table, source, cell_class, owner_cell[None, :], node_pos, node_weight[None, :]],
-        scalars=2,
-    )
+        name="prepare",
+        out_shape=[jax.ShapeDtypeStruct(o, F32) for o in ((3, 2, 64, 128), (blocks, 8, nodes))],
+        in_specs=[pl.BlockSpec(memory_space=pl.ANY)] * 6,
+        out_specs=[VMEM] * 2,
+        scratch_shapes=[
+            pltpu.SMEM(coeff_table.shape, F32),
+            pltpu.VMEM(cell_class.shape, jnp.int32),
+            pltpu.VMEM((1, nodes), jnp.int32),
+            pltpu.VMEM((3, nodes), F32),
+            pltpu.VMEM((1, nodes), F32),
+            pltpu.SemaphoreType.DMA((6,)),
+        ],
+        compiler_params=pltpu.CompilerParams(vmem_limit_bytes=60 << 20),
+    )(coeff_table, source, cell_class, owner_cell[None, :], node_pos, node_weight[None, :])
     other = lax.ppermute(packed, "gz", [(0, 1), (1, 0)])
+    target = lax.all_to_all(told, ("col", "gz"), 0, 0)
+    (packed,) = run(stage, "stage", [packed.shape], [packed], scalars=0)
     a, b = run(functools.partial(col_pack, n_col), "col_pack", [(64, 128)] * 2, [me, packed, other])
     a, b = swaps("col", n_col, a, b)
-    ext, a, b, told = run(
+    ext, edge = run(
         functools.partial(row_pack, n_col),
         "row_pack",
-        [(12, 64, 256), (12, H, 256), (12, H, 256), (blocks, 8, nodes)],
-        [me, packed, other, a, b, info],
-    )
-    a, b = swaps("row", n_row, a, b)
-    target = lax.all_to_all(told, ("col", "gz"), 0, 0)
+        [(12, 64, 256), (12, H, 256)],
+        [me, packed, other, a, b],
+    )
+    a, b = beside(edge)
 
     field = (2, 4, 64 + 2 * H, 256)
     full, first, sent = run(
         functools.partial(first_relax, n_col),
         "first_relax",
         [(3, 4, 64 + 2 * H, 256), field, (n_row, 8, nodes)],
-        [me, ext, a, b, info],
+        [me, ext, a, b, target],
         [field] * 2,
     )
     heard = lax.all_to_all(sent, "row", 0, 0)
@@ -429,7 +459,7 @@
         functools.partial(carry_relax, n_col),
         "carry_relax",
         [(2, 2, 64, 128), (2, nodes)],
-        [me, full, first, info],
+        [me, full, first, target],
         [field] * 3,
         flops=40 * size_of(field),
     )
@@ -445,7 +475,7 @@
             jax.ShapeDtypeStruct((n_row, nodes, blocks * nodes), F32),
             jax.ShapeDtypeStruct((blocks, 16, nodes), F32),
         ],
-        in_specs=[SMEM, everything((n_row, 8, nodes)), everything((blocks, 8, nodes))],
+        in_specs=[SMEM, everything((n_row, 8, nodes)), everything((blocks, 8, nodes)), everything((2, nodes))],
         out_specs=[
             pl.BlockSpec((1, nodes, blocks * nodes), lambda i: (i, 0, 0)),
             everything((blocks, 16, nodes)),
@@ -453,7 +483,7 @@
         scratch_shapes=sums,
         compiler_params=pltpu.CompilerParams(vmem_limit_bytes=16 << 20),
         cost_estimate=pl.CostEstimate(flops=18 * work, bytes_accessed=4 * work, transcendentals=work),
-    )(me, heard, target)
+    )(me, heard, target, kept)
     partial = lax.all_to_all(partial, ("col", "gz"), 0, 0)
     before, sent = run(
         functools.partial(respond, n_col, n_row),
@@ -481,13 +511,13 @@
         cost_estimate=pl.CostEstimate(flops=4 * work, bytes_accessed=4 * work, transcendentals=0),
     )(me, again, heard, pairs)
     partial = lax.all_to_all(partial, ("col", "gz"), 0, 0)
-    spread, a, b, values = run(
+    spread, edge, values = run(
         functools.partial(last_spread, n_col),
         "last_spread",
-        [(8, 64, 256), (16, H, 256), (16, H, 256), (2, nodes)],
+        [(8, 64, 256), (16, H, 256), (2, nodes)],
         [me, partial, target, before],
     )
-    a, b = swaps("row", n_row, a, b)
+    a, b = beside(edge)
     (potential,) = run(
         functools.partial(last_relax, n_col),
         "last_relax",

time: 143 us -> 125 us (0.87)
  local copies, waits for them, and re-layouts: 15.9 us -> 0.96 us
  blocking collectives: 38.5 us -> 32.5 us
  waiting for transfers between devices: 24.1 us -> 26.6 us
    all_to_all x1 -> x0, blocking collectives: 16.5 us -> none  [on_device(): heard = lax.all_to_all(sent, 'row', 0, 0)]
    unnamed x16 -> x2, local copies, waits for them, and re-layouts: 15.9 us -> 0.96 us
    ppermute x6 -> x2, waiting for transfers between devices: 15.2 us -> 0.53 us  [swaps(): return (lax.ppermute(a, axis, first), lax.ppermute(b, axis, second))]
    ppermute x6 -> x2, starting transfers between devices: 13.8 us -> 0.76 us  [swaps(): return (lax.ppermute(a, axis, first), lax.ppermute(b, axis, second))]
    ppermute x0 -> x4, starting transfers between devices: none -> 12.5 us  [the longest x2 10.5 us: beside(): came = lax.ppermute(edge, ('row', 'gz'), came + [(j, i) for i, j in came])]
    ppermute x0 -> x4, waiting for transfers between devices: none -> 11.4 us  [the longest x2 6.45 us: beside(): came = lax.ppermute(edge, ('row', 'gz'), came + [(j, i) for i, j in came])]
    all_to_all x1 -> x2, blocking collectives: 9.18 us -> 19.7 us  [on_device(): partial = lax.all_to_all(partial, ('col', 'gz'), 0, 0)]
    all_to_all x1, waiting for transfers between devices: 0.01 us -> 4.41 us  [on_device(): target = lax.all_to_all(told, ('col', 'gz'), 0, 0)]
  transfers between devices with their start and end apart: 9 -> 9, of which waited for: 6 -> 6; matrix products, arithmetic and copies ran while one was open for 0% -> 0% of each run, Pallas kernels for 3% -> 2%
where the time goes in v3:
time: 125 us; the launch traced here: 124 us
  Pallas kernels  32.5 us (26%)
  blocking collectives  32.5 us (26%)
  starting transfers between devices  31 us (25%)
  waiting for transfers between devices  26.6 us (21%)
    all_to_all x2, blocking collectives, on_device(): partial = lax.all_to_all(partial, ('col', 'gz'), 0, 0)  19.7 us
    pallas_call x8, Pallas kernels, run(): pl.pallas_call(body, name=name, out_shape=[jax.ShapeDtypeStruct(o, F32) f...  16.3 us
    all_to_all x1, blocking collectives, on_device(): again = lax.all_to_all(sent, 'row', 0, 0)  12.8 us
    pallas_call x1, Pallas kernels, on_device(): pl.pallas_call(functools.partial(build_apply, n_col, n_row), name='build_...  11.1 us
    ppermute x2, starting transfers between devices, beside(): came = lax.ppermute(edge, ('row', 'gz'), came + [(j, i) for i, j in came])  10.5 us
    all_to_all x1, starting transfers between devices, on_device(): target = lax.all_to_all(told, ('col', 'gz'), 0, 0)  8.45 us
    all_to_all x1, starting transfers between devices, on_device(): heard = lax.all_to_all(sent, 'row', 0, 0)  7.29 us
    ppermute x2, waiting for transfers between devices, beside(): came = lax.ppermute(edge, ('row', 'gz'), came + [(j, i) for i, j in came])  6.45 us
  transfers between devices with their start and end apart: 9, of which 6 were waited for; matrix products, arithmetic and copies ran while one was open for 0% of the time, Pallas kernels for 2%

profile of v3, /device:TPU:8, one launch (start us, length us, event | category | flops | bytes accessed | tf_op | source)
XLA Modules:
  0.0 124.4 jit_solution(1620968362881383990)
XLA Ops:
  0.6 1.8 %prepare.1 = (f32[3,2,64,128]{3,2,1,0:T(8,128)}, f32[16,8,128]{2,1,0:T(8,128)}) custom-call(f32[8]{0:T(128)} %table_hbm.1, f32[2,2,64,128]{3,2,1,0:T(8,128)} %source_hbm.1, s32[2,64,128]{2,1,0:T(8,128)} %class_hbm.1, s32[1,128]{1,0:T(1,128)} %bitcast.3, f32[3,128]{1,0:T(4,128)} %pos_hbm.1, f32[1,128]{1,0:T(1,128)} %bitcast.4), custom_call_target="tpu_custom_call" | custom-call | tf_op jit(solution)/shard_map/prepare/pallas_call | solution.py:420
  2.4 2.0 %collective-permute-start = (f32[3,2,64,128]{3,2,1,0:T(8,128)}, f32[3,2,64,128]{3,2,1,0:T(8,128)S(1)}, u32[]{:S(2)}, u32[]{:S(2)}) collective-permute-start(f32[3,2,64,128]{3,2,1,0:T(8,128)} %get-tuple-element.20.own_ref), channel_id=1, source_target_pairs={{0,1},{1,0},{2,3},{3,2},{4,5},{5,4},{6,7},{7,6},{8,9},{9,8},{10,11... | collective-permute-start | bytes 589832 | tf_op jit(solution)/shard_map/ppermute | solution.py:436
  4.4 1.0 copy-done
  5.4 4.1 %collective-permute-done.other_ref = f32[3,2,64,128]{3,2,1,0:T(8,128)S(1)} collective-permute-done((f32[3,2,64,128]{3,2,1,0:T(8,128)}, f32[3,2,64,128]{3,2,1,0:T(8,128)S(1)}, u32[]{:S(2)}, u32[]{:S(2)}) %collective-permute-start) | collective-permute-done | bytes 196640 | tf_op jit(solution)/shard_map/ppermute | solution.py:436
  9.5 0.3 col_pack.1
  9.8 0.1 collective-permute-start.1
  9.9 0.7 collective-permute-start.2
  10.6 0.5 collective-permute-done.1.a_in
  11.1 0.0 collective-permute-done.2.b_in
  11.1 0.3 row_pack.1
  11.4 7.5 %collective-permute-start.3 = (f32[12,8,256]{2,1,0:T(8,128)S(1)}, f32[12,8,256]{2,1,0:T(8,128)S(1)}, u32[]{:S(2)}, u32[]{:S(2)}) collective-permute-start(f32[12,8,256]{2,1,0:T(8,128)S(1)} %get-tuple-element.24), channel_id=1, source_target_pairs={{1,16},{17,32},{33,48},{49,64},{65,80},{81,96},{97,112},{113,128},... | collective-permute-start | bytes 294920 | tf_op jit(solution)/shard_map/ppermute | solution.py:417
  18.9 8.5 %all-to-all-start = ((f32[16,8,128]{2,1,0:T(8,128)}), f32[16,8,128]{2,1,0:T(8,128)S(1)}, u32[]{:S(2)}, u32[]{:S(2)}) async-start(f32[16,8,128]{2,1,0:T(8,128)} %get-tuple-element.25), calls=%async_computation | async-start | bytes 131072 | tf_op jit(solution)/shard_map/all_to_all | solution.py:437
  27.3 0.0 collective-permute-done.3.a_in
  27.3 2.0 %collective-permute-start.4 = (f32[12,8,256]{2,1,0:T(8,128)S(1)}, f32[12,8,256]{2,1,0:T(8,128)S(1)}, u32[]{:S(2)}, u32[]{:S(2)}) collective-permute-start(f32[12,8,256]{2,1,0:T(8,128)S(1)} %collective-permute-done.3.a_in), channel_id=1, source_target_pairs={{0,1},{1,0},{2,3},{3,2},{4,5},{5,4},{6,7},{7,6},{8,9},{9,8},{10,11... | collective-permute-start | bytes 294920 | tf_op jit(solution)/shard_map/ppermute | solution.py:418
  29.4 4.4 %all-to-all-done.target_ref = f32[16,8,128]{2,1,0:T(8,128)S(1)} async-done(((f32[16,8,128]{2,1,0:T(8,128)}), f32[16,8,128]{2,1,0:T(8,128)S(1)}, u32[]{:S(2)}, u32[]{:S(2)}) %all-to-all-start) | async-done | bytes 65568 | tf_op jit(solution)/shard_map/all_to_all | solution.py:437
  33.8 0.0 collective-permute-done.4.b_in
  33.8 2.6 %first_relax.1 = (f32[3,4,80,256]{3,2,1,0:T(8,128)S(1)}, f32[2,4,80,256]{3,2,1,0:T(8,128)S(1)}, f32[16,8,128]{2,1,0:T(8,128)}) custom-call(s32[1]{0:T(128)} %bitcast.me_ref, f32[12,64,256]{2,1,0:T(8,128)S(1)} %get-tuple-element.23.ext_ref, f32[12,8,256]{2,1,0:T(8,128)S(1)} %collective-permute-done.3.a_in, f32[12,8,256]{2,1,0:T(8,128)S(1)} %collective-permute-done.4.b_in, ...), custom_call_target="tpu_custom_call" | custom-call | bytes 2752516 | tf_op jit(solution)/shard_map/first_relax/pallas_call | solution.py:392
  36.4 7.3 %all-to-all-start.1 = ((f32[16,8,128]{2,1,0:T(8,128)}), f32[16,8,128]{2,1,0:T(8,128)S(1)}, u32[]{:S(2)}, u32[]{:S(2)}) async-start(f32[16,8,128]{2,1,0:T(8,128)} %get-tuple-element.27), calls=%async_computation.1 | async-start | bytes 131072 | tf_op jit(solution)/shard_map/all_to_all | solution.py:457
  43.7 2.5 %carry_relax.1 = (f32[2,2,64,128]{3,2,1,0:T(8,128)S(1)}, f32[2,128]{1,0:T(2,128)S(1)}) custom-call(s32[1]{0:T(128)} %bitcast.me_ref, f32[3,4,80,256]{3,2,1,0:T(8,128)S(1)} %get-tuple-element.26.full_ref, f32[2,4,80,256]{3,2,1,0:T(8,128)S(1)} %get-tuple-element.28.first_ref, f32[16,8,128]{2,1,0:T(8,128)S(1)} %all-to-all-done.target_ref), custom_call_target="tpu_custom_call" | custom-call | flops 6553600 | bytes 1836036 | tf_op jit(solution)/shard_map/carry_relax/pallas_call | solution.py:392
  46.2 6.2 %all-to-all-done.1.heard_ref.info_ref = f32[16,8,128]{2,1,0:T(8,128)S(1)} async-done(((f32[16,8,128]{2,1,0:T(8,128)}), f32[16,8,128]{2,1,0:T(8,128)S(1)}, u32[]{:S(2)}, u32[]{:S(2)}) %all-to-all-start.1) | async-done | bytes 65568 | tf_op jit(solution)/shard_map/all_to_all | solution.py:457
  52.4 11.1 %build_apply.1 = (f32[16,128,2048]{2,1,0:T(8,128)S(1)}, f32[16,16,128]{2,1,0:T(8,128)S(1)}) custom-call(s32[1]{0:T(128)} %bitcast.me_ref, f32[16,8,128]{2,1,0:T(8,128)S(1)} %all-to-all-done.1.heard_ref.info_ref, f32[16,8,128]{2,1,0:T(8,128)S(1)} %all-to-all-done.target_ref, f32[2,128]{1,0:T(2,128)S(1)} %get-tuple-element.29._.kept_ref), custom_call_target="tpu_custom_call" | custom-call | flops 75497472 | bytes 16777216 | tf_op jit(solution)/shard_map/build_apply/pallas_call | solution.py:470
  63.4 10.6 %all_to_all.25.part_ref = f32[16,16,128]{2,1,0:T(8,128)S(1)} all-to-all(f32[16,16,128]{2,1,0:T(8,128)S(1)} %get-tuple-element.30), channel_id=1, replica_groups=mesh['row'=16,'col'=8,'gz'=2] {'col','gz'}, dimensions={0} | all-to-all | bytes 262144 | tf_op jit(solution)/shard_map/all_to_all | solution.py:487
  74.0 4.9 %respond.1 = (f32[8,64,256]{2,1,0:T(8,128)S(1)}, f32[16,8,128]{2,1,0:T(8,128)S(1)}) custom-call(s32[1]{0:T(128)} %bitcast.me_ref, f32[16,16,128]{2,1,0:T(8,128)S(1)} %all_to_all.25.part_ref, f32[16,8,128]{2,1,0:T(8,128)S(1)} %all-to-all-done.target_ref, f32[3,4,80,256]{3,2,1,0:T(8,128)S(1)} %get-tuple-element.26.full_ref, ...), custom_call_target="tpu_custom_call" | custom-call | bytes 1836036 | tf_op jit(solution)/shard_map/respond/pallas_call | solution.py:392
  78.8 12.8 %all_to_all.26.heard_ref = f32[16,8,128]{2,1,0:T(8,128)S(1)} all-to-all(f32[16,8,128]{2,1,0:T(8,128)S(1)} %get-tuple-element.32), channel_id=1, replica_groups=mesh['row'=16,'col'=8,'gz'=2] {'row'}, dimensions={0} | all-to-all | bytes 131072 | tf_op jit(solution)/shard_map/all_to_all | solution.py:495
  91.6 3.4 %reapply.1 = f32[16,16,128]{2,1,0:T(8,128)S(1)} custom-call(s32[1]{0:T(128)} %bitcast.me_ref, f32[16,8,128]{2,1,0:T(8,128)S(1)} %all_to_all.26.heard_ref, f32[16,8,128]{2,1,0:T(8,128)S(1)} %all-to-all-done.1.heard_ref.info_ref, f32[16,128,2048]{2,1,0:T(8,128)S(1)} %get-tuple-element.33.pair_ref), custom_call_target="tpu_custom_call" | custom-call | flops 16777216 | bytes 16777216 | tf_op jit(solution)/shard_map/reapply/pallas_call | solution.py:497
  95.0 9.2 %all_to_all.27.part_ref = f32[16,16,128]{2,1,0:T(8,128)S(1)} all-to-all(f32[16,16,128]{2,1,0:T(8,128)S(1)} %reapply.1), channel_id=1, replica_groups=mesh['row'=16,'col'=8,'gz'=2] {'col','gz'}, dimensions={0} | all-to-all | bytes 262144 | tf_op jit(solution)/shard_map/all_to_all | solution.py:513
  104.2 1.3 %last_spread.1 = (f32[8,64,256]{2,1,0:T(8,128)S(1)}, f32[16,8,256]{2,1,0:T(8,128)S(1)}, f32[2,128]{1,0:T(2,128)}) custom-call(s32[1]{0:T(128)} %bitcast.me_ref, f32[16,16,128]{2,1,0:T(8,128)S(1)} %all_to_all.27.part_ref, f32[16,8,128]{2,1,0:T(8,128)S(1)} %all-to-all-done.target_ref, f32[8,64,256]{2,1,0:T(8,128)S(1)} %get-tuple-element.31.before_ref), custom_call_target="tpu_custom_call" | custom-call | bytes 1377284 | tf_op jit(solution)/shard_map/last_spread/pallas_call | solution.py:392
  105.4 3.1 %collective-permute-start.5 = (f32[16,8,256]{2,1,0:T(8,128)S(1)}, f32[16,8,256]{2,1,0:T(8,128)S(1)}, u32[]{:S(2)}, u32[]{:S(2)}) collective-permute-start(f32[16,8,256]{2,1,0:T(8,128)S(1)} %get-tuple-element.35), channel_id=1, source_target_pairs={{1,16},{17,32},{33,48},{49,64},{65,80},{81,96},{97,112},{113,128},... | collective-permute-start | bytes 393224 | tf_op jit(solution)/shard_map/ppermute | solution.py:417
  108.5 6.4 %collective-permute-done.5.a_in = f32[16,8,256]{2,1,0:T(8,128)S(1)} collective-permute-done((f32[16,8,256]{2,1,0:T(8,128)S(1)}, f32[16,8,256]{2,1,0:T(8,128)S(1)}, u32[]{:S(2)}, u32[]{:S(2)}) %collective-permute-start.5) | collective-permute-done | bytes 131104 | tf_op jit(solution)/shard_map/ppermute | solution.py:417
  114.9 0.0 collective-permute-start.6
  114.9 5.0 %collective-permute-done.6.b_in = f32[16,8,256]{2,1,0:T(8,128)S(1)} collective-permute-done((f32[16,8,256]{2,1,0:T(8,128)S(1)}, f32[16,8,256]{2,1,0:T(8,128)S(1)}, u32[]{:S(2)}, u32[]{:S(2)}) %collective-permute-start.6) | collective-permute-done | bytes 131104 | tf_op jit(solution)/shard_map/ppermute | solution.py:418
  119.9 4.5 %last_relax.1 = f32[2,2,64,128]{3,2,1,0:T(8,128)} custom-call(s32[1]{0:T(128)} %bitcast.me_ref, f32[3,4,80,256]{3,2,1,0:T(8,128)S(1)} %get-tuple-element.26.full_ref, f32[8,64,256]{2,1,0:T(8,128)S(1)} %get-tuple-element.31.before_ref, f32[8,64,256]{2,1,0:T(8,128)S(1)} %get-tuple-element.34.spread_ref, f32[16,8,256]{2,1,0:T(8,128)S(1)} %collective-permute-done.5.a_in, ...), custom_call_target="tpu_custom_call" | custom-call | bytes 2555908 | tf_op jit(solution)/shard_map/last_relax/pallas_call | solution.py:392
  (2 shorter events, 0.0 us)
Async XLA Ops:
  2.4 7.1 %collective-permute-start = (f32[3,2,64,128]{3,2,1,0:T(8,128)}, f32[3,2,64,128]{3,2,1,0:T(8,128)S(1)}, u32[]{:S(2)}, u32[]{:S(2)}) collective-permute-start(f32[3,2,64,128]{3,2,1,0:T(8,128)} %get-tuple-element.20.own_ref), channel_id=1, source_target_pairs={{0,1},{1,0},{2,3},{3,2},{4,5},{5,4},{6,7},{7,6},{8,9},{9,8},{10,11... | collective-permute-start | bytes 589832 | tf_op jit(solution)/shard_map/ppermute | solution.py:436
  4.4 1.0 copy-start
  9.8 1.3 %collective-permute-start.1 = (f32[64,128]{1,0:T(8,128)S(1)}, f32[64,128]{1,0:T(8,128)S(1)}, u32[]{:S(2)}, u32[]{:S(2)}) collective-permute-start(f32[64,128]{1,0:T(8,128)S(1)} %get-tuple-element.21), channel_id=1, source_target_pairs={{0,2},{2,0},{4,6},{6,4},{8,10},{10,8},{12,14},{14,12},{1,3},{3,1},... | collective-permute-start | bytes 98312 | tf_op jit(solution)/shard_map/ppermute | solution.py:413
  9.9 1.2 collective-permute-start.2
  11.4 15.9 %collective-permute-start.3 = (f32[12,8,256]{2,1,0:T(8,128)S(1)}, f32[12,8,256]{2,1,0:T(8,128)S(1)}, u32[]{:S(2)}, u32[]{:S(2)}) collective-permute-start(f32[12,8,256]{2,1,0:T(8,128)S(1)} %get-tuple-element.24), channel_id=1, source_target_pairs={{1,16},{17,32},{33,48},{49,64},{65,80},{81,96},{97,112},{113,128},... | collective-permute-start | bytes 294920 | tf_op jit(solution)/shard_map/ppermute | solution.py:417
  18.9 14.9 %all-to-all-start = ((f32[16,8,128]{2,1,0:T(8,128)}), f32[16,8,128]{2,1,0:T(8,128)S(1)}, u32[]{:S(2)}, u32[]{:S(2)}) async-start(f32[16,8,128]{2,1,0:T(8,128)} %get-tuple-element.25), calls=%async_computation | async-start | bytes 131072 | tf_op jit(solution)/shard_map/all_to_all | solution.py:437
  27.3 6.4 %collective-permute-start.4 = (f32[12,8,256]{2,1,0:T(8,128)S(1)}, f32[12,8,256]{2,1,0:T(8,128)S(1)}, u32[]{:S(2)}, u32[]{:S(2)}) collective-permute-start(f32[12,8,256]{2,1,0:T(8,128)S(1)} %collective-permute-done.3.a_in), channel_id=1, source_target_pairs={{0,1},{1,0},{2,3},{3,2},{4,5},{5,4},{6,7},{7,6},{8,9},{9,8},{10,11... | collective-permute-start | bytes 294920 | tf_op jit(solution)/shard_map/ppermute | solution.py:418
  36.4 16.0 %all-to-all-start.1 = ((f32[16,8,128]{2,1,0:T(8,128)}), f32[16,8,128]{2,1,0:T(8,128)S(1)}, u32[]{:S(2)}, u32[]{:S(2)}) async-start(f32[16,8,128]{2,1,0:T(8,128)} %get-tuple-element.27), calls=%async_computation.1 | async-start | bytes 131072 | tf_op jit(solution)/shard_map/all_to_all | solution.py:457
  105.4 9.5 %collective-permute-start.5 = (f32[16,8,256]{2,1,0:T(8,128)S(1)}, f32[16,8,256]{2,1,0:T(8,128)S(1)}, u32[]{:S(2)}, u32[]{:S(2)}) collective-permute-start(f32[16,8,256]{2,1,0:T(8,128)S(1)} %get-tuple-element.35), channel_id=1, source_target_pairs={{1,16},{17,32},{33,48},{49,64},{65,80},{81,96},{97,112},{113,128},... | collective-permute-start | bytes 393224 | tf_op jit(solution)/shard_map/ppermute | solution.py:417
  114.9 5.0 %collective-permute-start.6 = (f32[16,8,256]{2,1,0:T(8,128)S(1)}, f32[16,8,256]{2,1,0:T(8,128)S(1)}, u32[]{:S(2)}, u32[]{:S(2)}) collective-permute-start(f32[16,8,256]{2,1,0:T(8,128)S(1)} %collective-permute-done.5.a_in), channel_id=1, source_target_pairs={{0,1},{1,0},{2,3},{3,2},{4,5},{5,4},{6,7},{7,6},{8,9},{9,8},{10,11... | collective-permute-start | bytes 393224 | tf_op jit(solution)/shard_map/ppermute | solution.py:418

commit v4 on v3

--- a/solution.py
+++ b/solution.py
@@ -59,8 +59,38 @@
     return pick(gz, (H, lanes), from_ref[s, rows - H : rows, :], from_ref[s, 0:H, :])
 
 
-def halo_rows(came_ref, handed_ref, s, gz):
-    came, handed = came_ref[s], handed_ref[s]
+def tuck(side, s, into):
+    lane = iota(side.shape, 1)
+    moved = pltpu.roll(side, (16 * s + 8) % 128, 1)
+    return jnp.where((lane >= 16 * s) & (lane < 16 * s + 16), moved, into)
+
+
+def untuck(tile, s):
+    lane = iota(tile.shape, 1)
+    moved = pltpu.roll(tile, (128 - 16 * s - 8) % 128, 1)
+    return jnp.where((lane < 8) | (lane >= 120), moved, 0.0)
+
+
+def write_edges(edge_ref, start, from_ref, count, gz):
+    for first in range(0, count, 8):
+        side = jnp.zeros((H, 128), F32)
+        for s in range(first, min(first + 8, count)):
+            edge = edge_row(from_ref, s, gz)
+            edge_ref[start + s] = edge[:, 0:128]
+            side = tuck(edge[:, 128:256], s - first, side)
+        edge_ref[start + count + first // 8] = side
+
+
+def read_edge(ref, start, s, count):
+    return jnp.concatenate([ref[start + s], untuck(ref[start + count + s // 8], s % 8)], 1)
+
+
+def near_half(sent_gz):
+    line = iota((H, 128), 0)
+    return (line // 4) == jnp.full((H, 128), sent_gz, jnp.int32)
+
+
+def halo_rows(came, handed, gz):
     return pick(gz, came.shape, handed, came), pick(gz, came.shape, came, handed)
 
 
@@ -79,7 +109,7 @@
         side = jnp.where(lane < 8, low, jnp.where(lane >= lanes - 8, high, 0.0))
         ext_ref[s, :, 0:lanes] = cell
         ext_ref[s, :, lanes : 2 * lanes] = side
-        edge_ref[s] = edge_row(ext_ref, s, gz)
+    write_edges(edge_ref, 0, ext_ref, 12, gz)
 
 
 def sweep(now_ref, next_ref, force_ref, weight_ref):
@@ -139,9 +169,11 @@
             found = jnp.where(level == n, table[n], found)
         pack_ref[2, k] = OMEGA / (6.0 + found)
     told_ref[0] = jnp.zeros(told_ref.shape[1:], F32)
-    told_ref[0, 2:5, :] = pos_ref[...]
+    centred = pos_ref[...] - 0.5
+    told_ref[0, 2:5, :] = centred
     told_ref[0, 5:6, :] = owner_ref[...].astype(F32)
     told_ref[0, 6:7, :] = node_ref[...]
+    told_ref[0, 7:8, :] = jnp.sum(centred * centred, axis=0, keepdims=True)
     for k in range(1, told_ref.shape[0]):
         told_ref[k] = told_ref[0]
 
@@ -153,7 +185,7 @@
 def first_relax(n_col, me_ref, ext_ref, a_in, b_in, target_ref, full_ref, first_ref, sent_ref, force, spare):
     _, col, gz = place(me_ref, n_col)
     for s in range(12):
-        top, bottom = halo_rows(a_in, b_in, s, gz)
+        top, bottom = halo_rows(read_edge(a_in, 0, s, 12), read_edge(b_in, 0, s, 12), gz)
         full_ref[s // 4, s % 4, 0:H, :] = top
         full_ref[s // 4, s % 4, H : H + 64, :] = ext_ref[s]
         full_ref[s // 4, s % 4, H + 64 : 2 * H + 64, :] = bottom
@@ -209,27 +241,52 @@
             out_ref[2 * c + 1, 8 * m : 8 * m + 8, :] = near
 
 
-def build_apply(n_col, n_row, me_ref, heard_ref, target_ref, _, pair_ref, out_ref, acc, lined):
+def split(x):
+    high = x.astype(jnp.bfloat16).astype(F32)
+    rest = x - high
+    middle = rest.astype(jnp.bfloat16).astype(F32)
+    return high, middle, rest - middle
+
+
+def build_apply(n_col, n_row, me_ref, heard_ref, target_ref, _, pair_ref, out_ref, acc, lined, goal):
     step = pl.program_id(0)
     row, col, gz = place(me_ref, n_col)
     nodes = heard_ref.shape[2]
+    blocks = target_ref.shape[0]
+    line = iota((8, nodes), 0)
+    at_pos = (line >= 2) & (line <= 4)
 
     @pl.when(step == 0)
     def _():
         acc[...] = jnp.zeros_like(acc)
+        for t in range(blocks):
+            info = target_ref[t]
+            norm = pltpu.roll(info, 1, 0) + SOFTEN
+            base = jnp.where(line == 0, norm, jnp.where(at_pos, -2.0 * info, jnp.where(line == 7, 1.0, 0.0)))
+            high, middle, low = split(base)
+            rows = jnp.concatenate([high, middle, high, low, high, middle], 0)
+            goal[:, t * nodes : (t + 1) * nodes] = rows.astype(jnp.bfloat16)
 
     heard = heard_ref[step]
-    at = columns(heard[2:5, :], 3)
+    base = jnp.where(at_pos | (line == 7), heard, jnp.where(line == 0, 1.0, 0.0))
+    high, middle, low = split(base)
+    start = jnp.concatenate([high, high, middle, high, low, middle], 0).astype(jnp.bfloat16)
+    z_at = columns(heard[4:5, :], 1)[0]
     by = columns(heard[0:2, :] * heard[6:7, :], 2)
-    for t in range(target_ref.shape[0]):
-        dx = target_ref[t, 2:3, :] - at[0]
-        dy = target_ref[t, 3:4, :] - at[1]
-        dz = target_ref[t, 4:5, :] - at[2]
-        inverse = lax.rsqrt(dx * dx + dy * dy + (dz * dz + SOFTEN))
-        pair = dz * inverse * (inverse * inverse)
-        pair_ref[0, :, t * nodes : (t + 1) * nodes] = pair
-        for m in range(2):
-            acc[m, t] = acc[m, t] + jnp.sum((pair * by[m]).reshape(nodes // 8, 8, nodes), axis=0)
+    for t in range(0, blocks, 2):
+        squares = lax.dot_general(
+            start,
+            goal[:, t * nodes : (t + 2) * nodes],
+            (((0,), (0,)), ((), ())),
+            preferred_element_type=F32,
+        )
+        for k in range(2):
+            dz = target_ref[t + k, 4:5, :] - z_at
+            inverse = lax.rsqrt(squares[:, k * nodes : (k + 1) * nodes])
+            pair = dz * inverse * (inverse * inverse)
+            pair_ref[0, :, (t + k) * nodes : (t + k + 1) * nodes] = pair
+            for m in range(2):
+                acc[m, t + k] = acc[m, t + k] + jnp.sum((pair * by[m]).reshape(nodes // 8, 8, nodes), axis=0)
 
     @pl.when(step == n_row - 1)
     def _():
@@ -307,7 +364,7 @@
 
 def respond(
     n_col, n_row, me_ref, part_ref, target_ref, full_ref, heard_ref, kept_ref,
-    spread_ref, sent_ref, force, spare, other,
+    spread_ref, sent_ref, second_ref, force, spare, other,
 ):
     row, col, gz = place(me_ref, n_col)
     weight = full_ref.at[2]
@@ -320,10 +377,10 @@
             force[m, z, H + 64 : 2 * H + 64, :] = empty
     sweep(force, spare, force, weight)
     sweep(spare, other, force, weight)
-    sweep(other, spare, force, weight)
+    sweep(other, second_ref, force, weight)
     for m in range(2):
         for z in range(4):
-            force[m, z] = (-RELAX * spare[m, z]) * weight[z]
+            force[m, z] = (-RELAX * second_ref[m, z]) * weight[z]
     sweep(force, other, force, weight)
     sweep(other, spare, force, weight)
     sweep(spare, other, force, weight)
@@ -344,26 +401,61 @@
 def last_spread(n_col, me_ref, part_ref, target_ref, before_ref, spread_ref, edge_ref, value_ref):
     _, col, gz = place(me_ref, n_col)
     value = spread_nodes(n_col, col, part_ref, target_ref, spread_ref)
-    for s in range(16):
-        edge_ref[s] = edge_row(before_ref if s < 8 else spread_ref, s % 8, gz)
+    write_edges(edge_ref, 0, before_ref, 8, gz)
+    near = near_half(gz)
+    side = jnp.zeros((H, 128), F32)
+    for s in range(0, 8, 2):
+        one, two = edge_row(spread_ref, s, gz), edge_row(spread_ref, s + 1, gz)
+        edge_ref[9 + s // 2] = jnp.where(near, one[:, 0:128], pltpu.roll(two[:, 0:128], 4, 0))
+        side = tuck(one[:, 128:256], s, side)
+        side = tuck(two[:, 128:256], s + 1, side)
+    edge_ref[13] = side
     for m in range(2):
         value_ref[m : m + 1, :] = pick(
             gz, (1, value.shape[1]), value[8 * m + 3 : 8 * m + 4, :], value[8 * m + 2 : 8 * m + 3, :]
         )
 
 
+def own_relax(n_col, me_ref, full_ref, second_ref, spread_ref, keep_ref, out_ref, force, spare, other):
+    _, _, gz = place(me_ref, n_col)
+    weight = full_ref.at[2]
+    for m in range(2):
+        for z in range(4):
+            force[m, z] = (-RELAX * second_ref[m, z]) * weight[z]
+            mid = force[m, z, H : H + 64, :]
+            force[m, z, H : H + 64, :] = mid + spread_ref[4 * m + z] * weight[z, H : H + 64]
+    sweep(second_ref, spare, force, weight)
+    sweep(spare, other, force, weight)
+    sweep(other, spare, force, weight)
+    sweep(spare, other, force, weight)
+    for m in range(2):
+        for k in range(2):
+            out_ref[m, k] = keep_ref[m, k] + other[m, 2 * gz + k, H : H + 64, 0:128]
+
+
 def last_relax(
-    n_col, me_ref, full_ref, before_ref, spread_ref, a_in, b_in, keep_ref, out_ref, force, spare, other, later
+    n_col, me_ref, full_ref, came_ref, handed_ref, part_ref, out_ref, weight, force, later, spare, other
 ):
     _, _, gz = place(me_ref, n_col)
-    weight = full_ref.at[2]
-    for s in range(16):
-        m, z = s % 8 // 4, s % 4
-        into, own = (force, before_ref) if s < 8 else (later, spread_ref)
-        top, bottom = halo_rows(a_in, b_in, s, gz)
-        into[m, z, 0:H, :] = top * weight[z, 0:H]
-        into[m, z, H : H + 64, :] = own[4 * m + z] * weight[z, H : H + 64]
-        into[m, z, H + 64 : 2 * H + 64, :] = bottom * weight[z, H + 64 : 2 * H + 64]
+    empty = jnp.zeros((2 * H, 256), F32)
+    for z in range(4):
+        weight[z, 0 : 2 * H] = full_ref[2, z, 0 : 2 * H]
+        weight[z, 2 * H : 4 * H] = full_ref[2, z, 64 : 64 + 2 * H]
+    for s in range(8):
+        m, z = s // 4, s % 4
+        top, bottom = halo_rows(read_edge(came_ref, 0, s, 8), read_edge(handed_ref, 0, s, 8), gz)
+        force[m, z, 0:H] = top * weight[z, 0:H]
+        force[m, z, H : 3 * H] = empty
+        force[m, z, 3 * H : 4 * H] = bottom * weight[z, 3 * H : 4 * H]
+        ends = []
+        for ref, sender in ((came_ref, 1 - gz), (handed_ref, gz)):
+            tile = ref[9 + s // 2]
+            main = jnp.where(near_half(sender), pltpu.roll(tile, 4, 0) if s % 2 else tile, 0.0)
+            ends.append(jnp.concatenate([main, untuck(ref[13], s)], 1))
+        top, bottom = halo_rows(ends[0], ends[1], gz)
+        later[m, z, 0:H] = top * weight[z, 0:H]
+        later[m, z, H : 3 * H] = empty
+        later[m, z, 3 * H : 4 * H] = bottom * weight[z, 3 * H : 4 * H]
     sweep(force, spare, force, weight)
     sweep(spare, other, force, weight)
     sweep(other, spare, force, weight)
@@ -376,7 +468,10 @@
     sweep(other, spare, later, weight)
     for m in range(2):
         for k in range(2):
-            out_ref[m, k] = keep_ref[m, k] + spare[m, 2 * gz + k, H : H + 64, 0:128]
+            found = spare.at[m, 2 * gz + k]
+            out_ref[m, k, 0:H, :] = part_ref[m, k, 0:H, :] + found[H : 2 * H, 0:128]
+            out_ref[m, k, H : 64 - H, :] = part_ref[m, k, H : 64 - H, :]
+            out_ref[m, k, 64 - H : 64, :] = part_ref[m, k, 64 - H : 64, :] + found[2 * H : 3 * H, 0:128]
 
 
 SMEM = pl.BlockSpec(memory_space=pltpu.SMEM)
@@ -441,7 +536,7 @@
     ext, edge = run(
         functools.partial(row_pack, n_col),
         "row_pack",
-        [(12, 64, 256), (12, H, 256)],
+        [(12, 64, 256), (14, H, 128)],
         [me, packed, other, a, b],
     )
     a, b = beside(edge)
@@ -480,15 +575,15 @@
             pl.BlockSpec((1, nodes, blocks * nodes), lambda i: (i, 0, 0)),
             everything((blocks, 16, nodes)),
         ],
-        scratch_shapes=sums,
+        scratch_shapes=sums + [pltpu.VMEM((48, blocks * nodes), jnp.bfloat16)],
         compiler_params=pltpu.CompilerParams(vmem_limit_bytes=16 << 20),
         cost_estimate=pl.CostEstimate(flops=18 * work, bytes_accessed=4 * work, transcendentals=work),
     )(me, heard, target, kept)
     partial = lax.all_to_all(partial, ("col", "gz"), 0, 0)
-    before, sent = run(
+    before, sent, second = run(
         functools.partial(respond, n_col, n_row),
         "respond",
-        [(8, 64, 256), (n_row, 8, nodes)],
+        [(8, 64, 256), (n_row, 8, nodes), field],
         [me, partial, target, full, heard, kept],
         [field] * 3,
     )
@@ -514,16 +609,25 @@
     spread, edge, values = run(
         functools.partial(last_spread, n_col),
         "last_spread",
-        [(8, 64, 256), (16, H, 256), (2, nodes)],
+        [(8, 64, 256), (14, H, 128), (2, nodes)],
         [me, partial, target, before],
     )
     a, b = beside(edge)
+    (part,) = run(
+        functools.partial(own_relax, n_col),
+        "own_relax",
+        [(2, 2, 64, 128)],
+        [me, full, second, spread, keep],
+        [field] * 3,
+        flops=40 * size_of(field),
+    )
+    strip = (2, 4, 4 * H, 256)
     (potential,) = run(
         functools.partial(last_relax, n_col),
         "last_relax",
         [(2, 2, 64, 128)],
-        [me, full, before, spread, a, b, keep],
-        [field] * 4,
+        [me, full, a, b, part],
+        [strip[1:]] + [strip] * 4,
     )
     return potential, values
 

time: 125 us -> 120 us (0.960)
  waiting for transfers between devices: 26.6 us -> 23.9 us
  Pallas kernels: 32.5 us -> 30.9 us
  starting transfers between devices: 31 us -> 29.4 us
  blocking collectives: 32.5 us -> 33.8 us
    all_to_all x1, waiting for transfers between devices: 4.41 us -> 0.01 us  [on_device(): target = lax.all_to_all(told, ('col', 'gz'), 0, 0)]
    pallas_call x1, Pallas kernels: 11.1 us -> 8.81 us  [on_device(): pl.pallas_call(functools.partial(build_apply, n_col, n_row), name='build_...]
    ppermute x2, starting transfers between devices: 2.01 us -> 0.01 us  [beside(): return (came, lax.ppermute(came, 'gz', [(0, 1), (1, 0)]))]
    all_to_all x2, blocking collectives: 19.7 us -> 21.1 us  [on_device(): partial = lax.all_to_all(partial, ('col', 'gz'), 0, 0)]
    pallas_call x8 -> x9, Pallas kernels: 16.3 us -> 16.9 us  [run(): pl.pallas_call(body, name=name, out_shape=[jax.ShapeDtypeStruct(o, F32) f...]
  transfers between devices with their start and end apart: 9 -> 9, of which waited for: 6 -> 6; matrix products, arithmetic and copies ran while one was open for 0% -> 0% of each run, Pallas kernels for 2% -> 4%
where the time goes in v4:
time: 120 us
  blocking collectives  33.8 us (28%)
  Pallas kernels  30.9 us (26%)
  starting transfers between devices  29.4 us (24%)
  waiting for transfers between devices  23.9 us (20%)
    all_to_all x2, blocking collectives, on_device(): partial = lax.all_to_all(partial, ('col', 'gz'), 0, 0)  21.1 us
    pallas_call x9, Pallas kernels, run(): pl.pallas_call(body, name=name, out_shape=[jax.ShapeDtypeStruct(o, F32) f...  16.9 us
    all_to_all x1, blocking collectives, on_device(): again = lax.all_to_all(sent, 'row', 0, 0)  12.8 us
    ppermute x2, starting transfers between devices, beside(): came = lax.ppermute(edge, ('row', 'gz'), came + [(j, i) for i, j in came])  10.7 us
    pallas_call x1, Pallas kernels, on_device(): pl.pallas_call(functools.partial(build_apply, n_col, n_row), name='build_...  8.81 us
    all_to_all x1, starting transfers between devices, on_device(): heard = lax.all_to_all(sent, 'row', 0, 0)  8.15 us
    all_to_all x1, starting transfers between devices, on_device(): target = lax.all_to_all(told, ('col', 'gz'), 0, 0)  7.76 us
    ppermute x2, waiting for transfers between devices, beside(): came = lax.ppermute(edge, ('row', 'gz'), came + [(j, i) for i, j in came])  7.28 us
  transfers between devices with their start and end apart: 9, of which 6 were waited for; matrix products, arithmetic and copies ran while one was open for 0% of the time, Pallas kernels for 4%

profile of v4, /device:TPU:8, one launch (start us, length us, event | category | flops | bytes accessed | tf_op | source)
XLA Modules:
  0.0 119.7 jit_solution(11630083763506609294)
XLA Ops:
  0.6 1.8 %prepare.1 = (f32[3,2,64,128]{3,2,1,0:T(8,128)}, f32[16,8,128]{2,1,0:T(8,128)}) custom-call(f32[8]{0:T(128)} %table_hbm.1, f32[2,2,64,128]{3,2,1,0:T(8,128)} %source_hbm.1, s32[2,64,128]{2,1,0:T(8,128)} %class_hbm.1, s32[1,128]{1,0:T(1,128)} %bitcast.3, f32[3,128]{1,0:T(4,128)} %pos_hbm.1, f32[1,128]{1,0:T(1,128)} %bitcast.4), custom_call_target="tpu_custom_call" | custom-call | tf_op jit(solution)/shard_map/prepare/pallas_call | solution.py:515
  2.4 2.0 %collective-permute-start = (f32[3,2,64,128]{3,2,1,0:T(8,128)}, f32[3,2,64,128]{3,2,1,0:T(8,128)S(1)}, u32[]{:S(2)}, u32[]{:S(2)}) collective-permute-start(f32[3,2,64,128]{3,2,1,0:T(8,128)} %get-tuple-element.21.own_ref), channel_id=1, source_target_pairs={{0,1},{1,0},{2,3},{3,2},{4,5},{5,4},{6,7},{7,6},{8,9},{9,8},{10,11... | collective-permute-start | bytes 589832 | tf_op jit(solution)/shard_map/ppermute | solution.py:531
  4.4 1.0 copy-done
  5.4 4.1 %collective-permute-done.other_ref = f32[3,2,64,128]{3,2,1,0:T(8,128)S(1)} collective-permute-done((f32[3,2,64,128]{3,2,1,0:T(8,128)}, f32[3,2,64,128]{3,2,1,0:T(8,128)S(1)}, u32[]{:S(2)}, u32[]{:S(2)}) %collective-permute-start) | collective-permute-done | bytes 196640 | tf_op jit(solution)/shard_map/ppermute | solution.py:531
  9.5 0.3 col_pack.1
  9.8 0.1 collective-permute-start.1
  9.9 0.7 collective-permute-start.2
  10.6 7.8 %all-to-all-start = ((f32[16,8,128]{2,1,0:T(8,128)}), f32[16,8,128]{2,1,0:T(8,128)S(1)}, u32[]{:S(2)}, u32[]{:S(2)}) async-start(f32[16,8,128]{2,1,0:T(8,128)} %get-tuple-element.26), calls=%async_computation | async-start | bytes 131072 | tf_op jit(solution)/shard_map/all_to_all | solution.py:532
  18.3 0.0 collective-permute-done.1.a_in
  18.4 0.0 collective-permute-done.2.b_in
  18.4 0.3 row_pack.1
  18.7 7.7 %collective-permute-start.3 = (f32[14,8,128]{2,1,0:T(8,128)S(1)}, f32[14,8,128]{2,1,0:T(8,128)S(1)}, u32[]{:S(2)}, u32[]{:S(2)}) collective-permute-start(f32[14,8,128]{2,1,0:T(8,128)S(1)} %get-tuple-element.25), channel_id=1, source_target_pairs={{1,16},{17,32},{33,48},{49,64},{65,80},{81,96},{97,112},{113,128},... | collective-permute-start | bytes 172040 | tf_op jit(solution)/shard_map/ppermute | solution.py:512
  26.4 2.2 %collective-permute-done.3.a_in = f32[14,8,128]{2,1,0:T(8,128)S(1)} collective-permute-done((f32[14,8,128]{2,1,0:T(8,128)S(1)}, f32[14,8,128]{2,1,0:T(8,128)S(1)}, u32[]{:S(2)}, u32[]{:S(2)}) %collective-permute-start.3) | collective-permute-done | bytes 57376 | tf_op jit(solution)/shard_map/ppermute | solution.py:512
  28.5 0.0 collective-permute-start.4
  28.5 4.2 %collective-permute-done.4.b_in = f32[14,8,128]{2,1,0:T(8,128)S(1)} collective-permute-done((f32[14,8,128]{2,1,0:T(8,128)S(1)}, f32[14,8,128]{2,1,0:T(8,128)S(1)}, u32[]{:S(2)}, u32[]{:S(2)}) %collective-permute-start.4) | collective-permute-done | bytes 57376 | tf_op jit(solution)/shard_map/ppermute | solution.py:513
  32.7 2.6 %first_relax.1 = (f32[3,4,80,256]{3,2,1,0:T(8,128)S(1)}, f32[2,4,80,256]{3,2,1,0:T(8,128)S(1)}, f32[16,8,128]{2,1,0:T(8,128)}) custom-call(s32[1]{0:T(128)} %bitcast.me_ref, f32[12,64,256]{2,1,0:T(8,128)S(1)} %get-tuple-element.24.ext_ref, f32[14,8,128]{2,1,0:T(8,128)S(1)} %collective-permute-done.3.a_in, f32[14,8,128]{2,1,0:T(8,128)S(1)} %collective-permute-done.4.b_in, ...), custom_call_target="tpu_custom_call" | custom-call | bytes 2670596 | tf_op jit(solution)/shard_map/first_relax/pallas_call | solution.py:487
  35.4 8.1 %all-to-all-start.1 = ((f32[16,8,128]{2,1,0:T(8,128)}), f32[16,8,128]{2,1,0:T(8,128)S(1)}, u32[]{:S(2)}, u32[]{:S(2)}) async-start(f32[16,8,128]{2,1,0:T(8,128)} %get-tuple-element.28), calls=%async_computation.1 | async-start | bytes 131072 | tf_op jit(solution)/shard_map/all_to_all | solution.py:552
  43.5 2.5 %carry_relax.1 = (f32[2,2,64,128]{3,2,1,0:T(8,128)S(1)}, f32[2,128]{1,0:T(2,128)S(1)}) custom-call(s32[1]{0:T(128)} %bitcast.me_ref, f32[3,4,80,256]{3,2,1,0:T(8,128)S(1)} %get-tuple-element.27.full_ref, f32[2,4,80,256]{3,2,1,0:T(8,128)S(1)} %get-tuple-element.29.first_ref, f32[16,8,128]{2,1,0:T(8,128)S(1)} %all-to-all-done.target_ref), custom_call_target="tpu_custom_call" | custom-call | flops 6553600 | bytes 1836036 | tf_op jit(solution)/shard_map/carry_relax/pallas_call | solution.py:487
  46.0 6.3 %all-to-all-done.1.heard_ref.info_ref = f32[16,8,128]{2,1,0:T(8,128)S(1)} async-done(((f32[16,8,128]{2,1,0:T(8,128)}), f32[16,8,128]{2,1,0:T(8,128)S(1)}, u32[]{:S(2)}, u32[]{:S(2)}) %all-to-all-start.1) | async-done | bytes 65568 | tf_op jit(solution)/shard_map/all_to_all | solution.py:552
  52.3 8.8 %build_apply.1 = (f32[16,128,2048]{2,1,0:T(8,128)S(1)}, f32[16,16,128]{2,1,0:T(8,128)S(1)}) custom-call(s32[1]{0:T(128)} %bitcast.me_ref, f32[16,8,128]{2,1,0:T(8,128)S(1)} %all-to-all-done.1.heard_ref.info_ref, f32[16,8,128]{2,1,0:T(8,128)S(1)} %all-to-all-done.target_ref, f32[2,128]{1,0:T(2,128)S(1)} %get-tuple-element.30._.kept_ref), custom_call_target="tpu_custom_call" | custom-call | flops 75497472 | bytes 16777216 | tf_op jit(solution)/shard_map/build_apply/pallas_call | solution.py:565
  61.1 11.9 %all_to_all.25.part_ref = f32[16,16,128]{2,1,0:T(8,128)S(1)} all-to-all(f32[16,16,128]{2,1,0:T(8,128)S(1)} %get-tuple-element.31), channel_id=1, replica_groups=mesh['row'=16,'col'=8,'gz'=2] {'col','gz'}, dimensions={0} | all-to-all | bytes 262144 | tf_op jit(solution)/shard_map/all_to_all | solution.py:582
  73.0 4.9 %respond.1 = (f32[8,64,256]{2,1,0:T(8,128)S(1)}, f32[16,8,128]{2,1,0:T(8,128)S(1)}, f32[2,4,80,256]{3,2,1,0:T(8,128)S(1)}) custom-call(s32[1]{0:T(128)} %bitcast.me_ref, f32[16,16,128]{2,1,0:T(8,128)S(1)} %all_to_all.25.part_ref, f32[16,8,128]{2,1,0:T(8,128)S(1)} %all-to-all-done.target_ref, f32[3,4,80,256]{3,2,1,0:T(8,128)S(1)} %get-tuple-element.27.full_ref, ...), custom_call_target="tpu_custom_call" | custom-call | bytes 2491396 | tf_op jit(solution)/shard_map/respond/pallas_call | solution.py:487
  77.9 12.8 %all_to_all.26.heard_ref = f32[16,8,128]{2,1,0:T(8,128)S(1)} all-to-all(f32[16,8,128]{2,1,0:T(8,128)S(1)} %get-tuple-element.32), channel_id=1, replica_groups=mesh['row'=16,'col'=8,'gz'=2] {'row'}, dimensions={0} | all-to-all | bytes 131072 | tf_op jit(solution)/shard_map/all_to_all | solution.py:590
  90.6 3.4 %reapply.1 = f32[16,16,128]{2,1,0:T(8,128)S(1)} custom-call(s32[1]{0:T(128)} %bitcast.me_ref, f32[16,8,128]{2,1,0:T(8,128)S(1)} %all_to_all.26.heard_ref, f32[16,8,128]{2,1,0:T(8,128)S(1)} %all-to-all-done.1.heard_ref.info_ref, f32[16,128,2048]{2,1,0:T(8,128)S(1)} %get-tuple-element.33.pair_ref), custom_call_target="tpu_custom_call" | custom-call | flops 16777216 | bytes 16777216 | tf_op jit(solution)/shard_map/reapply/pallas_call | solution.py:592
  94.0 9.2 %all_to_all.27.part_ref = f32[16,16,128]{2,1,0:T(8,128)S(1)} all-to-all(f32[16,16,128]{2,1,0:T(8,128)S(1)} %reapply.1), channel_id=1, replica_groups=mesh['row'=16,'col'=8,'gz'=2] {'col','gz'}, dimensions={0} | all-to-all | bytes 262144 | tf_op jit(solution)/shard_map/all_to_all | solution.py:608
  103.2 1.4 %last_spread.1 = (f32[8,64,256]{2,1,0:T(8,128)S(1)}, f32[14,8,128]{2,1,0:T(8,128)S(1)}, f32[2,128]{1,0:T(2,128)}) custom-call(s32[1]{0:T(128)} %bitcast.me_ref, f32[16,16,128]{2,1,0:T(8,128)S(1)} %all_to_all.27.part_ref, f32[16,8,128]{2,1,0:T(8,128)S(1)} %all-to-all-done.target_ref, f32[8,64,256]{2,1,0:T(8,128)S(1)} %get-tuple-element.34.before_ref), custom_call_target="tpu_custom_call" | custom-call | bytes 1303556 | tf_op jit(solution)/shard_map/last_spread/pallas_call | solution.py:487
  104.6 3.1 %collective-permute-start.5 = (f32[14,8,128]{2,1,0:T(8,128)S(1)}, f32[14,8,128]{2,1,0:T(8,128)S(1)}, u32[]{:S(2)}, u32[]{:S(2)}) collective-permute-start(f32[14,8,128]{2,1,0:T(8,128)S(1)} %get-tuple-element.35), channel_id=1, source_target_pairs={{1,16},{17,32},{33,48},{49,64},{65,80},{81,96},{97,112},{113,128},... | collective-permute-start | bytes 172040 | tf_op jit(solution)/shard_map/ppermute | solution.py:512
  107.6 5.1 %collective-permute-done.5.came_ref = f32[14,8,128]{2,1,0:T(8,128)S(1)} collective-permute-done((f32[14,8,128]{2,1,0:T(8,128)S(1)}, f32[14,8,128]{2,1,0:T(8,128)S(1)}, u32[]{:S(2)}, u32[]{:S(2)}) %collective-permute-start.5) | collective-permute-done | bytes 57376 | tf_op jit(solution)/shard_map/ppermute | solution.py:512
  112.7 0.0 collective-permute-start.6
  112.7 2.2 %own_relax.1.part_ref = f32[2,2,64,128]{3,2,1,0:T(8,128)S(1)} custom-call(s32[1]{0:T(128)} %bitcast.me_ref, f32[3,4,80,256]{3,2,1,0:T(8,128)S(1)} %get-tuple-element.27.full_ref, f32[2,4,80,256]{3,2,1,0:T(8,128)S(1)} %get-tuple-element.36.second_ref, f32[8,64,256]{2,1,0:T(8,128)S(1)} %get-tuple-element.37.spread_ref, ...), custom_call_target="tpu_custom_call" | custom-call | flops 6553600 | bytes 2424836 | tf_op jit(solution)/shard_map/own_relax/pallas_call | solution.py:487
  114.9 2.0 %collective-permute-done.6.handed_ref = f32[14,8,128]{2,1,0:T(8,128)S(1)} collective-permute-done((f32[14,8,128]{2,1,0:T(8,128)S(1)}, f32[14,8,128]{2,1,0:T(8,128)S(1)}, u32[]{:S(2)}, u32[]{:S(2)}) %collective-permute-start.6) | collective-permute-done | bytes 57376 | tf_op jit(solution)/shard_map/ppermute | solution.py:513
  116.9 2.8 %last_relax.1 = f32[2,2,64,128]{3,2,1,0:T(8,128)} custom-call(s32[1]{0:T(128)} %bitcast.me_ref, f32[3,4,80,256]{3,2,1,0:T(8,128)S(1)} %get-tuple-element.27.full_ref, f32[14,8,128]{2,1,0:T(8,128)S(1)} %collective-permute-done.5.came_ref, f32[14,8,128]{2,1,0:T(8,128)S(1)} %collective-permute-done.6.handed_ref, f32[2,2,64,128]{3,2,1,0:T(8,128)S(1)} %own_relax.1.part_ref), custom_call_target="tpu_custom_call" | custom-call | bytes 1359876 | tf_op jit(solution)/shard_map/last_relax/pallas_call | solution.py:487
  (3 shorter events, 0.0 us)
Async XLA Ops:
  2.4 7.1 %collective-permute-start = (f32[3,2,64,128]{3,2,1,0:T(8,128)}, f32[3,2,64,128]{3,2,1,0:T(8,128)S(1)}, u32[]{:S(2)}, u32[]{:S(2)}) collective-permute-start(f32[3,2,64,128]{3,2,1,0:T(8,128)} %get-tuple-element.21.own_ref), channel_id=1, source_target_pairs={{0,1},{1,0},{2,3},{3,2},{4,5},{5,4},{6,7},{7,6},{8,9},{9,8},{10,11... | collective-permute-start | bytes 589832 | tf_op jit(solution)/shard_map/ppermute | solution.py:531
  4.4 1.0 copy-start
  9.8 8.5 %collective-permute-start.1 = (f32[64,128]{1,0:T(8,128)S(1)}, f32[64,128]{1,0:T(8,128)S(1)}, u32[]{:S(2)}, u32[]{:S(2)}) collective-permute-start(f32[64,128]{1,0:T(8,128)S(1)} %get-tuple-element.22), channel_id=1, source_target_pairs={{0,2},{2,0},{4,6},{6,4},{8,10},{10,8},{12,14},{14,12},{1,3},{3,1},... | collective-permute-start | bytes 98312 | tf_op jit(solution)/shard_map/ppermute | solution.py:508
  9.9 8.4 %collective-permute-start.2 = (f32[64,128]{1,0:T(8,128)S(1)}, f32[64,128]{1,0:T(8,128)S(1)}, u32[]{:S(2)}, u32[]{:S(2)}) collective-permute-start(f32[64,128]{1,0:T(8,128)S(1)} %get-tuple-element.23), channel_id=1, source_target_pairs={{2,4},{6,8},{10,12},{4,2},{8,6},{12,10},{3,5},{7,9},{11,13},{5,3},... | collective-permute-start | bytes 98312 | tf_op jit(solution)/shard_map/ppermute | solution.py:508
  10.6 18.0 %all-to-all-start = ((f32[16,8,128]{2,1,0:T(8,128)}), f32[16,8,128]{2,1,0:T(8,128)S(1)}, u32[]{:S(2)}, u32[]{:S(2)}) async-start(f32[16,8,128]{2,1,0:T(8,128)} %get-tuple-element.26), calls=%async_computation | async-start | bytes 131072 | tf_op jit(solution)/shard_map/all_to_all | solution.py:532
  18.7 9.8 %collective-permute-start.3 = (f32[14,8,128]{2,1,0:T(8,128)S(1)}, f32[14,8,128]{2,1,0:T(8,128)S(1)}, u32[]{:S(2)}, u32[]{:S(2)}) collective-permute-start(f32[14,8,128]{2,1,0:T(8,128)S(1)} %get-tuple-element.25), channel_id=1, source_target_pairs={{1,16},{17,32},{33,48},{49,64},{65,80},{81,96},{97,112},{113,128},... | collective-permute-start | bytes 172040 | tf_op jit(solution)/shard_map/ppermute | solution.py:512
  28.5 4.2 %collective-permute-start.4 = (f32[14,8,128]{2,1,0:T(8,128)S(1)}, f32[14,8,128]{2,1,0:T(8,128)S(1)}, u32[]{:S(2)}, u32[]{:S(2)}) collective-permute-start(f32[14,8,128]{2,1,0:T(8,128)S(1)} %collective-permute-done.3.a_in), channel_id=1, source_target_pairs={{0,1},{1,0},{2,3},{3,2},{4,5},{5,4},{6,7},{7,6},{8,9},{9,8},{10,11... | collective-permute-start | bytes 172040 | tf_op jit(solution)/shard_map/ppermute | solution.py:513
  35.4 16.9 %all-to-all-start.1 = ((f32[16,8,128]{2,1,0:T(8,128)}), f32[16,8,128]{2,1,0:T(8,128)S(1)}, u32[]{:S(2)}, u32[]{:S(2)}) async-start(f32[16,8,128]{2,1,0:T(8,128)} %get-tuple-element.28), calls=%async_computation.1 | async-start | bytes 131072 | tf_op jit(solution)/shard_map/all_to_all | solution.py:552
  104.6 8.2 %collective-permute-start.5 = (f32[14,8,128]{2,1,0:T(8,128)S(1)}, f32[14,8,128]{2,1,0:T(8,128)S(1)}, u32[]{:S(2)}, u32[]{:S(2)}) collective-permute-start(f32[14,8,128]{2,1,0:T(8,128)S(1)} %get-tuple-element.35), channel_id=1, source_target_pairs={{1,16},{17,32},{33,48},{49,64},{65,80},{81,96},{97,112},{113,128},... | collective-permute-start | bytes 172040 | tf_op jit(solution)/shard_map/ppermute | solution.py:512
  112.7 4.2 %collective-permute-start.6 = (f32[14,8,128]{2,1,0:T(8,128)S(1)}, f32[14,8,128]{2,1,0:T(8,128)S(1)}, u32[]{:S(2)}, u32[]{:S(2)}) collective-permute-start(f32[14,8,128]{2,1,0:T(8,128)S(1)} %collective-permute-done.5.came_ref), channel_id=1, source_target_pairs={{0,1},{1,0},{2,3},{3,2},{4,5},{5,4},{6,7},{7,6},{8,9},{9,8},{10,11... | collective-permute-start | bytes 172040 | tf_op jit(solution)/shard_map/ppermute | solution.py:513

commit v5 on v4

--- a/solution.py
+++ b/solution.py
@@ -7,12 +7,11 @@
 from jax.experimental.pallas import tpu as pltpu
 from jax.sharding import PartitionSpec as P
 
-SWEEPS = 4
+
 OMEGA = 0.8
 RELAX = 0.5
 SOFTEN = 0.01
 H = 8
-HIGH = lax.Precision.HIGHEST
 F32 = jnp.float32
 
 
@@ -54,9 +53,9 @@
     b_ref[...] = pick(odd, shape, right, left)
 
 
-def edge_row(from_ref, s, gz):
+def edge_row(from_ref, s, last):
     rows, lanes = from_ref.shape[1:]
-    return pick(gz, (H, lanes), from_ref[s, rows - H : rows, :], from_ref[s, 0:H, :])
+    return pick(last, (H, lanes), from_ref[s, rows - H : rows, :], from_ref[s, 0:H, :])
 
 
 def tuck(side, s, into):
@@ -71,11 +70,11 @@
     return jnp.where((lane < 8) | (lane >= 120), moved, 0.0)
 
 
-def write_edges(edge_ref, start, from_ref, count, gz):
+def write_edges(edge_ref, start, from_ref, count, last):
     for first in range(0, count, 8):
         side = jnp.zeros((H, 128), F32)
         for s in range(first, min(first + 8, count)):
-            edge = edge_row(from_ref, s, gz)
+            edge = edge_row(from_ref, s, last)
             edge_ref[start + s] = edge[:, 0:128]
             side = tuck(edge[:, 128:256], s - first, side)
         edge_ref[start + count + first // 8] = side
@@ -85,19 +84,18 @@
     return jnp.concatenate([ref[start + s], untuck(ref[start + count + s // 8], s % 8)], 1)
 
 
-def near_half(sent_gz):
-    line = iota((H, 128), 0)
-    return (line // 4) == jnp.full((H, 128), sent_gz, jnp.int32)
-
-
-def halo_rows(came, handed, gz):
-    return pick(gz, came.shape, handed, came), pick(gz, came.shape, came, handed)
-
-
-def row_pack(n_col, me_ref, own_ref, other_ref, a_in, b_in, ext_ref, edge_ref):
-    _, col, gz = place(me_ref, n_col)
+def near_half(last):
+    return (iota((H, 128), 0) // 4) == jnp.full((H, 128), last, jnp.int32)
+
+
+def halo_rows(a, b, odd):
+    return pick(odd, a.shape, a, b), pick(odd, a.shape, b, a)
+
+
+def row_pack(n_col, me_ref, own_ref, other_ref, a_in, b_in, ext_ref, a_ref, b_ref):
+    row, col, gz = place(me_ref, n_col)
     shape = own_ref.shape[2:]
-    rows, lanes = shape
+    _, lanes = shape
     lane = iota(shape, 1)
     odd_col = lax.rem(col, 2)
     from_right = pick(odd_col, shape, b_in[...], a_in[...])
@@ -109,7 +107,9 @@
         side = jnp.where(lane < 8, low, jnp.where(lane >= lanes - 8, high, 0.0))
         ext_ref[s, :, 0:lanes] = cell
         ext_ref[s, :, lanes : 2 * lanes] = side
-    write_edges(edge_ref, 0, ext_ref, 12, gz)
+    odd = lax.rem(row, 2)
+    write_edges(a_ref, 0, ext_ref, 12, 1 - odd)
+    write_edges(b_ref, 0, ext_ref, 12, odd)
 
 
 def sweep(now_ref, next_ref, force_ref, weight_ref):
@@ -127,7 +127,14 @@
             next_ref[m, z] = (1.0 - OMEGA) * cell + (force_ref[m, z] + weight_ref[z] * beside)
         return carry
 
-    lax.fori_loop(0, now_ref.shape[0], image, 0)
+    lax.fori_loop(0, now_ref.shape[0], image, 0, unroll=rows < 64)
+
+
+def split(x):
+    high = x.astype(jnp.bfloat16).astype(F32)
+    rest = x - high
+    middle = rest.astype(jnp.bfloat16).astype(F32)
+    return high, middle, rest - middle
 
 
 def trace_of(rows, owner, first_row):
@@ -135,9 +142,14 @@
     nodes = owner.shape[1]
     line = iota((2 * span, nodes), 0)
     line = line + first_row + jnp.where(line >= span, 64 - span, 0)
-    at_row = jnp.where(line == owner // 128, 1.0, 0.0).astype(F32)
+    at_row = jnp.where(line == owner // 128, 1.0, 0.0).astype(jnp.bfloat16)
     at_lane = iota((128, nodes), 0) == lax.rem(owner, 128)
-    found = lax.dot_general(rows, at_row, (((0,), (0,)), ((), ())), precision=HIGH, preferred_element_type=F32)
+    found = sum(
+        lax.dot_general(
+            part.astype(jnp.bfloat16), at_row, (((0,), (0,)), ((), ())), preferred_element_type=F32
+        )
+        for part in split(rows)
+    )
     return jnp.sum(jnp.where(at_lane, found, 0.0), axis=0, keepdims=True)
 
 
@@ -183,9 +195,10 @@
 
 
 def first_relax(n_col, me_ref, ext_ref, a_in, b_in, target_ref, full_ref, first_ref, sent_ref, force, spare):
-    _, col, gz = place(me_ref, n_col)
+    row, col, gz = place(me_ref, n_col)
+    odd = lax.rem(row, 2)
     for s in range(12):
-        top, bottom = halo_rows(read_edge(a_in, 0, s, 12), read_edge(b_in, 0, s, 12), gz)
+        top, bottom = halo_rows(read_edge(a_in, 0, s, 12), read_edge(b_in, 0, s, 12), odd)
         full_ref[s // 4, s % 4, 0:H, :] = top
         full_ref[s // 4, s % 4, H : H + 64, :] = ext_ref[s]
         full_ref[s // 4, s % 4, H + 64 : 2 * H + 64, :] = bottom
@@ -239,13 +252,6 @@
             near = lined[m, 2 * c : 2 * c + 8, :]
             out_ref[2 * c, 8 * m : 8 * m + 8, :] = near
             out_ref[2 * c + 1, 8 * m : 8 * m + 8, :] = near
-
-
-def split(x):
-    high = x.astype(jnp.bfloat16).astype(F32)
-    rest = x - high
-    middle = rest.astype(jnp.bfloat16).astype(F32)
-    return high, middle, rest - middle
 
 
 def build_apply(n_col, n_row, me_ref, heard_ref, target_ref, _, pair_ref, out_ref, acc, lined, goal):
@@ -344,10 +350,13 @@
             lane = lane & (down >= 128 - H)
         if b > 3:
             lane = lane & (down < H)
-        lanes.append(jnp.where(lane, 1.0, 0.0).astype(F32))
+        lanes.append(jnp.where(lane, 1.0, 0.0).astype(jnp.bfloat16))
 
     def product(a, b):
-        return lax.dot_general(a, b, (((1,), (1,)), ((), ())), precision=HIGH, preferred_element_type=F32)
+        parts = jnp.concatenate(split(a), 0).astype(jnp.bfloat16)
+        found = lax.dot_general(parts, b, (((1,), (1,)), ((), ())), preferred_element_type=F32)
+        count = a.shape[0]
+        return found[0:count] + (found[count : 2 * count] + found[2 * count : 3 * count])
 
     for g in range(2):
         own = product(weighted[2 + g], lanes[2 + g])
@@ -398,18 +407,20 @@
         sent_ref[k] = sent
 
 
-def last_spread(n_col, me_ref, part_ref, target_ref, before_ref, spread_ref, edge_ref, value_ref):
-    _, col, gz = place(me_ref, n_col)
+def last_spread(n_col, me_ref, part_ref, target_ref, before_ref, spread_ref, a_ref, b_ref, value_ref):
+    row, col, gz = place(me_ref, n_col)
     value = spread_nodes(n_col, col, part_ref, target_ref, spread_ref)
-    write_edges(edge_ref, 0, before_ref, 8, gz)
-    near = near_half(gz)
-    side = jnp.zeros((H, 128), F32)
-    for s in range(0, 8, 2):
-        one, two = edge_row(spread_ref, s, gz), edge_row(spread_ref, s + 1, gz)
-        edge_ref[9 + s // 2] = jnp.where(near, one[:, 0:128], pltpu.roll(two[:, 0:128], 4, 0))
-        side = tuck(one[:, 128:256], s, side)
-        side = tuck(two[:, 128:256], s + 1, side)
-    edge_ref[13] = side
+    odd = lax.rem(row, 2)
+    for edge_ref, last in ((a_ref, 1 - odd), (b_ref, odd)):
+        write_edges(edge_ref, 0, before_ref, 8, last)
+        near = near_half(last)
+        side = jnp.zeros((H, 128), F32)
+        for s in range(0, 8, 2):
+            one, two = edge_row(spread_ref, s, last), edge_row(spread_ref, s + 1, last)
+            edge_ref[9 + s // 2] = jnp.where(near, one[:, 0:128], pltpu.roll(two[:, 0:128], 4, 0))
+            side = tuck(one[:, 128:256], s, side)
+            side = tuck(two[:, 128:256], s + 1, side)
+        edge_ref[13] = side
     for m in range(2):
         value_ref[m : m + 1, :] = pick(
             gz, (1, value.shape[1]), value[8 * m + 3 : 8 * m + 4, :], value[8 * m + 2 : 8 * m + 3, :]
@@ -434,25 +445,26 @@
 
 
 def last_relax(
-    n_col, me_ref, full_ref, came_ref, handed_ref, part_ref, out_ref, weight, force, later, spare, other
+    n_col, me_ref, full_ref, a_in, b_in, part_ref, out_ref, weight, force, later, spare, other
 ):
-    _, _, gz = place(me_ref, n_col)
+    row, _, gz = place(me_ref, n_col)
+    odd = lax.rem(row, 2)
     empty = jnp.zeros((2 * H, 256), F32)
     for z in range(4):
         weight[z, 0 : 2 * H] = full_ref[2, z, 0 : 2 * H]
         weight[z, 2 * H : 4 * H] = full_ref[2, z, 64 : 64 + 2 * H]
     for s in range(8):
         m, z = s // 4, s % 4
-        top, bottom = halo_rows(read_edge(came_ref, 0, s, 8), read_edge(handed_ref, 0, s, 8), gz)
+        top, bottom = halo_rows(read_edge(a_in, 0, s, 8), read_edge(b_in, 0, s, 8), odd)
         force[m, z, 0:H] = top * weight[z, 0:H]
         force[m, z, H : 3 * H] = empty
         force[m, z, 3 * H : 4 * H] = bottom * weight[z, 3 * H : 4 * H]
         ends = []
-        for ref, sender in ((came_ref, 1 - gz), (handed_ref, gz)):
+        for ref, last in ((a_in, odd), (b_in, 1 - odd)):
             tile = ref[9 + s // 2]
-            main = jnp.where(near_half(sender), pltpu.roll(tile, 4, 0) if s % 2 else tile, 0.0)
+            main = jnp.where(near_half(last), pltpu.roll(tile, 4, 0) if s % 2 else tile, 0.0)
             ends.append(jnp.concatenate([main, untuck(ref[13], s)], 1))
-        top, bottom = halo_rows(ends[0], ends[1], gz)
+        top, bottom = halo_rows(ends[0], ends[1], odd)
         later[m, z, 0:H] = top * weight[z, 0:H]
         later[m, z, H : 3 * H] = empty
         later[m, z, 3 * H : 4 * H] = bottom * weight[z, 3 * H : 4 * H]
@@ -482,11 +494,10 @@
     return functools.reduce(lambda a, b: a * b, shape)
 
 
-def run(body, name, outs, args, scratch=(), flops=0, scalars=1):
+def run(body, outs, args, scratch=(), flops=0, scalars=1):
     moved = sum(a.size * 4 for a in args) + sum(4 * size_of(o) for o in outs)
     return pl.pallas_call(
         body,
-        name=name,
         out_shape=[jax.ShapeDtypeStruct(o, F32) for o in outs],
         in_specs=[SMEM] * scalars + [VMEM] * (len(args) - scalars),
         out_specs=[VMEM] * len(outs),
@@ -505,12 +516,9 @@
         first = [(i, i ^ 1) for i in range(size)]
         second = [(i + 1, i + 2) for i in range(0, size - 2, 2)]
         second = second + [(j, i) for i, j in second]
-        return lax.ppermute(a, axis, first), lax.ppermute(b, axis, second)
-
-    def beside(edge):
-        came = [(2 * i + 1, 2 * i + 2) for i in range(n_row - 1)]
-        came = lax.ppermute(edge, ("row", "gz"), came + [(j, i) for i, j in came])
-        return came, lax.ppermute(came, "gz", [(0, 1), (1, 0)])
+        a = lax.ppermute(a, axis, first)
+        b = lax.ppermute(b, axis, second)
+        return a, b
 
     packed, told = pl.pallas_call(
         prepare,
@@ -530,21 +538,17 @@
     )(coeff_table, source, cell_class, owner_cell[None, :], node_pos, node_weight[None, :])
     other = lax.ppermute(packed, "gz", [(0, 1), (1, 0)])
     target = lax.all_to_all(told, ("col", "gz"), 0, 0)
-    (packed,) = run(stage, "stage", [packed.shape], [packed], scalars=0)
-    a, b = run(functools.partial(col_pack, n_col), "col_pack", [(64, 128)] * 2, [me, packed, other])
+    (packed,) = run(stage, [packed.shape], [packed], scalars=0)
+    a, b = run(functools.partial(col_pack, n_col), [(64, 128)] * 2, [me, packed, other])
     a, b = swaps("col", n_col, a, b)
-    ext, edge = run(
-        functools.partial(row_pack, n_col),
-        "row_pack",
-        [(12, 64, 256), (14, H, 128)],
-        [me, packed, other, a, b],
-    )
-    a, b = beside(edge)
+    ext, a, b = run(
+        functools.partial(row_pack, n_col), [(12, 64, 256), (14, H, 128), (14, H, 128)], [me, packed, other, a, b]
+    )
+    a, b = swaps("row", n_row, a, b)
 
     field = (2, 4, 64 + 2 * H, 256)
     full, first, sent = run(
         functools.partial(first_relax, n_col),
-        "first_relax",
         [(3, 4, 64 + 2 * H, 256), field, (n_row, 8, nodes)],
         [me, ext, a, b, target],
         [field] * 2,
@@ -552,7 +556,6 @@
     heard = lax.all_to_all(sent, "row", 0, 0)
     keep, kept = run(
         functools.partial(carry_relax, n_col),
-        "carry_relax",
         [(2, 2, 64, 128), (2, nodes)],
         [me, full, first, target],
         [field] * 3,
@@ -582,7 +585,6 @@
     partial = lax.all_to_all(partial, ("col", "gz"), 0, 0)
     before, sent, second = run(
         functools.partial(respond, n_col, n_row),
-        "respond",
         [(8, 64, 256), (n_row, 8, nodes), field],
         [me, partial, target, full, heard, kept],
         [field] * 3,
@@ -606,16 +608,14 @@
         cost_estimate=pl.CostEstimate(flops=4 * work, bytes_accessed=4 * work, transcendentals=0),
     )(me, again, heard, pairs)
     partial = lax.all_to_all(partial, ("col", "gz"), 0, 0)
-    spread, edge, values = run(
+    spread, a, b, values = run(
         functools.partial(last_spread, n_col),
-        "last_spread",
-        [(8, 64, 256), (14, H, 128), (2, nodes)],
+        [(8, 64, 256), (14, H, 128), (14, H, 128), (2, nodes)],
         [me, partial, target, before],
     )
-    a, b = beside(edge)
+    a, b = swaps("row", n_row, a, b)
     (part,) = run(
         functools.partial(own_relax, n_col),
-        "own_relax",
         [(2, 2, 64, 128)],
         [me, full, second, spread, keep],
         [field] * 3,
@@ -623,11 +623,7 @@
     )
     strip = (2, 4, 4 * H, 256)
     (potential,) = run(
-        functools.partial(last_relax, n_col),
-        "last_relax",
-        [(2, 2, 64, 128)],
-        [me, full, a, b, part],
-        [strip[1:]] + [strip] * 4,
+        functools.partial(last_relax, n_col), [(2, 2, 64, 128)], [me, full, a, b, part], [strip[1:]] + [strip] * 4
     )
     return potential, values
 

time: 120 us -> 113 us (0.942)
  waiting for transfers between devices: 23.9 us -> 13.2 us
  blocking collectives: 33.8 us -> 38.9 us
  Pallas kernels: 30.9 us -> 28.8 us
    ppermute x6, waiting for transfers between devices: 13.4 us -> 6.84 us  [the longest x3 6.63 us: swaps(): b = lax.ppermute(b, axis, second)]
    all_to_all x2, blocking collectives: 21.1 us -> 26.2 us  [on_device(): partial = lax.all_to_all(partial, ('col', 'gz'), 0, 0)]
    ppermute x1, waiting for transfers between devices: 4.12 us -> 0.01 us  [on_device(): other = lax.ppermute(packed, 'gz', [(0, 1), (1, 0)])]
    all_to_all x1, starting transfers between devices: 7.76 us -> 4.4 us  [on_device(): target = lax.all_to_all(told, ('col', 'gz'), 0, 0)]
    ppermute x6, starting transfers between devices: 11.5 us -> 14.7 us  [the longest x3 9.95 us: swaps(): b = lax.ppermute(b, axis, second)]
    pallas_call x9, Pallas kernels: 16.9 us -> 14.8 us  [run(): pl.pallas_call(body, out_shape=[jax.ShapeDtypeStruct(o, F32) for o in out...]
  transfers between devices with their start and end apart: 9 -> 9, of which waited for: 6 -> 4; matrix products, arithmetic and copies ran while one was open for 0% -> 0% of each run, Pallas kernels for 4% -> 5%
where the time goes in v5:
time: 113 us; the launch traced here: 112 us
  blocking collectives  38.9 us (34%)
  starting transfers between devices  29.5 us (26%)
  Pallas kernels  28.8 us (25%)
  waiting for transfers between devices  13.2 us (12%)
    all_to_all x2, blocking collectives, on_device(): partial = lax.all_to_all(partial, ('col', 'gz'), 0, 0)  26.2 us
    pallas_call x9, Pallas kernels, run(): pl.pallas_call(body, out_shape=[jax.ShapeDtypeStruct(o, F32) for o in out...  14.8 us
    all_to_all x1, blocking collectives, on_device(): again = lax.all_to_all(sent, 'row', 0, 0)  12.8 us
    ppermute x3, starting transfers between devices, swaps(): b = lax.ppermute(b, axis, second)  9.95 us
    pallas_call x1, Pallas kernels, on_device(): pl.pallas_call(functools.partial(build_apply, n_col, n_row), name='build_...  8.81 us
    all_to_all x1, starting transfers between devices, on_device(): heard = lax.all_to_all(sent, 'row', 0, 0)  8.41 us
    ppermute x3, waiting for transfers between devices, swaps(): b = lax.ppermute(b, axis, second)  6.63 us
    all_to_all x1, waiting for transfers between devices, on_device(): heard = lax.all_to_all(sent, 'row', 0, 0)  6.35 us
  transfers between devices with their start and end apart: 9, of which 4 were waited for; matrix products, arithmetic and copies ran while one was open for 0% of the time, Pallas kernels for 5%

profile of v5, /device:TPU:8, one launch (start us, length us, event | category | flops | bytes accessed | tf_op | source)
XLA Modules:
  0.0 112.1 jit_solution(2874646561211552131)
XLA Ops:
  0.6 1.8 %prepare.1 = (f32[3,2,64,128]{3,2,1,0:T(8,128)}, f32[16,8,128]{2,1,0:T(8,128)}) custom-call(f32[8]{0:T(128)} %table_hbm.1, f32[2,2,64,128]{3,2,1,0:T(8,128)} %source_hbm.1, s32[2,64,128]{2,1,0:T(8,128)} %class_hbm.1, s32[1,128]{1,0:T(1,128)} %bitcast.3, f32[3,128]{1,0:T(4,128)} %pos_hbm.1, f32[1,128]{1,0:T(1,128)} %bitcast.4), custom_call_target="tpu_custom_call" | custom-call | tf_op jit(solution)/shard_map/prepare/pallas_call | solution.py:523
  2.4 2.0 %collective-permute-start = (f32[3,2,64,128]{3,2,1,0:T(8,128)}, f32[3,2,64,128]{3,2,1,0:T(8,128)S(1)}, u32[]{:S(2)}, u32[]{:S(2)}) collective-permute-start(f32[3,2,64,128]{3,2,1,0:T(8,128)} %get-tuple-element.23.own_ref), channel_id=1, source_target_pairs={{0,1},{1,0},{2,3},{3,2},{4,5},{5,4},{6,7},{7,6},{8,9},{9,8},{10,11... | collective-permute-start | bytes 589832 | tf_op jit(solution)/shard_map/ppermute | solution.py:539
  4.4 4.4 %all-to-all-start = ((f32[16,8,128]{2,1,0:T(8,128)}), f32[16,8,128]{2,1,0:T(8,128)S(1)}, u32[]{:S(2)}, u32[]{:S(2)}) async-start(f32[16,8,128]{2,1,0:T(8,128)} %get-tuple-element.29), calls=%async_computation | async-start | bytes 131072 | tf_op jit(solution)/shard_map/all_to_all | solution.py:540
  8.9 0.9 copy-done
  9.8 0.0 collective-permute-done.other_ref
  9.8 0.3 shard_map.78
  10.1 0.5 collective-permute-start.1
  10.6 0.7 collective-permute-start.2
  11.2 0.2 collective-permute-done.1.a_in
  11.4 0.0 collective-permute-done.2.b_in
  11.4 0.3 shard_map.79
  11.8 3.4 %collective-permute-start.3 = (f32[14,8,128]{2,1,0:T(8,128)S(1)}, f32[14,8,128]{2,1,0:T(8,128)S(1)}, u32[]{:S(2)}, u32[]{:S(2)}) collective-permute-start(f32[14,8,128]{2,1,0:T(8,128)S(1)} %get-tuple-element.27), channel_id=1, source_target_pairs={{0,16},{16,0},{32,48},{48,32},{64,80},{80,64},{96,112},{112,96},{1... | collective-permute-start | bytes 172040 | tf_op jit(solution)/shard_map/ppermute | solution.py:519
  15.1 5.8 %collective-permute-start.4 = (f32[14,8,128]{2,1,0:T(8,128)S(1)}, f32[14,8,128]{2,1,0:T(8,128)S(1)}, u32[]{:S(2)}, u32[]{:S(2)}) collective-permute-start(f32[14,8,128]{2,1,0:T(8,128)S(1)} %get-tuple-element.28), channel_id=1, source_target_pairs={{16,32},{48,64},{80,96},{112,128},{144,160},{176,192},{208,224},{3... | collective-permute-start | bytes 172040 | tf_op jit(solution)/shard_map/ppermute | solution.py:520
  20.9 0.0 all-to-all-done.target_ref
  21.0 0.0 collective-permute-done.3.a_in
  21.0 3.2 %collective-permute-done.4.b_in = f32[14,8,128]{2,1,0:T(8,128)S(1)} collective-permute-done((f32[14,8,128]{2,1,0:T(8,128)S(1)}, f32[14,8,128]{2,1,0:T(8,128)S(1)}, u32[]{:S(2)}, u32[]{:S(2)}) %collective-permute-start.4) | collective-permute-done | bytes 57376 | tf_op jit(solution)/shard_map/ppermute | solution.py:520
  24.2 2.6 %shard_map.80 = (f32[3,4,80,256]{3,2,1,0:T(8,128)S(1)}, f32[2,4,80,256]{3,2,1,0:T(8,128)S(1)}, f32[16,8,128]{2,1,0:T(8,128)}) custom-call(s32[1]{0:T(128)} %bitcast.me_ref, f32[12,64,256]{2,1,0:T(8,128)S(1)} %get-tuple-element.26.ext_ref, f32[14,8,128]{2,1,0:T(8,128)S(1)} %collective-permute-done.3.a_in, f32[14,8,128]{2,1,0:T(8,128)S(1)} %collective-permute-done.4.b_in, ...), custom_call_target="tpu_custom_call" | custom-call | bytes 2670596 | tf_op jit(solution)/shard_map/pallas_call | solution.py:499
  26.8 8.4 %all-to-all-start.1 = ((f32[16,8,128]{2,1,0:T(8,128)}), f32[16,8,128]{2,1,0:T(8,128)S(1)}, u32[]{:S(2)}, u32[]{:S(2)}) async-start(f32[16,8,128]{2,1,0:T(8,128)} %get-tuple-element.31), calls=%async_computation.1 | async-start | bytes 131072 | tf_op jit(solution)/shard_map/all_to_all | solution.py:556
  35.2 2.4 %shard_map.81 = (f32[2,2,64,128]{3,2,1,0:T(8,128)S(1)}, f32[2,128]{1,0:T(2,128)S(1)}) custom-call(s32[1]{0:T(128)} %bitcast.me_ref, f32[3,4,80,256]{3,2,1,0:T(8,128)S(1)} %get-tuple-element.30.full_ref, f32[2,4,80,256]{3,2,1,0:T(8,128)S(1)} %get-tuple-element.32.first_ref, f32[16,8,128]{2,1,0:T(8,128)S(1)} %all-to-all-done.target_ref), custom_call_target="tpu_custom_call" | custom-call | flops 6553600 | bytes 1836036 | tf_op jit(solution)/shard_map/pallas_call | solution.py:499
  37.6 6.4 %all-to-all-done.1.heard_ref.info_ref = f32[16,8,128]{2,1,0:T(8,128)S(1)} async-done(((f32[16,8,128]{2,1,0:T(8,128)}), f32[16,8,128]{2,1,0:T(8,128)S(1)}, u32[]{:S(2)}, u32[]{:S(2)}) %all-to-all-start.1) | async-done | bytes 65568 | tf_op jit(solution)/shard_map/all_to_all | solution.py:556
  44.0 8.8 %build_apply.1 = (f32[16,128,2048]{2,1,0:T(8,128)S(1)}, f32[16,16,128]{2,1,0:T(8,128)S(1)}) custom-call(s32[1]{0:T(128)} %bitcast.me_ref, f32[16,8,128]{2,1,0:T(8,128)S(1)} %all-to-all-done.1.heard_ref.info_ref, f32[16,8,128]{2,1,0:T(8,128)S(1)} %all-to-all-done.target_ref, f32[2,128]{1,0:T(2,128)S(1)} %get-tuple-element.33._.kept_ref), custom_call_target="tpu_custom_call" | custom-call | flops 75497472 | bytes 16777216 | tf_op jit(solution)/shard_map/build_apply/pallas_call | solution.py:568
  52.8 17.0 %all_to_all.25.part_ref = f32[16,16,128]{2,1,0:T(8,128)S(1)} all-to-all(f32[16,16,128]{2,1,0:T(8,128)S(1)} %get-tuple-element.34), channel_id=1, replica_groups=mesh['row'=16,'col'=8,'gz'=2] {'col','gz'}, dimensions={0} | all-to-all | bytes 262144 | tf_op jit(solution)/shard_map/all_to_all | solution.py:585
  69.8 4.2 %shard_map.82 = (f32[8,64,256]{2,1,0:T(8,128)S(1)}, f32[16,8,128]{2,1,0:T(8,128)S(1)}, f32[2,4,80,256]{3,2,1,0:T(8,128)S(1)}) custom-call(s32[1]{0:T(128)} %bitcast.me_ref, f32[16,16,128]{2,1,0:T(8,128)S(1)} %all_to_all.25.part_ref, f32[16,8,128]{2,1,0:T(8,128)S(1)} %all-to-all-done.target_ref, f32[3,4,80,256]{3,2,1,0:T(8,128)S(1)} %get-tuple-element.30.full_ref, ...), custom_call_target="tpu_custom_call" | custom-call | bytes 2491396 | tf_op jit(solution)/shard_map/pallas_call | solution.py:499
  74.0 12.8 %all_to_all.26.heard_ref = f32[16,8,128]{2,1,0:T(8,128)S(1)} all-to-all(f32[16,8,128]{2,1,0:T(8,128)S(1)} %get-tuple-element.35), channel_id=1, replica_groups=mesh['row'=16,'col'=8,'gz'=2] {'row'}, dimensions={0} | all-to-all | bytes 131072 | tf_op jit(solution)/shard_map/all_to_all | solution.py:592
  86.7 3.4 %reapply.1 = f32[16,16,128]{2,1,0:T(8,128)S(1)} custom-call(s32[1]{0:T(128)} %bitcast.me_ref, f32[16,8,128]{2,1,0:T(8,128)S(1)} %all_to_all.26.heard_ref, f32[16,8,128]{2,1,0:T(8,128)S(1)} %all-to-all-done.1.heard_ref.info_ref, f32[16,128,2048]{2,1,0:T(8,128)S(1)} %get-tuple-element.36.pair_ref), custom_call_target="tpu_custom_call" | custom-call | flops 16777216 | bytes 16777216 | tf_op jit(solution)/shard_map/reapply/pallas_call | solution.py:594
  90.1 9.2 %all_to_all.27.part_ref = f32[16,16,128]{2,1,0:T(8,128)S(1)} all-to-all(f32[16,16,128]{2,1,0:T(8,128)S(1)} %reapply.1), channel_id=1, replica_groups=mesh['row'=16,'col'=8,'gz'=2] {'col','gz'}, dimensions={0} | all-to-all | bytes 262144 | tf_op jit(solution)/shard_map/all_to_all | solution.py:610
  99.3 1.1 shard_map.83
  100.4 0.9 collective-permute-start.5
  101.3 3.5 %collective-permute-start.6 = (f32[14,8,128]{2,1,0:T(8,128)S(1)}, f32[14,8,128]{2,1,0:T(8,128)S(1)}, u32[]{:S(2)}, u32[]{:S(2)}) collective-permute-start(f32[14,8,128]{2,1,0:T(8,128)S(1)} %get-tuple-element.39), channel_id=1, source_target_pairs={{16,32},{48,64},{80,96},{112,128},{144,160},{176,192},{208,224},{3... | collective-permute-start | bytes 172040 | tf_op jit(solution)/shard_map/ppermute | solution.py:520
  104.7 2.2 %shard_map.84.part_ref = f32[2,2,64,128]{3,2,1,0:T(8,128)S(1)} custom-call(s32[1]{0:T(128)} %bitcast.me_ref, f32[3,4,80,256]{3,2,1,0:T(8,128)S(1)} %get-tuple-element.30.full_ref, f32[2,4,80,256]{3,2,1,0:T(8,128)S(1)} %get-tuple-element.40.second_ref, f32[8,64,256]{2,1,0:T(8,128)S(1)} %get-tuple-element.41.spread_ref, ...), custom_call_target="tpu_custom_call" | custom-call | flops 6553600 | bytes 2424836 | tf_op jit(solution)/shard_map/pallas_call | solution.py:499
  106.9 3.4 %collective-permute-done.6.b_in = f32[14,8,128]{2,1,0:T(8,128)S(1)} collective-permute-done((f32[14,8,128]{2,1,0:T(8,128)S(1)}, f32[14,8,128]{2,1,0:T(8,128)S(1)}, u32[]{:S(2)}, u32[]{:S(2)}) %collective-permute-start.6) | collective-permute-done | bytes 57376 | tf_op jit(solution)/shard_map/ppermute | solution.py:520
  110.3 1.8 %shard_map.85 = f32[2,2,64,128]{3,2,1,0:T(8,128)} custom-call(s32[1]{0:T(128)} %bitcast.me_ref, f32[3,4,80,256]{3,2,1,0:T(8,128)S(1)} %get-tuple-element.30.full_ref, f32[14,8,128]{2,1,0:T(8,128)S(1)} %collective-permute-done.5.a_in, f32[14,8,128]{2,1,0:T(8,128)S(1)} %collective-permute-done.6.b_in, f32[2,2,64,128]{3,2,1,0:T(8,128)S(1)} %shard_map.84.part_ref), custom_call_target="tpu_custom_call" | custom-call | bytes 1359876 | tf_op jit(solution)/shard_map/pallas_call | solution.py:499
  (3 shorter events, 0.0 us)
Async XLA Ops:
  2.4 7.4 %collective-permute-start = (f32[3,2,64,128]{3,2,1,0:T(8,128)}, f32[3,2,64,128]{3,2,1,0:T(8,128)S(1)}, u32[]{:S(2)}, u32[]{:S(2)}) collective-permute-start(f32[3,2,64,128]{3,2,1,0:T(8,128)} %get-tuple-element.23.own_ref), channel_id=1, source_target_pairs={{0,1},{1,0},{2,3},{3,2},{4,5},{5,4},{6,7},{7,6},{8,9},{9,8},{10,11... | collective-permute-start | bytes 589832 | tf_op jit(solution)/shard_map/ppermute | solution.py:539
  4.4 16.5 %all-to-all-start = ((f32[16,8,128]{2,1,0:T(8,128)}), f32[16,8,128]{2,1,0:T(8,128)S(1)}, u32[]{:S(2)}, u32[]{:S(2)}) async-start(f32[16,8,128]{2,1,0:T(8,128)} %get-tuple-element.29), calls=%async_computation | async-start | bytes 131072 | tf_op jit(solution)/shard_map/all_to_all | solution.py:540
  8.8 0.9 copy-start
  10.1 1.4 %collective-permute-start.1 = (f32[64,128]{1,0:T(8,128)S(1)}, f32[64,128]{1,0:T(8,128)S(1)}, u32[]{:S(2)}, u32[]{:S(2)}) collective-permute-start(f32[64,128]{1,0:T(8,128)S(1)} %get-tuple-element.24), channel_id=1, source_target_pairs={{0,2},{2,0},{4,6},{6,4},{8,10},{10,8},{12,14},{14,12},{1,3},{3,1},... | collective-permute-start | bytes 98312 | tf_op jit(solution)/shard_map/ppermute | solution.py:519
  10.6 0.9 collective-permute-start.2
  11.8 9.2 %collective-permute-start.3 = (f32[14,8,128]{2,1,0:T(8,128)S(1)}, f32[14,8,128]{2,1,0:T(8,128)S(1)}, u32[]{:S(2)}, u32[]{:S(2)}) collective-permute-start(f32[14,8,128]{2,1,0:T(8,128)S(1)} %get-tuple-element.27), channel_id=1, source_target_pairs={{0,16},{16,0},{32,48},{48,32},{64,80},{80,64},{96,112},{112,96},{1... | collective-permute-start | bytes 172040 | tf_op jit(solution)/shard_map/ppermute | solution.py:519
  15.1 9.1 %collective-permute-start.4 = (f32[14,8,128]{2,1,0:T(8,128)S(1)}, f32[14,8,128]{2,1,0:T(8,128)S(1)}, u32[]{:S(2)}, u32[]{:S(2)}) collective-permute-start(f32[14,8,128]{2,1,0:T(8,128)S(1)} %get-tuple-element.28), channel_id=1, source_target_pairs={{16,32},{48,64},{80,96},{112,128},{144,160},{176,192},{208,224},{3... | collective-permute-start | bytes 172040 | tf_op jit(solution)/shard_map/ppermute | solution.py:520
  26.8 17.2 %all-to-all-start.1 = ((f32[16,8,128]{2,1,0:T(8,128)}), f32[16,8,128]{2,1,0:T(8,128)S(1)}, u32[]{:S(2)}, u32[]{:S(2)}) async-start(f32[16,8,128]{2,1,0:T(8,128)} %get-tuple-element.31), calls=%async_computation.1 | async-start | bytes 131072 | tf_op jit(solution)/shard_map/all_to_all | solution.py:556
  100.4 6.6 %collective-permute-start.5 = (f32[14,8,128]{2,1,0:T(8,128)S(1)}, f32[14,8,128]{2,1,0:T(8,128)S(1)}, u32[]{:S(2)}, u32[]{:S(2)}) collective-permute-start(f32[14,8,128]{2,1,0:T(8,128)S(1)} %get-tuple-element.38), channel_id=1, source_target_pairs={{0,16},{16,0},{32,48},{48,32},{64,80},{80,64},{96,112},{112,96},{1... | collective-permute-start | bytes 172040 | tf_op jit(solution)/shard_map/ppermute | solution.py:519
  101.3 9.1 %collective-permute-start.6 = (f32[14,8,128]{2,1,0:T(8,128)S(1)}, f32[14,8,128]{2,1,0:T(8,128)S(1)}, u32[]{:S(2)}, u32[]{:S(2)}) collective-permute-start(f32[14,8,128]{2,1,0:T(8,128)S(1)} %get-tuple-element.39), channel_id=1, source_target_pairs={{16,32},{48,64},{80,96},{112,128},{144,160},{176,192},{208,224},{3... | collective-permute-start | bytes 172040 | tf_op jit(solution)/shard_map/ppermute | solution.py:520

commit v6 on v5

--- a/solution.py
+++ b/solution.py
@@ -218,7 +218,7 @@
         sent_ref[k] = info
 
 
-def carry_relax(n_col, me_ref, full_ref, first_ref, target_ref, keep_ref, trace_ref, force, spare, other):
+def carry_relax(n_col, me_ref, full_ref, first_ref, target_ref, keep_ref, trace_ref, goal, force, spare, other):
     _, col, gz = place(me_ref, n_col)
     weight = full_ref.at[2]
     for m in range(2):
@@ -233,6 +233,16 @@
         for k in range(2):
             keep_ref[m, k] = other[m, 2 * gz + k, H : H + 64, 0:128]
         trace_ref[m : m + 1, :] = trace_of(two_layers(other, m, gz, H, 64), owner, 0)
+    nodes = target_ref.shape[2]
+    line = iota((8, nodes), 0)
+    at_pos = (line >= 2) & (line <= 4)
+    for t in range(target_ref.shape[0]):
+        info = target_ref[t]
+        norm = pltpu.roll(info, 1, 0) + SOFTEN
+        base = jnp.where(line == 0, norm, jnp.where(at_pos, -2.0 * info, jnp.where(line == 7, 1.0, 0.0)))
+        high, middle, low = split(base)
+        rows = jnp.concatenate([high, middle, high, low, high, middle], 0)
+        goal[:, t * nodes : (t + 1) * nodes] = rows.astype(jnp.bfloat16)
 
 
 def columns(rows, count):
@@ -254,7 +264,7 @@
             out_ref[2 * c + 1, 8 * m : 8 * m + 8, :] = near
 
 
-def build_apply(n_col, n_row, me_ref, heard_ref, target_ref, _, pair_ref, out_ref, acc, lined, goal):
+def build_apply(n_col, n_row, me_ref, heard_ref, target_ref, goal, pair_ref, out_ref, acc, lined):
     step = pl.program_id(0)
     row, col, gz = place(me_ref, n_col)
     nodes = heard_ref.shape[2]
@@ -265,13 +275,6 @@
     @pl.when(step == 0)
     def _():
         acc[...] = jnp.zeros_like(acc)
-        for t in range(blocks):
-            info = target_ref[t]
-            norm = pltpu.roll(info, 1, 0) + SOFTEN
-            base = jnp.where(line == 0, norm, jnp.where(at_pos, -2.0 * info, jnp.where(line == 7, 1.0, 0.0)))
-            high, middle, low = split(base)
-            rows = jnp.concatenate([high, middle, high, low, high, middle], 0)
-            goal[:, t * nodes : (t + 1) * nodes] = rows.astype(jnp.bfloat16)
 
     heard = heard_ref[step]
     base = jnp.where(at_pos | (line == 7), heard, jnp.where(line == 0, 1.0, 0.0))
@@ -554,13 +557,22 @@
         [field] * 2,
     )
     heard = lax.all_to_all(sent, "row", 0, 0)
-    keep, kept = run(
+    keep, kept, goal = pl.pallas_call(
         functools.partial(carry_relax, n_col),
-        [(2, 2, 64, 128), (2, nodes)],
-        [me, full, first, target],
-        [field] * 3,
-        flops=40 * size_of(field),
-    )
+        name="carry_relax",
+        out_shape=[
+            jax.ShapeDtypeStruct((2, 2, 64, 128), F32),
+            jax.ShapeDtypeStruct((2, nodes), F32),
+            jax.ShapeDtypeStruct((48, blocks * nodes), jnp.bfloat16),
+        ],
+        in_specs=[SMEM] + [VMEM] * 3,
+        out_specs=[VMEM] * 3,
+        scratch_shapes=[pltpu.VMEM(field, F32)] * 3,
+        compiler_params=pltpu.CompilerParams(vmem_limit_bytes=20 << 20),
+        cost_estimate=pl.CostEstimate(
+            flops=40 * size_of(field), bytes_accessed=4 * size_of(field), transcendentals=0
+        ),
+    )(me, full, first, target)
 
     everything = lambda shape: pl.BlockSpec(shape, lambda i: (0,) * len(shape))
     work = n_row * blocks * nodes * nodes
@@ -573,15 +585,15 @@
             jax.ShapeDtypeStruct((n_row, nodes, blocks * nodes), F32),
             jax.ShapeDtypeStruct((blocks, 16, nodes), F32),
         ],
-        in_specs=[SMEM, everything((n_row, 8, nodes)), everything((blocks, 8, nodes)), everything((2, nodes))],
+        in_specs=[SMEM, everything((n_row, 8, nodes)), everything((blocks, 8, nodes)), everything((48, blocks * nodes))],
         out_specs=[
             pl.BlockSpec((1, nodes, blocks * nodes), lambda i: (i, 0, 0)),
             everything((blocks, 16, nodes)),
         ],
-        scratch_shapes=sums + [pltpu.VMEM((48, blocks * nodes), jnp.bfloat16)],
+        scratch_shapes=sums,
         compiler_params=pltpu.CompilerParams(vmem_limit_bytes=16 << 20),
         cost_estimate=pl.CostEstimate(flops=18 * work, bytes_accessed=4 * work, transcendentals=work),
-    )(me, heard, target, kept)
+    )(me, heard, target, goal)
     partial = lax.all_to_all(partial, ("col", "gz"), 0, 0)
     before, sent, second = run(
         functools.partial(respond, n_col, n_row),

time: 113 us -> 113 us (level)
    pallas_call x0 -> x1, Pallas kernels: none -> 2.42 us  [on_device(): pl.pallas_call(functools.partial(carry_relax, n_col), name='carry_relax',...]
    pallas_call x9 -> x8, Pallas kernels: 14.8 us -> 12.4 us  [run(): pl.pallas_call(body, out_shape=[jax.ShapeDtypeStruct(o, F32) for o in out...]
where the time goes in v6:
time: 113 us; the launch traced here: 112 us
  blocking collectives  38.9 us (34%)
  starting transfers between devices  29.5 us (26%)
  Pallas kernels  28.8 us (25%)
  waiting for transfers between devices  13.2 us (12%)
    all_to_all x2, blocking collectives, on_device(): partial = lax.all_to_all(partial, ('col', 'gz'), 0, 0)  26.2 us
    all_to_all x1, blocking collectives, on_device(): again = lax.all_to_all(sent, 'row', 0, 0)  12.8 us
    pallas_call x8, Pallas kernels, run(): pl.pallas_call(body, out_shape=[jax.ShapeDtypeStruct(o, F32) for o in out...  12.4 us
    ppermute x3, starting transfers between devices, swaps(): b = lax.ppermute(b, axis, second)  9.95 us
    pallas_call x1, Pallas kernels, on_device(): pl.pallas_call(functools.partial(build_apply, n_col, n_row), name='build_...  8.79 us
    all_to_all x1, starting transfers between devices, on_device(): heard = lax.all_to_all(sent, 'row', 0, 0)  8.41 us
    ppermute x3, waiting for transfers between devices, swaps(): b = lax.ppermute(b, axis, second)  6.63 us
    all_to_all x1, waiting for transfers between devices, on_device(): heard = lax.all_to_all(sent, 'row', 0, 0)  6.34 us
  transfers between devices with their start and end apart: 9, of which 4 were waited for; matrix products, arithmetic and copies ran while one was open for 0% of the time, Pallas kernels for 5%

profile of v6, /device:TPU:8, one launch (start us, length us, event | category | flops | bytes accessed | tf_op | source)
XLA Modules:
  0.0 112.1 jit_solution(14706288981715135410)
XLA Ops:
  0.6 1.8 %prepare.1 = (f32[3,2,64,128]{3,2,1,0:T(8,128)}, f32[16,8,128]{2,1,0:T(8,128)}) custom-call(f32[8]{0:T(128)} %table_hbm.1, f32[2,2,64,128]{3,2,1,0:T(8,128)} %source_hbm.1, s32[2,64,128]{2,1,0:T(8,128)} %class_hbm.1, s32[1,128]{1,0:T(1,128)} %bitcast.3, f32[3,128]{1,0:T(4,128)} %pos_hbm.1, f32[1,128]{1,0:T(1,128)} %bitcast.4), custom_call_target="tpu_custom_call" | custom-call | tf_op jit(solution)/shard_map/prepare/pallas_call | solution.py:526
  2.4 2.0 %collective-permute-start = (f32[3,2,64,128]{3,2,1,0:T(8,128)}, f32[3,2,64,128]{3,2,1,0:T(8,128)S(1)}, u32[]{:S(2)}, u32[]{:S(2)}) collective-permute-start(f32[3,2,64,128]{3,2,1,0:T(8,128)} %get-tuple-element.24.own_ref), channel_id=1, source_target_pairs={{0,1},{1,0},{2,3},{3,2},{4,5},{5,4},{6,7},{7,6},{8,9},{9,8},{10,11... | collective-permute-start | bytes 589832 | tf_op jit(solution)/shard_map/ppermute | solution.py:542
  4.4 4.4 %all-to-all-start = ((f32[16,8,128]{2,1,0:T(8,128)}), f32[16,8,128]{2,1,0:T(8,128)S(1)}, u32[]{:S(2)}, u32[]{:S(2)}) async-start(f32[16,8,128]{2,1,0:T(8,128)} %get-tuple-element.30), calls=%async_computation | async-start | bytes 131072 | tf_op jit(solution)/shard_map/all_to_all | solution.py:543
  8.9 0.9 copy-done
  9.8 0.0 collective-permute-done.other_ref
  9.8 0.3 shard_map.78
  10.1 0.5 collective-permute-start.1
  10.6 0.7 collective-permute-start.2
  11.2 0.2 collective-permute-done.1.a_in
  11.4 0.0 collective-permute-done.2.b_in
  11.4 0.3 shard_map.79
  11.8 3.4 %collective-permute-start.3 = (f32[14,8,128]{2,1,0:T(8,128)S(1)}, f32[14,8,128]{2,1,0:T(8,128)S(1)}, u32[]{:S(2)}, u32[]{:S(2)}) collective-permute-start(f32[14,8,128]{2,1,0:T(8,128)S(1)} %get-tuple-element.28), channel_id=1, source_target_pairs={{0,16},{16,0},{32,48},{48,32},{64,80},{80,64},{96,112},{112,96},{1... | collective-permute-start | bytes 172040 | tf_op jit(solution)/shard_map/ppermute | solution.py:522
  15.1 5.8 %collective-permute-start.4 = (f32[14,8,128]{2,1,0:T(8,128)S(1)}, f32[14,8,128]{2,1,0:T(8,128)S(1)}, u32[]{:S(2)}, u32[]{:S(2)}) collective-permute-start(f32[14,8,128]{2,1,0:T(8,128)S(1)} %get-tuple-element.29), channel_id=1, source_target_pairs={{16,32},{48,64},{80,96},{112,128},{144,160},{176,192},{208,224},{3... | collective-permute-start | bytes 172040 | tf_op jit(solution)/shard_map/ppermute | solution.py:523
  20.9 0.0 all-to-all-done.target_ref
  21.0 0.0 collective-permute-done.3.a_in
  21.0 3.2 %collective-permute-done.4.b_in = f32[14,8,128]{2,1,0:T(8,128)S(1)} collective-permute-done((f32[14,8,128]{2,1,0:T(8,128)S(1)}, f32[14,8,128]{2,1,0:T(8,128)S(1)}, u32[]{:S(2)}, u32[]{:S(2)}) %collective-permute-start.4) | collective-permute-done | bytes 57376 | tf_op jit(solution)/shard_map/ppermute | solution.py:523
  24.2 2.6 %shard_map.80 = (f32[3,4,80,256]{3,2,1,0:T(8,128)S(1)}, f32[2,4,80,256]{3,2,1,0:T(8,128)S(1)}, f32[16,8,128]{2,1,0:T(8,128)}) custom-call(s32[1]{0:T(128)} %bitcast.me_ref, f32[12,64,256]{2,1,0:T(8,128)S(1)} %get-tuple-element.27.ext_ref, f32[14,8,128]{2,1,0:T(8,128)S(1)} %collective-permute-done.3.a_in, f32[14,8,128]{2,1,0:T(8,128)S(1)} %collective-permute-done.4.b_in, ...), custom_call_target="tpu_custom_call" | custom-call | bytes 2670596 | tf_op jit(solution)/shard_map/pallas_call | solution.py:502
  26.8 8.4 %all-to-all-start.1 = ((f32[16,8,128]{2,1,0:T(8,128)}), f32[16,8,128]{2,1,0:T(8,128)S(1)}, u32[]{:S(2)}, u32[]{:S(2)}) async-start(f32[16,8,128]{2,1,0:T(8,128)} %get-tuple-element.32), calls=%async_computation.1 | async-start | bytes 131072 | tf_op jit(solution)/shard_map/all_to_all | solution.py:559
  35.2 2.4 %carry_relax.1 = (f32[2,2,64,128]{3,2,1,0:T(8,128)S(1)}, f32[2,128]{1,0:T(2,128)S(1)}, bf16[48,2048]{1,0:T(8,128)(2,1)S(1)}) custom-call(s32[1]{0:T(128)} %bitcast.me_ref, f32[3,4,80,256]{3,2,1,0:T(8,128)S(1)} %get-tuple-element.31.full_ref, f32[2,4,80,256]{3,2,1,0:T(8,128)S(1)} %get-tuple-element.33.first_ref, f32[16,8,128]{2,1,0:T(8,128)S(1)} %all-to-all-done.target_ref), custom_call_target="tpu_custom_call" | custom-call | flops 6553600 | bytes 655360 | tf_op jit(solution)/shard_map/carry_relax/pallas_call | solution.py:560
  37.6 6.3 %all-to-all-done.1.heard_ref.info_ref = f32[16,8,128]{2,1,0:T(8,128)S(1)} async-done(((f32[16,8,128]{2,1,0:T(8,128)}), f32[16,8,128]{2,1,0:T(8,128)S(1)}, u32[]{:S(2)}, u32[]{:S(2)}) %all-to-all-start.1) | async-done | bytes 65568 | tf_op jit(solution)/shard_map/all_to_all | solution.py:559
  44.0 8.8 %build_apply.1 = (f32[16,128,2048]{2,1,0:T(8,128)S(1)}, f32[16,16,128]{2,1,0:T(8,128)S(1)}) custom-call(s32[1]{0:T(128)} %bitcast.me_ref, f32[16,8,128]{2,1,0:T(8,128)S(1)} %all-to-all-done.1.heard_ref.info_ref, f32[16,8,128]{2,1,0:T(8,128)S(1)} %all-to-all-done.target_ref, bf16[48,2048]{1,0:T(8,128)(2,1)S(1)} %get-tuple-element.34.goal), custom_call_target="tpu_custom_call" | custom-call | flops 75497472 | bytes 16777216 | tf_op jit(solution)/shard_map/build_apply/pallas_call | solution.py:580
  52.8 17.0 %all_to_all.25.part_ref = f32[16,16,128]{2,1,0:T(8,128)S(1)} all-to-all(f32[16,16,128]{2,1,0:T(8,128)S(1)} %get-tuple-element.35), channel_id=1, replica_groups=mesh['row'=16,'col'=8,'gz'=2] {'col','gz'}, dimensions={0} | all-to-all | bytes 262144 | tf_op jit(solution)/shard_map/all_to_all | solution.py:597
  69.8 4.2 %shard_map.81 = (f32[8,64,256]{2,1,0:T(8,128)S(1)}, f32[16,8,128]{2,1,0:T(8,128)S(1)}, f32[2,4,80,256]{3,2,1,0:T(8,128)S(1)}) custom-call(s32[1]{0:T(128)} %bitcast.me_ref, f32[16,16,128]{2,1,0:T(8,128)S(1)} %all_to_all.25.part_ref, f32[16,8,128]{2,1,0:T(8,128)S(1)} %all-to-all-done.target_ref, f32[3,4,80,256]{3,2,1,0:T(8,128)S(1)} %get-tuple-element.31.full_ref, ...), custom_call_target="tpu_custom_call" | custom-call | bytes 2491396 | tf_op jit(solution)/shard_map/pallas_call | solution.py:502
  74.0 12.8 %all_to_all.26.heard_ref = f32[16,8,128]{2,1,0:T(8,128)S(1)} all-to-all(f32[16,8,128]{2,1,0:T(8,128)S(1)} %get-tuple-element.37), channel_id=1, replica_groups=mesh['row'=16,'col'=8,'gz'=2] {'row'}, dimensions={0} | all-to-all | bytes 131072 | tf_op jit(solution)/shard_map/all_to_all | solution.py:604
  86.7 3.4 %reapply.1 = f32[16,16,128]{2,1,0:T(8,128)S(1)} custom-call(s32[1]{0:T(128)} %bitcast.me_ref, f32[16,8,128]{2,1,0:T(8,128)S(1)} %all_to_all.26.heard_ref, f32[16,8,128]{2,1,0:T(8,128)S(1)} %all-to-all-done.1.heard_ref.info_ref, f32[16,128,2048]{2,1,0:T(8,128)S(1)} %get-tuple-element.38.pair_ref), custom_call_target="tpu_custom_call" | custom-call | flops 16777216 | bytes 16777216 | tf_op jit(solution)/shard_map/reapply/pallas_call | solution.py:606
  90.1 9.2 %all_to_all.27.part_ref = f32[16,16,128]{2,1,0:T(8,128)S(1)} all-to-all(f32[16,16,128]{2,1,0:T(8,128)S(1)} %reapply.1), channel_id=1, replica_groups=mesh['row'=16,'col'=8,'gz'=2] {'col','gz'}, dimensions={0} | all-to-all | bytes 262144 | tf_op jit(solution)/shard_map/all_to_all | solution.py:622
  99.3 1.1 shard_map.82
  100.4 0.9 collective-permute-start.5
  101.2 3.5 %collective-permute-start.6 = (f32[14,8,128]{2,1,0:T(8,128)S(1)}, f32[14,8,128]{2,1,0:T(8,128)S(1)}, u32[]{:S(2)}, u32[]{:S(2)}) collective-permute-start(f32[14,8,128]{2,1,0:T(8,128)S(1)} %get-tuple-element.41), channel_id=1, source_target_pairs={{16,32},{48,64},{80,96},{112,128},{144,160},{176,192},{208,224},{3... | collective-permute-start | bytes 172040 | tf_op jit(solution)/shard_map/ppermute | solution.py:523
  104.7 2.2 %shard_map.83.part_ref = f32[2,2,64,128]{3,2,1,0:T(8,128)S(1)} custom-call(s32[1]{0:T(128)} %bitcast.me_ref, f32[3,4,80,256]{3,2,1,0:T(8,128)S(1)} %get-tuple-element.31.full_ref, f32[2,4,80,256]{3,2,1,0:T(8,128)S(1)} %get-tuple-element.42.second_ref, f32[8,64,256]{2,1,0:T(8,128)S(1)} %get-tuple-element.43.spread_ref, ...), custom_call_target="tpu_custom_call" | custom-call | flops 6553600 | bytes 2424836 | tf_op jit(solution)/shard_map/pallas_call | solution.py:502
  106.9 3.4 %collective-permute-done.6.b_in = f32[14,8,128]{2,1,0:T(8,128)S(1)} collective-permute-done((f32[14,8,128]{2,1,0:T(8,128)S(1)}, f32[14,8,128]{2,1,0:T(8,128)S(1)}, u32[]{:S(2)}, u32[]{:S(2)}) %collective-permute-start.6) | collective-permute-done | bytes 57376 | tf_op jit(solution)/shard_map/ppermute | solution.py:523
  110.3 1.8 %shard_map.84 = f32[2,2,64,128]{3,2,1,0:T(8,128)} custom-call(s32[1]{0:T(128)} %bitcast.me_ref, f32[3,4,80,256]{3,2,1,0:T(8,128)S(1)} %get-tuple-element.31.full_ref, f32[14,8,128]{2,1,0:T(8,128)S(1)} %collective-permute-done.5.a_in, f32[14,8,128]{2,1,0:T(8,128)S(1)} %collective-permute-done.6.b_in, f32[2,2,64,128]{3,2,1,0:T(8,128)S(1)} %shard_map.83.part_ref), custom_call_target="tpu_custom_call" | custom-call | bytes 1359876 | tf_op jit(solution)/shard_map/pallas_call | solution.py:502
  (3 shorter events, 0.0 us)
Async XLA Ops:
  2.4 7.4 %collective-permute-start = (f32[3,2,64,128]{3,2,1,0:T(8,128)}, f32[3,2,64,128]{3,2,1,0:T(8,128)S(1)}, u32[]{:S(2)}, u32[]{:S(2)}) collective-permute-start(f32[3,2,64,128]{3,2,1,0:T(8,128)} %get-tuple-element.24.own_ref), channel_id=1, source_target_pairs={{0,1},{1,0},{2,3},{3,2},{4,5},{5,4},{6,7},{7,6},{8,9},{9,8},{10,11... | collective-permute-start | bytes 589832 | tf_op jit(solution)/shard_map/ppermute | solution.py:542
  4.4 16.5 %all-to-all-start = ((f32[16,8,128]{2,1,0:T(8,128)}), f32[16,8,128]{2,1,0:T(8,128)S(1)}, u32[]{:S(2)}, u32[]{:S(2)}) async-start(f32[16,8,128]{2,1,0:T(8,128)} %get-tuple-element.30), calls=%async_computation | async-start | bytes 131072 | tf_op jit(solution)/shard_map/all_to_all | solution.py:543
  8.8 0.9 copy-start
  10.1 1.4 %collective-permute-start.1 = (f32[64,128]{1,0:T(8,128)S(1)}, f32[64,128]{1,0:T(8,128)S(1)}, u32[]{:S(2)}, u32[]{:S(2)}) collective-permute-start(f32[64,128]{1,0:T(8,128)S(1)} %get-tuple-element.25), channel_id=1, source_target_pairs={{0,2},{2,0},{4,6},{6,4},{8,10},{10,8},{12,14},{14,12},{1,3},{3,1},... | collective-permute-start | bytes 98312 | tf_op jit(solution)/shard_map/ppermute | solution.py:522
  10.6 0.9 collective-permute-start.2
  11.8 9.2 %collective-permute-start.3 = (f32[14,8,128]{2,1,0:T(8,128)S(1)}, f32[14,8,128]{2,1,0:T(8,128)S(1)}, u32[]{:S(2)}, u32[]{:S(2)}) collective-permute-start(f32[14,8,128]{2,1,0:T(8,128)S(1)} %get-tuple-element.28), channel_id=1, source_target_pairs={{0,16},{16,0},{32,48},{48,32},{64,80},{80,64},{96,112},{112,96},{1... | collective-permute-start | bytes 172040 | tf_op jit(solution)/shard_map/ppermute | solution.py:522
  15.1 9.1 %collective-permute-start.4 = (f32[14,8,128]{2,1,0:T(8,128)S(1)}, f32[14,8,128]{2,1,0:T(8,128)S(1)}, u32[]{:S(2)}, u32[]{:S(2)}) collective-permute-start(f32[14,8,128]{2,1,0:T(8,128)S(1)} %get-tuple-element.29), channel_id=1, source_target_pairs={{16,32},{48,64},{80,96},{112,128},{144,160},{176,192},{208,224},{3... | collective-permute-start | bytes 172040 | tf_op jit(solution)/shard_map/ppermute | solution.py:523
  26.8 17.2 %all-to-all-start.1 = ((f32[16,8,128]{2,1,0:T(8,128)}), f32[16,8,128]{2,1,0:T(8,128)S(1)}, u32[]{:S(2)}, u32[]{:S(2)}) async-start(f32[16,8,128]{2,1,0:T(8,128)} %get-tuple-element.32), calls=%async_computation.1 | async-start | bytes 131072 | tf_op jit(solution)/shard_map/all_to_all | solution.py:559
  100.4 6.6 %collective-permute-start.5 = (f32[14,8,128]{2,1,0:T(8,128)S(1)}, f32[14,8,128]{2,1,0:T(8,128)S(1)}, u32[]{:S(2)}, u32[]{:S(2)}) collective-permute-start(f32[14,8,128]{2,1,0:T(8,128)S(1)} %get-tuple-element.40), channel_id=1, source_target_pairs={{0,16},{16,0},{32,48},{48,32},{64,80},{80,64},{96,112},{112,96},{1... | collective-permute-start | bytes 172040 | tf_op jit(solution)/shard_map/ppermute | solution.py:522
  101.2 9.1 %collective-permute-start.6 = (f32[14,8,128]{2,1,0:T(8,128)S(1)}, f32[14,8,128]{2,1,0:T(8,128)S(1)}, u32[]{:S(2)}, u32[]{:S(2)}) collective-permute-start(f32[14,8,128]{2,1,0:T(8,128)S(1)} %get-tuple-element.41), channel_id=1, source_target_pairs={{16,32},{48,64},{80,96},{112,128},{144,160},{176,192},{208,224},{3... | collective-permute-start | bytes 172040 | tf_op jit(solution)/shard_map/ppermute | solution.py:523

commit v7 on v6

--- a/solution.py
+++ b/solution.py
@@ -114,17 +114,26 @@
 
 def sweep(now_ref, next_ref, force_ref, weight_ref):
     rows, lanes = now_ref.shape[2:]
+    line = iota((8, lanes), 0)
+
+    def one(m, z, low, high):
+        tiles = rows // 8
+        cells = [now_ref[m, z, 8 * i : 8 * i + 8, :] for i in range(tiles)]
+        downs = [pltpu.roll(cell, 1, 0) for cell in cells]
+        ups = [pltpu.roll(cell, 7, 0) for cell in cells]
+        for i in range(tiles):
+            beside = jnp.where(line == 0, downs[i - 1], downs[i]) + jnp.where(line == 7, ups[(i + 1) % tiles], ups[i])
+            beside = beside + (pltpu.roll(cells[i], 1, 1) + pltpu.roll(cells[i], lanes - 1, 1))
+            at = slice(8 * i, 8 * i + 8)
+            if low is not None:
+                beside = beside + now_ref[m, low, at, :]
+            if high is not None:
+                beside = beside + now_ref[m, high, at, :]
+            next_ref[m, z, at, :] = (1.0 - OMEGA) * cells[i] + (force_ref[m, z, at, :] + weight_ref[z, at, :] * beside)
 
     def image(m, carry):
         for z in range(4):
-            cell = now_ref[m, z]
-            beside = pltpu.roll(cell, 1, 0) + pltpu.roll(cell, rows - 1, 0)
-            beside = beside + (pltpu.roll(cell, 1, 1) + pltpu.roll(cell, lanes - 1, 1))
-            if z > 0:
-                beside = beside + now_ref[m, z - 1]
-            if z < 3:
-                beside = beside + now_ref[m, z + 1]
-            next_ref[m, z] = (1.0 - OMEGA) * cell + (force_ref[m, z] + weight_ref[z] * beside)
+            one(m, z, z - 1 if z > 0 else None, z + 1 if z < 3 else None)
         return carry
 
     lax.fori_loop(0, now_ref.shape[0], image, 0, unroll=rows < 64)
@@ -251,24 +260,26 @@
 
 
 def finish_apply(n_col, col, gz, acc, lined, own, out_ref):
+    nodes = own.shape[1]
     lined[...] = jnp.zeros_like(lined)
     for t in range(2 * n_col):
         mine = jnp.where(2 * col + gz == t, -0.5, 0.0).astype(F32)
         for m in range(2):
             whole = jnp.sum(acc[m, t], axis=0, keepdims=True)
-            lined[m, t + 2 : t + 3, :] = whole + mine * own[m : m + 1, :]
+            lined[t + 2, m : m + 1, :] = whole + mine * own[m : m + 1, :]
     for c in range(n_col):
-        for m in range(2):
-            near = lined[m, 2 * c : 2 * c + 8, :]
-            out_ref[2 * c, 8 * m : 8 * m + 8, :] = near
-            out_ref[2 * c + 1, 8 * m : 8 * m + 8, :] = near
-
-
-def build_apply(n_col, n_row, me_ref, heard_ref, target_ref, goal, pair_ref, out_ref, acc, lined):
+        for b in range(6):
+            near = lined[2 * c + b]
+            out_ref[2 * c, :, b * nodes : (b + 1) * nodes] = near
+            out_ref[2 * c + 1, :, b * nodes : (b + 1) * nodes] = near
+
+
+def build_apply(n_col, steps, me_ref, heard_ref, target_ref, goal, pair_ref, out_ref, acc, lined):
     step = pl.program_id(0)
     row, col, gz = place(me_ref, n_col)
     nodes = heard_ref.shape[2]
     blocks = target_ref.shape[0]
+    group = pair_ref.shape[0]
     line = iota((8, nodes), 0)
     at_pos = (line >= 2) & (line <= 4)
 
@@ -276,28 +287,32 @@
     def _():
         acc[...] = jnp.zeros_like(acc)
 
-    heard = heard_ref[step]
-    base = jnp.where(at_pos | (line == 7), heard, jnp.where(line == 0, 1.0, 0.0))
-    high, middle, low = split(base)
-    start = jnp.concatenate([high, high, middle, high, low, middle], 0).astype(jnp.bfloat16)
-    z_at = columns(heard[4:5, :], 1)[0]
-    by = columns(heard[0:2, :] * heard[6:7, :], 2)
-    for t in range(0, blocks, 2):
-        squares = lax.dot_general(
-            start,
-            goal[:, t * nodes : (t + 2) * nodes],
-            (((0,), (0,)), ((), ())),
-            preferred_element_type=F32,
-        )
-        for k in range(2):
-            dz = target_ref[t + k, 4:5, :] - z_at
-            inverse = lax.rsqrt(squares[:, k * nodes : (k + 1) * nodes])
-            pair = dz * inverse * (inverse * inverse)
-            pair_ref[0, :, (t + k) * nodes : (t + k + 1) * nodes] = pair
-            for m in range(2):
-                acc[m, t + k] = acc[m, t + k] + jnp.sum((pair * by[m]).reshape(nodes // 8, 8, nodes), axis=0)
-
-    @pl.when(step == n_row - 1)
+    starts, z_at, by = [], [], []
+    for g in range(group):
+        heard = heard_ref[step * group + g]
+        base = jnp.where(at_pos | (line == 7), heard, jnp.where(line == 0, 1.0, 0.0))
+        high, middle, low = split(base)
+        starts.append(jnp.concatenate([high, high, middle, high, low, middle], 0).astype(jnp.bfloat16))
+        z_at.append(columns(heard[4:5, :], 1)[0])
+        by.append(columns(heard[0:2, :] * heard[6:7, :], 2))
+    for g in range(group):
+        for t in range(0, blocks, 2):
+            squares = lax.dot_general(
+                starts[g],
+                goal[:, t * nodes : (t + 2) * nodes],
+                (((0,), (0,)), ((), ())),
+                preferred_element_type=F32,
+            )
+            for k in range(2):
+                dz = target_ref[t + k, 4:5, :] - z_at[g]
+                inverse = lax.rsqrt(squares[:, k * nodes : (k + 1) * nodes])
+                pair = dz * inverse * (inverse * inverse)
+                pair_ref[g, :, (t + k) * nodes : (t + k + 1) * nodes] = pair
+                for m in range(2):
+                    part = jnp.sum((pair * by[g][m]).reshape(nodes // 8, 8, nodes), axis=0)
+                    acc[m, t + k] = acc[m, t + k] + part
+
+    @pl.when(step == steps - 1)
     def _():
         finish_apply(n_col, col, gz, acc, lined, heard_ref[row], out_ref)
 
@@ -333,8 +348,8 @@
 
 
 def spread_nodes(n_col, col, part_ref, target_ref, spread_ref):
-    nodes = part_ref.shape[2]
     blocks = 2 * n_col
+    nodes = target_ref.shape[2]
     value = part_ref[0]
     for k in range(1, blocks):
         value = value + part_ref[k]
@@ -346,7 +361,7 @@
         owner = target_ref[at, 5:6, :].astype(jnp.int32)
         hit = down == owner // 128
         weighted.append(
-            jnp.concatenate([jnp.where(hit, value[8 * m + b : 8 * m + b + 1, :], 0.0) for m in range(2)], 0)
+            jnp.concatenate([jnp.where(hit, value[m : m + 1, nodes * b : nodes * (b + 1)], 0.0) for m in range(2)], 0)
         )
         lane = down == lax.rem(owner, 128)
         if b < 2:
@@ -426,7 +441,10 @@
         edge_ref[13] = side
     for m in range(2):
         value_ref[m : m + 1, :] = pick(
-            gz, (1, value.shape[1]), value[8 * m + 3 : 8 * m + 4, :], value[8 * m + 2 : 8 * m + 3, :]
+            gz,
+            (1, value_ref.shape[1]),
+            value[m : m + 1, 3 * value_ref.shape[1] : 4 * value_ref.shape[1]],
+            value[m : m + 1, 2 * value_ref.shape[1] : 3 * value_ref.shape[1]],
         )
 
 
@@ -576,19 +594,20 @@
 
     everything = lambda shape: pl.BlockSpec(shape, lambda i: (0,) * len(shape))
     work = n_row * blocks * nodes * nodes
-    sums = [pltpu.VMEM((2, blocks, 8, nodes), F32), pltpu.VMEM((2, blocks + 8, nodes), F32)]
+    sums = [pltpu.VMEM((2, blocks, 8, nodes), F32), pltpu.VMEM((blocks + 4, 2, nodes), F32)]
+    group = min(4, n_row)
     pairs, partial = pl.pallas_call(
-        functools.partial(build_apply, n_col, n_row),
+        functools.partial(build_apply, n_col, n_row // group),
         name="build_apply",
-        grid=(n_row,),
+        grid=(n_row // group,),
         out_shape=[
             jax.ShapeDtypeStruct((n_row, nodes, blocks * nodes), F32),
-            jax.ShapeDtypeStruct((blocks, 16, nodes), F32),
+            jax.ShapeDtypeStruct((blocks, 2, 6 * nodes), F32),
         ],
         in_specs=[SMEM, everything((n_row, 8, nodes)), everything((blocks, 8, nodes)), everything((48, blocks * nodes))],
         out_specs=[
-            pl.BlockSpec((1, nodes, blocks * nodes), lambda i: (i, 0, 0)),
-            everything((blocks, 16, nodes)),
+            pl.BlockSpec((group, nodes, blocks * nodes), lambda i: (i, 0, 0)),
+            everything((blocks, 2, 6 * nodes)),
         ],
         scratch_shapes=sums,
         compiler_params=pltpu.CompilerParams(vmem_limit_bytes=16 << 20),
@@ -602,19 +621,18 @@
         [field] * 3,
     )
     again = lax.all_to_all(sent, "row", 0, 0)
-    group = 2
     partial = pl.pallas_call(
         functools.partial(reapply, n_col, n_row // group),
         name="reapply",
         grid=(n_row // group,),
-        out_shape=jax.ShapeDtypeStruct((blocks, 16, nodes), F32),
+        out_shape=jax.ShapeDtypeStruct((blocks, 2, 6 * nodes), F32),
         in_specs=[
             SMEM,
             everything((n_row, 8, nodes)),
             everything((n_row, 8, nodes)),
             pl.BlockSpec((group, nodes, blocks * nodes), lambda i: (i, 0, 0)),
         ],
-        out_specs=everything((blocks, 16, nodes)),
+        out_specs=everything((blocks, 2, 6 * nodes)),
         scratch_shapes=sums + [pltpu.VMEM((n_row, 8, nodes), F32)],
         compiler_params=pltpu.CompilerParams(vmem_limit_bytes=20 << 20),
         cost_estimate=pl.CostEstimate(flops=4 * work, bytes_accessed=4 * work, transcendentals=0),

time: 113 us -> 110 us (0.973)
  Pallas kernels: 28.8 us -> 26.2 us
    pallas_call x1, Pallas kernels: 8.79 us -> 7.18 us  [on_device(): pl.pallas_call(functools.partial(build_apply, n_col, n_row // group), nam...]
where the time goes in v7:
time: 110 us; the launch traced here: 109 us
  blocking collectives  38.4 us (35%)
  starting transfers between devices  29.5 us (27%)
  Pallas kernels  26.2 us (24%)
  waiting for transfers between devices  13.5 us (12%)
    all_to_all x2, blocking collectives, on_device(): partial = lax.all_to_all(partial, ('col', 'gz'), 0, 0)  25.7 us
    all_to_all x1, blocking collectives, on_device(): again = lax.all_to_all(sent, 'row', 0, 0)  12.8 us
    pallas_call x8, Pallas kernels, run(): pl.pallas_call(body, out_shape=[jax.ShapeDtypeStruct(o, F32) for o in out...  12 us
    ppermute x3, starting transfers between devices, swaps(): b = lax.ppermute(b, axis, second)  9.95 us
    all_to_all x1, starting transfers between devices, on_device(): heard = lax.all_to_all(sent, 'row', 0, 0)  8.41 us
    pallas_call x1, Pallas kernels, on_device(): pl.pallas_call(functools.partial(build_apply, n_col, n_row // group), nam...  7.18 us
    ppermute x3, waiting for transfers between devices, swaps(): b = lax.ppermute(b, axis, second)  6.76 us
    all_to_all x1, waiting for transfers between devices, on_device(): heard = lax.all_to_all(sent, 'row', 0, 0)  6.48 us
  transfers between devices with their start and end apart: 9, of which 4 were waited for; matrix products, arithmetic and copies ran while one was open for 0% of the time, Pallas kernels for 5%

profile of v7, /device:TPU:8, one launch (start us, length us, event | category | flops | bytes accessed | tf_op | source)
XLA Modules:
  0.0 109.3 jit_solution(17838486744763278074)
XLA Ops:
  0.6 1.8 %prepare.1 = (f32[3,2,64,128]{3,2,1,0:T(8,128)}, f32[16,8,128]{2,1,0:T(8,128)}) custom-call(f32[8]{0:T(128)} %table_hbm.1, f32[2,2,64,128]{3,2,1,0:T(8,128)} %source_hbm.1, s32[2,64,128]{2,1,0:T(8,128)} %class_hbm.1, s32[1,128]{1,0:T(1,128)} %bitcast.3, f32[3,128]{1,0:T(4,128)} %pos_hbm.1, f32[1,128]{1,0:T(1,128)} %bitcast.4), custom_call_target="tpu_custom_call" | custom-call | tf_op jit(solution)/shard_map/prepare/pallas_call | solution.py:544
  2.4 2.0 %collective-permute-start = (f32[3,2,64,128]{3,2,1,0:T(8,128)}, f32[3,2,64,128]{3,2,1,0:T(8,128)S(1)}, u32[]{:S(2)}, u32[]{:S(2)}) collective-permute-start(f32[3,2,64,128]{3,2,1,0:T(8,128)} %get-tuple-element.24.own_ref), channel_id=1, source_target_pairs={{0,1},{1,0},{2,3},{3,2},{4,5},{5,4},{6,7},{7,6},{8,9},{9,8},{10,11... | collective-permute-start | bytes 589832 | tf_op jit(solution)/shard_map/ppermute | solution.py:560
  4.4 4.4 %all-to-all-start = ((f32[16,8,128]{2,1,0:T(8,128)}), f32[16,8,128]{2,1,0:T(8,128)S(1)}, u32[]{:S(2)}, u32[]{:S(2)}) async-start(f32[16,8,128]{2,1,0:T(8,128)} %get-tuple-element.30), calls=%async_computation | async-start | bytes 131072 | tf_op jit(solution)/shard_map/all_to_all | solution.py:561
  8.9 0.9 copy-done
  9.8 0.0 collective-permute-done.other_ref
  9.8 0.3 shard_map.78
  10.1 0.5 collective-permute-start.1
  10.6 0.7 collective-permute-start.2
  11.2 0.2 collective-permute-done.1.a_in
  11.4 0.0 collective-permute-done.2.b_in
  11.4 0.3 shard_map.79
  11.8 3.4 %collective-permute-start.3 = (f32[14,8,128]{2,1,0:T(8,128)S(1)}, f32[14,8,128]{2,1,0:T(8,128)S(1)}, u32[]{:S(2)}, u32[]{:S(2)}) collective-permute-start(f32[14,8,128]{2,1,0:T(8,128)S(1)} %get-tuple-element.28), channel_id=1, source_target_pairs={{0,16},{16,0},{32,48},{48,32},{64,80},{80,64},{96,112},{112,96},{1... | collective-permute-start | bytes 172040 | tf_op jit(solution)/shard_map/ppermute | solution.py:540
  15.1 5.8 %collective-permute-start.4 = (f32[14,8,128]{2,1,0:T(8,128)S(1)}, f32[14,8,128]{2,1,0:T(8,128)S(1)}, u32[]{:S(2)}, u32[]{:S(2)}) collective-permute-start(f32[14,8,128]{2,1,0:T(8,128)S(1)} %get-tuple-element.29), channel_id=1, source_target_pairs={{16,32},{48,64},{80,96},{112,128},{144,160},{176,192},{208,224},{3... | collective-permute-start | bytes 172040 | tf_op jit(solution)/shard_map/ppermute | solution.py:541
  20.9 0.0 all-to-all-done.target_ref
  21.0 0.0 collective-permute-done.3.a_in
  21.0 3.2 %collective-permute-done.4.b_in = f32[14,8,128]{2,1,0:T(8,128)S(1)} collective-permute-done((f32[14,8,128]{2,1,0:T(8,128)S(1)}, f32[14,8,128]{2,1,0:T(8,128)S(1)}, u32[]{:S(2)}, u32[]{:S(2)}) %collective-permute-start.4) | collective-permute-done | bytes 57376 | tf_op jit(solution)/shard_map/ppermute | solution.py:541
  24.2 2.5 %shard_map.80 = (f32[3,4,80,256]{3,2,1,0:T(8,128)S(1)}, f32[2,4,80,256]{3,2,1,0:T(8,128)S(1)}, f32[16,8,128]{2,1,0:T(8,128)}) custom-call(s32[1]{0:T(128)} %bitcast.me_ref, f32[12,64,256]{2,1,0:T(8,128)S(1)} %get-tuple-element.27.ext_ref, f32[14,8,128]{2,1,0:T(8,128)S(1)} %collective-permute-done.3.a_in, f32[14,8,128]{2,1,0:T(8,128)S(1)} %collective-permute-done.4.b_in, ...), custom_call_target="tpu_custom_call" | custom-call | bytes 2670596 | tf_op jit(solution)/shard_map/pallas_call | solution.py:520
  26.7 8.4 %all-to-all-start.1 = ((f32[16,8,128]{2,1,0:T(8,128)}), f32[16,8,128]{2,1,0:T(8,128)S(1)}, u32[]{:S(2)}, u32[]{:S(2)}) async-start(f32[16,8,128]{2,1,0:T(8,128)} %get-tuple-element.32), calls=%async_computation.1 | async-start | bytes 131072 | tf_op jit(solution)/shard_map/all_to_all | solution.py:577
  35.1 2.3 %carry_relax.1 = (f32[2,2,64,128]{3,2,1,0:T(8,128)S(1)}, f32[2,128]{1,0:T(2,128)S(1)}, bf16[48,2048]{1,0:T(8,128)(2,1)S(1)}) custom-call(s32[1]{0:T(128)} %bitcast.me_ref, f32[3,4,80,256]{3,2,1,0:T(8,128)S(1)} %get-tuple-element.31.full_ref, f32[2,4,80,256]{3,2,1,0:T(8,128)S(1)} %get-tuple-element.33.first_ref, f32[16,8,128]{2,1,0:T(8,128)S(1)} %all-to-all-done.target_ref), custom_call_target="tpu_custom_call" | custom-call | flops 6553600 | bytes 655360 | tf_op jit(solution)/shard_map/carry_relax/pallas_call | solution.py:578
  37.4 6.5 %all-to-all-done.1.heard_ref.info_ref = f32[16,8,128]{2,1,0:T(8,128)S(1)} async-done(((f32[16,8,128]{2,1,0:T(8,128)}), f32[16,8,128]{2,1,0:T(8,128)S(1)}, u32[]{:S(2)}, u32[]{:S(2)}) %all-to-all-start.1) | async-done | bytes 65568 | tf_op jit(solution)/shard_map/all_to_all | solution.py:577
  43.9 7.2 %build_apply.1 = (f32[16,128,2048]{2,1,0:T(8,128)S(1)}, f32[16,2,768]{2,1,0:T(2,128)S(1)}) custom-call(s32[1]{0:T(128)} %bitcast.me_ref, f32[16,8,128]{2,1,0:T(8,128)S(1)} %all-to-all-done.1.heard_ref.info_ref, f32[16,8,128]{2,1,0:T(8,128)S(1)} %all-to-all-done.target_ref, bf16[48,2048]{1,0:T(8,128)(2,1)S(1)} %get-tuple-element.34.goal), custom_call_target="tpu_custom_call" | custom-call | flops 75497472 | bytes 16777216 | tf_op jit(solution)/shard_map/build_apply/pallas_call | solution.py:599
  51.1 16.8 %all_to_all.25.part_ref = f32[16,2,768]{2,1,0:T(2,128)S(1)} all-to-all(f32[16,2,768]{2,1,0:T(2,128)S(1)} %get-tuple-element.35), channel_id=1, replica_groups=mesh['row'=16,'col'=8,'gz'=2] {'col','gz'}, dimensions={0} | all-to-all | bytes 196608 | tf_op jit(solution)/shard_map/all_to_all | solution.py:616
  67.8 4.0 %shard_map.81 = (f32[8,64,256]{2,1,0:T(8,128)S(1)}, f32[16,8,128]{2,1,0:T(8,128)S(1)}, f32[2,4,80,256]{3,2,1,0:T(8,128)S(1)}) custom-call(s32[1]{0:T(128)} %bitcast.me_ref, f32[16,2,768]{2,1,0:T(2,128)S(1)} %all_to_all.25.part_ref, f32[16,8,128]{2,1,0:T(8,128)S(1)} %all-to-all-done.target_ref, f32[3,4,80,256]{3,2,1,0:T(8,128)S(1)} %get-tuple-element.31.full_ref, ...), custom_call_target="tpu_custom_call" | custom-call | bytes 2458628 | tf_op jit(solution)/shard_map/pallas_call | solution.py:520
  71.9 12.8 %all_to_all.26.heard_ref = f32[16,8,128]{2,1,0:T(8,128)S(1)} all-to-all(f32[16,8,128]{2,1,0:T(8,128)S(1)} %get-tuple-element.37), channel_id=1, replica_groups=mesh['row'=16,'col'=8,'gz'=2] {'row'}, dimensions={0} | all-to-all | bytes 131072 | tf_op jit(solution)/shard_map/all_to_all | solution.py:623
  84.6 2.9 %reapply.1 = f32[16,2,768]{2,1,0:T(2,128)S(1)} custom-call(s32[1]{0:T(128)} %bitcast.me_ref, f32[16,8,128]{2,1,0:T(8,128)S(1)} %all_to_all.26.heard_ref, f32[16,8,128]{2,1,0:T(8,128)S(1)} %all-to-all-done.1.heard_ref.info_ref, f32[16,128,2048]{2,1,0:T(8,128)S(1)} %get-tuple-element.38.pair_ref), custom_call_target="tpu_custom_call" | custom-call | flops 16777216 | bytes 16777216 | tf_op jit(solution)/shard_map/reapply/pallas_call | solution.py:624
  87.5 8.9 %all_to_all.27.part_ref = f32[16,2,768]{2,1,0:T(2,128)S(1)} all-to-all(f32[16,2,768]{2,1,0:T(2,128)S(1)} %reapply.1), channel_id=1, replica_groups=mesh['row'=16,'col'=8,'gz'=2] {'col','gz'}, dimensions={0} | all-to-all | bytes 196608 | tf_op jit(solution)/shard_map/all_to_all | solution.py:640
  96.4 1.1 shard_map.82
  97.5 0.9 collective-permute-start.5
  98.4 3.5 %collective-permute-start.6 = (f32[14,8,128]{2,1,0:T(8,128)S(1)}, f32[14,8,128]{2,1,0:T(8,128)S(1)}, u32[]{:S(2)}, u32[]{:S(2)}) collective-permute-start(f32[14,8,128]{2,1,0:T(8,128)S(1)} %get-tuple-element.41), channel_id=1, source_target_pairs={{16,32},{48,64},{80,96},{112,128},{144,160},{176,192},{208,224},{3... | collective-permute-start | bytes 172040 | tf_op jit(solution)/shard_map/ppermute | solution.py:541
  101.9 2.0 %shard_map.83.part_ref = f32[2,2,64,128]{3,2,1,0:T(8,128)S(1)} custom-call(s32[1]{0:T(128)} %bitcast.me_ref, f32[3,4,80,256]{3,2,1,0:T(8,128)S(1)} %get-tuple-element.31.full_ref, f32[2,4,80,256]{3,2,1,0:T(8,128)S(1)} %get-tuple-element.42.second_ref, f32[8,64,256]{2,1,0:T(8,128)S(1)} %get-tuple-element.43.spread_ref, ...), custom_call_target="tpu_custom_call" | custom-call | flops 6553600 | bytes 2424836 | tf_op jit(solution)/shard_map/pallas_call | solution.py:520
  104.0 3.5 %collective-permute-done.6.b_in = f32[14,8,128]{2,1,0:T(8,128)S(1)} collective-permute-done((f32[14,8,128]{2,1,0:T(8,128)S(1)}, f32[14,8,128]{2,1,0:T(8,128)S(1)}, u32[]{:S(2)}, u32[]{:S(2)}) %collective-permute-start.6) | collective-permute-done | bytes 57376 | tf_op jit(solution)/shard_map/ppermute | solution.py:541
  107.5 1.8 %shard_map.84 = f32[2,2,64,128]{3,2,1,0:T(8,128)} custom-call(s32[1]{0:T(128)} %bitcast.me_ref, f32[3,4,80,256]{3,2,1,0:T(8,128)S(1)} %get-tuple-element.31.full_ref, f32[14,8,128]{2,1,0:T(8,128)S(1)} %collective-permute-done.5.a_in, f32[14,8,128]{2,1,0:T(8,128)S(1)} %collective-permute-done.6.b_in, f32[2,2,64,128]{3,2,1,0:T(8,128)S(1)} %shard_map.83.part_ref), custom_call_target="tpu_custom_call" | custom-call | bytes 1359876 | tf_op jit(solution)/shard_map/pallas_call | solution.py:520
  (3 shorter events, 0.0 us)
Async XLA Ops:
  2.4 7.4 %collective-permute-start = (f32[3,2,64,128]{3,2,1,0:T(8,128)}, f32[3,2,64,128]{3,2,1,0:T(8,128)S(1)}, u32[]{:S(2)}, u32[]{:S(2)}) collective-permute-start(f32[3,2,64,128]{3,2,1,0:T(8,128)} %get-tuple-element.24.own_ref), channel_id=1, source_target_pairs={{0,1},{1,0},{2,3},{3,2},{4,5},{5,4},{6,7},{7,6},{8,9},{9,8},{10,11... | collective-permute-start | bytes 589832 | tf_op jit(solution)/shard_map/ppermute | solution.py:560
  4.4 16.5 %all-to-all-start = ((f32[16,8,128]{2,1,0:T(8,128)}), f32[16,8,128]{2,1,0:T(8,128)S(1)}, u32[]{:S(2)}, u32[]{:S(2)}) async-start(f32[16,8,128]{2,1,0:T(8,128)} %get-tuple-element.30), calls=%async_computation | async-start | bytes 131072 | tf_op jit(solution)/shard_map/all_to_all | solution.py:561
  8.8 0.9 copy-start
  10.1 1.4 %collective-permute-start.1 = (f32[64,128]{1,0:T(8,128)S(1)}, f32[64,128]{1,0:T(8,128)S(1)}, u32[]{:S(2)}, u32[]{:S(2)}) collective-permute-start(f32[64,128]{1,0:T(8,128)S(1)} %get-tuple-element.25), channel_id=1, source_target_pairs={{0,2},{2,0},{4,6},{6,4},{8,10},{10,8},{12,14},{14,12},{1,3},{3,1},... | collective-permute-start | bytes 98312 | tf_op jit(solution)/shard_map/ppermute | solution.py:540
  10.6 0.9 collective-permute-start.2
  11.8 9.2 %collective-permute-start.3 = (f32[14,8,128]{2,1,0:T(8,128)S(1)}, f32[14,8,128]{2,1,0:T(8,128)S(1)}, u32[]{:S(2)}, u32[]{:S(2)}) collective-permute-start(f32[14,8,128]{2,1,0:T(8,128)S(1)} %get-tuple-element.28), channel_id=1, source_target_pairs={{0,16},{16,0},{32,48},{48,32},{64,80},{80,64},{96,112},{112,96},{1... | collective-permute-start | bytes 172040 | tf_op jit(solution)/shard_map/ppermute | solution.py:540
  15.1 9.1 %collective-permute-start.4 = (f32[14,8,128]{2,1,0:T(8,128)S(1)}, f32[14,8,128]{2,1,0:T(8,128)S(1)}, u32[]{:S(2)}, u32[]{:S(2)}) collective-permute-start(f32[14,8,128]{2,1,0:T(8,128)S(1)} %get-tuple-element.29), channel_id=1, source_target_pairs={{16,32},{48,64},{80,96},{112,128},{144,160},{176,192},{208,224},{3... | collective-permute-start | bytes 172040 | tf_op jit(solution)/shard_map/ppermute | solution.py:541
  26.7 17.2 %all-to-all-start.1 = ((f32[16,8,128]{2,1,0:T(8,128)}), f32[16,8,128]{2,1,0:T(8,128)S(1)}, u32[]{:S(2)}, u32[]{:S(2)}) async-start(f32[16,8,128]{2,1,0:T(8,128)} %get-tuple-element.32), calls=%async_computation.1 | async-start | bytes 131072 | tf_op jit(solution)/shard_map/all_to_all | solution.py:577
  97.5 6.4 %collective-permute-start.5 = (f32[14,8,128]{2,1,0:T(8,128)S(1)}, f32[14,8,128]{2,1,0:T(8,128)S(1)}, u32[]{:S(2)}, u32[]{:S(2)}) collective-permute-start(f32[14,8,128]{2,1,0:T(8,128)S(1)} %get-tuple-element.40), channel_id=1, source_target_pairs={{0,16},{16,0},{32,48},{48,32},{64,80},{80,64},{96,112},{112,96},{1... | collective-permute-start | bytes 172040 | tf_op jit(solution)/shard_map/ppermute | solution.py:540
  98.4 9.1 %collective-permute-start.6 = (f32[14,8,128]{2,1,0:T(8,128)S(1)}, f32[14,8,128]{2,1,0:T(8,128)S(1)}, u32[]{:S(2)}, u32[]{:S(2)}) collective-permute-start(f32[14,8,128]{2,1,0:T(8,128)S(1)} %get-tuple-element.41), channel_id=1, source_target_pairs={{16,32},{48,64},{80,96},{112,128},{144,160},{176,192},{208,224},{3... | collective-permute-start | bytes 172040 | tf_op jit(solution)/shard_map/ppermute | solution.py:541

commit v8 on v7

--- a/solution.py
+++ b/solution.py
@@ -227,7 +227,10 @@
         sent_ref[k] = info
 
 
-def carry_relax(n_col, me_ref, full_ref, first_ref, target_ref, keep_ref, trace_ref, goal, force, spare, other):
+def carry_relax(
+    n_col, me_ref, full_ref, first_ref, target_ref, ready_ref,
+    keep_ref, trace_ref, goal, sent_ref, force, spare, other,
+):
     _, col, gz = place(me_ref, n_col)
     weight = full_ref.at[2]
     for m in range(2):
@@ -242,6 +245,7 @@
         for k in range(2):
             keep_ref[m, k] = other[m, 2 * gz + k, H : H + 64, 0:128]
         trace_ref[m : m + 1, :] = trace_of(two_layers(other, m, gz, H, 64), owner, 0)
+    sent_ref[...] = ready_ref[...]
     nodes = target_ref.shape[2]
     line = iota((8, nodes), 0)
     at_pos = (line >= 2) & (line <= 4)
@@ -574,23 +578,24 @@
         [me, ext, a, b, target],
         [field] * 2,
     )
-    heard = lax.all_to_all(sent, "row", 0, 0)
-    keep, kept, goal = pl.pallas_call(
+    keep, kept, goal, sent = pl.pallas_call(
         functools.partial(carry_relax, n_col),
         name="carry_relax",
         out_shape=[
             jax.ShapeDtypeStruct((2, 2, 64, 128), F32),
             jax.ShapeDtypeStruct((2, nodes), F32),
             jax.ShapeDtypeStruct((48, blocks * nodes), jnp.bfloat16),
+            jax.ShapeDtypeStruct(sent.shape, F32),
         ],
-        in_specs=[SMEM] + [VMEM] * 3,
-        out_specs=[VMEM] * 3,
+        in_specs=[SMEM] + [VMEM] * 4,
+        out_specs=[VMEM] * 4,
         scratch_shapes=[pltpu.VMEM(field, F32)] * 3,
         compiler_params=pltpu.CompilerParams(vmem_limit_bytes=20 << 20),
         cost_estimate=pl.CostEstimate(
             flops=40 * size_of(field), bytes_accessed=4 * size_of(field), transcendentals=0
         ),
-    )(me, full, first, target)
+    )(me, full, first, target, sent)
+    heard = lax.all_to_all(sent, "row", 0, 0)
 
     everything = lambda shape: pl.BlockSpec(shape, lambda i: (0,) * len(shape))
     work = n_row * blocks * nodes * nodes

time: 110 us -> 111 us (level)
  blocking collectives: 38.4 us -> 55.4 us
  starting transfers between devices: 29.5 us -> 21.1 us
  waiting for transfers between devices: 13.5 us -> 6.97 us
    all_to_all x0 -> x1, blocking collectives: none -> 17 us  [on_device(): heard = lax.all_to_all(sent, 'row', 0, 0)]
    all_to_all x1 -> x0, starting transfers between devices: 8.41 us -> none  [on_device(): heard = lax.all_to_all(sent, 'row', 0, 0)]
    all_to_all x1 -> x0, waiting for transfers between devices: 6.48 us -> none  [on_device(): heard = lax.all_to_all(sent, 'row', 0, 0)]
  transfers between devices with their start and end apart: 9 -> 8, of which waited for: 4 -> 3; matrix products, arithmetic and copies ran while one was open for 0% -> 0% of each run, Pallas kernels for 5% -> 2%
where the time goes in v8:
time: 111 us
  blocking collectives  55.4 us (50%)
  Pallas kernels  25.5 us (23%)
  starting transfers between devices  21.1 us (19%)
  waiting for transfers between devices  6.97 us (6%)
    all_to_all x2, blocking collectives, on_device(): partial = lax.all_to_all(partial, ('col', 'gz'), 0, 0)  25.7 us
    all_to_all x1, blocking collectives, on_device(): heard = lax.all_to_all(sent, 'row', 0, 0)  17 us
    all_to_all x1, blocking collectives, on_device(): again = lax.all_to_all(sent, 'row', 0, 0)  12.8 us
    pallas_call x8, Pallas kernels, run(): pl.pallas_call(body, out_shape=[jax.ShapeDtypeStruct(o, F32) for o in out...  11.4 us
    ppermute x3, starting transfers between devices, swaps(): b = lax.ppermute(b, axis, second)  9.95 us
    pallas_call x1, Pallas kernels, on_device(): pl.pallas_call(functools.partial(build_apply, n_col, n_row // group), nam...  7.18 us
    ppermute x3, waiting for transfers between devices, swaps(): b = lax.ppermute(b, axis, second)  6.76 us
    ppermute x3, starting transfers between devices, swaps(): a = lax.ppermute(a, axis, first)  4.74 us
  transfers between devices with their start and end apart: 8, of which 3 were waited for; matrix products, arithmetic and copies ran while one was open for 0% of the time, Pallas kernels for 2%

profile of v8, /device:TPU:8, one launch (start us, length us, event | category | flops | bytes accessed | tf_op | source)
XLA Modules:
  0.0 110.7 jit_solution(17416879659546453639)
XLA Ops:
  0.6 1.8 %prepare.1 = (f32[3,2,64,128]{3,2,1,0:T(8,128)}, f32[16,8,128]{2,1,0:T(8,128)}) custom-call(f32[8]{0:T(128)} %table_hbm.1, f32[2,2,64,128]{3,2,1,0:T(8,128)} %source_hbm.1, s32[2,64,128]{2,1,0:T(8,128)} %class_hbm.1, s32[1,128]{1,0:T(1,128)} %bitcast.3, f32[3,128]{1,0:T(4,128)} %pos_hbm.1, f32[1,128]{1,0:T(1,128)} %bitcast.4), custom_call_target="tpu_custom_call" | custom-call | tf_op jit(solution)/shard_map/prepare/pallas_call | solution.py:548
  2.4 2.0 %collective-permute-start = (f32[3,2,64,128]{3,2,1,0:T(8,128)}, f32[3,2,64,128]{3,2,1,0:T(8,128)S(1)}, u32[]{:S(2)}, u32[]{:S(2)}) collective-permute-start(f32[3,2,64,128]{3,2,1,0:T(8,128)} %get-tuple-element.25.own_ref), channel_id=1, source_target_pairs={{0,1},{1,0},{2,3},{3,2},{4,5},{5,4},{6,7},{7,6},{8,9},{9,8},{10,11... | collective-permute-start | bytes 589832 | tf_op jit(solution)/shard_map/ppermute | solution.py:564
  4.4 4.4 %all-to-all-start = ((f32[16,8,128]{2,1,0:T(8,128)}), f32[16,8,128]{2,1,0:T(8,128)S(1)}, u32[]{:S(2)}, u32[]{:S(2)}) async-start(f32[16,8,128]{2,1,0:T(8,128)} %get-tuple-element.31), calls=%async_computation | async-start | bytes 131072 | tf_op jit(solution)/shard_map/all_to_all | solution.py:565
  8.9 0.9 copy-done
  9.8 0.0 collective-permute-done.other_ref
  9.8 0.3 shard_map.78
  10.1 0.5 collective-permute-start.1
  10.6 0.7 collective-permute-start.2
  11.2 0.2 collective-permute-done.1.a_in
  11.4 0.0 collective-permute-done.2.b_in
  11.4 0.3 shard_map.79
  11.8 3.4 %collective-permute-start.3 = (f32[14,8,128]{2,1,0:T(8,128)S(1)}, f32[14,8,128]{2,1,0:T(8,128)S(1)}, u32[]{:S(2)}, u32[]{:S(2)}) collective-permute-start(f32[14,8,128]{2,1,0:T(8,128)S(1)} %get-tuple-element.29), channel_id=1, source_target_pairs={{0,16},{16,0},{32,48},{48,32},{64,80},{80,64},{96,112},{112,96},{1... | collective-permute-start | bytes 172040 | tf_op jit(solution)/shard_map/ppermute | solution.py:544
  15.1 5.8 %collective-permute-start.4 = (f32[14,8,128]{2,1,0:T(8,128)S(1)}, f32[14,8,128]{2,1,0:T(8,128)S(1)}, u32[]{:S(2)}, u32[]{:S(2)}) collective-permute-start(f32[14,8,128]{2,1,0:T(8,128)S(1)} %get-tuple-element.30), channel_id=1, source_target_pairs={{16,32},{48,64},{80,96},{112,128},{144,160},{176,192},{208,224},{3... | collective-permute-start | bytes 172040 | tf_op jit(solution)/shard_map/ppermute | solution.py:545
  20.9 0.0 all-to-all-done.target_ref
  21.0 0.0 collective-permute-done.3.a_in
  21.0 3.2 %collective-permute-done.4.b_in = f32[14,8,128]{2,1,0:T(8,128)S(1)} collective-permute-done((f32[14,8,128]{2,1,0:T(8,128)S(1)}, f32[14,8,128]{2,1,0:T(8,128)S(1)}, u32[]{:S(2)}, u32[]{:S(2)}) %collective-permute-start.4) | collective-permute-done | bytes 57376 | tf_op jit(solution)/shard_map/ppermute | solution.py:545
  24.2 1.8 %shard_map.80 = (f32[3,4,80,256]{3,2,1,0:T(8,128)S(1)}, f32[2,4,80,256]{3,2,1,0:T(8,128)S(1)}, f32[16,8,128]{2,1,0:T(8,128)S(1)}) custom-call(s32[1]{0:T(128)} %bitcast.me_ref, f32[12,64,256]{2,1,0:T(8,128)S(1)} %get-tuple-element.28.ext_ref, f32[14,8,128]{2,1,0:T(8,128)S(1)} %collective-permute-done.3.a_in, f32[14,8,128]{2,1,0:T(8,128)S(1)} %collective-permute-done.4.b_in, ...), custom_call_target="tpu_custom_call" | custom-call | bytes 2670596 | tf_op jit(solution)/shard_map/pallas_call | solution.py:524
  26.1 2.3 %carry_relax.1 = (f32[2,2,64,128]{3,2,1,0:T(8,128)S(1)}, f32[2,128]{1,0:T(2,128)S(1)}, bf16[48,2048]{1,0:T(8,128)(2,1)S(1)}, f32[16,8,128]{2,1,0:T(8,128)S(1)}) custom-call(s32[1]{0:T(128)} %bitcast.me_ref, f32[3,4,80,256]{3,2,1,0:T(8,128)S(1)} %get-tuple-element.32.full_ref, f32[2,4,80,256]{3,2,1,0:T(8,128)S(1)} %get-tuple-element.33.first_ref, ...), custom_call_target="tpu_custom_call" | custom-call | flops 6553600 | bytes 655360 | tf_op jit(solution)/shard_map/carry_relax/pallas_call | solution.py:581
  28.4 17.0 %all_to_all.25.heard_ref.info_ref = f32[16,8,128]{2,1,0:T(8,128)S(1)} all-to-all(f32[16,8,128]{2,1,0:T(8,128)S(1)} %get-tuple-element.35), channel_id=1, replica_groups=mesh['row'=16,'col'=8,'gz'=2] {'row'}, dimensions={0} | all-to-all | bytes 131072 | tf_op jit(solution)/shard_map/all_to_all | solution.py:598
  45.3 7.2 %build_apply.1 = (f32[16,128,2048]{2,1,0:T(8,128)S(1)}, f32[16,2,768]{2,1,0:T(2,128)S(1)}) custom-call(s32[1]{0:T(128)} %bitcast.me_ref, f32[16,8,128]{2,1,0:T(8,128)S(1)} %all_to_all.25.heard_ref.info_ref, f32[16,8,128]{2,1,0:T(8,128)S(1)} %all-to-all-done.target_ref, bf16[48,2048]{1,0:T(8,128)(2,1)S(1)} %get-tuple-element.36.goal), custom_call_target="tpu_custom_call" | custom-call | flops 75497472 | bytes 16777216 | tf_op jit(solution)/shard_map/build_apply/pallas_call | solution.py:604
  52.5 16.8 %all_to_all.26.part_ref = f32[16,2,768]{2,1,0:T(2,128)S(1)} all-to-all(f32[16,2,768]{2,1,0:T(2,128)S(1)} %get-tuple-element.37), channel_id=1, replica_groups=mesh['row'=16,'col'=8,'gz'=2] {'col','gz'}, dimensions={0} | all-to-all | bytes 196608 | tf_op jit(solution)/shard_map/all_to_all | solution.py:621
  69.3 4.0 %shard_map.81 = (f32[8,64,256]{2,1,0:T(8,128)S(1)}, f32[16,8,128]{2,1,0:T(8,128)S(1)}, f32[2,4,80,256]{3,2,1,0:T(8,128)S(1)}) custom-call(s32[1]{0:T(128)} %bitcast.me_ref, f32[16,2,768]{2,1,0:T(2,128)S(1)} %all_to_all.26.part_ref, f32[16,8,128]{2,1,0:T(8,128)S(1)} %all-to-all-done.target_ref, f32[3,4,80,256]{3,2,1,0:T(8,128)S(1)} %get-tuple-element.32.full_ref, ...), custom_call_target="tpu_custom_call" | custom-call | bytes 2458628 | tf_op jit(solution)/shard_map/pallas_call | solution.py:524
  73.3 12.8 %all_to_all.27.heard_ref = f32[16,8,128]{2,1,0:T(8,128)S(1)} all-to-all(f32[16,8,128]{2,1,0:T(8,128)S(1)} %get-tuple-element.39), channel_id=1, replica_groups=mesh['row'=16,'col'=8,'gz'=2] {'row'}, dimensions={0} | all-to-all | bytes 131072 | tf_op jit(solution)/shard_map/all_to_all | solution.py:628
  86.1 2.9 %reapply.1 = f32[16,2,768]{2,1,0:T(2,128)S(1)} custom-call(s32[1]{0:T(128)} %bitcast.me_ref, f32[16,8,128]{2,1,0:T(8,128)S(1)} %all_to_all.27.heard_ref, f32[16,8,128]{2,1,0:T(8,128)S(1)} %all_to_all.25.heard_ref.info_ref, f32[16,128,2048]{2,1,0:T(8,128)S(1)} %get-tuple-element.40.pair_ref), custom_call_target="tpu_custom_call" | custom-call | flops 16777216 | bytes 16777216 | tf_op jit(solution)/shard_map/reapply/pallas_call | solution.py:629
  89.0 8.9 %all_to_all.28.part_ref = f32[16,2,768]{2,1,0:T(2,128)S(1)} all-to-all(f32[16,2,768]{2,1,0:T(2,128)S(1)} %reapply.1), channel_id=1, replica_groups=mesh['row'=16,'col'=8,'gz'=2] {'col','gz'}, dimensions={0} | all-to-all | bytes 196608 | tf_op jit(solution)/shard_map/all_to_all | solution.py:645
  97.9 1.1 shard_map.82
  99.0 0.9 collective-permute-start.5
  99.9 3.5 %collective-permute-start.6 = (f32[14,8,128]{2,1,0:T(8,128)S(1)}, f32[14,8,128]{2,1,0:T(8,128)S(1)}, u32[]{:S(2)}, u32[]{:S(2)}) collective-permute-start(f32[14,8,128]{2,1,0:T(8,128)S(1)} %get-tuple-element.43), channel_id=1, source_target_pairs={{16,32},{48,64},{80,96},{112,128},{144,160},{176,192},{208,224},{3... | collective-permute-start | bytes 172040 | tf_op jit(solution)/shard_map/ppermute | solution.py:545
  103.4 2.0 %shard_map.83.part_ref = f32[2,2,64,128]{3,2,1,0:T(8,128)S(1)} custom-call(s32[1]{0:T(128)} %bitcast.me_ref, f32[3,4,80,256]{3,2,1,0:T(8,128)S(1)} %get-tuple-element.32.full_ref, f32[2,4,80,256]{3,2,1,0:T(8,128)S(1)} %get-tuple-element.44.second_ref, f32[8,64,256]{2,1,0:T(8,128)S(1)} %get-tuple-element.45.spread_ref, ...), custom_call_target="tpu_custom_call" | custom-call | flops 6553600 | bytes 2424836 | tf_op jit(solution)/shard_map/pallas_call | solution.py:524
  105.4 0.0 collective-permute-done.5.a_in
  105.4 3.5 %collective-permute-done.6.b_in = f32[14,8,128]{2,1,0:T(8,128)S(1)} collective-permute-done((f32[14,8,128]{2,1,0:T(8,128)S(1)}, f32[14,8,128]{2,1,0:T(8,128)S(1)}, u32[]{:S(2)}, u32[]{:S(2)}) %collective-permute-start.6) | collective-permute-done | bytes 57376 | tf_op jit(solution)/shard_map/ppermute | solution.py:545
  109.0 1.8 %shard_map.84 = f32[2,2,64,128]{3,2,1,0:T(8,128)} custom-call(s32[1]{0:T(128)} %bitcast.me_ref, f32[3,4,80,256]{3,2,1,0:T(8,128)S(1)} %get-tuple-element.32.full_ref, f32[14,8,128]{2,1,0:T(8,128)S(1)} %collective-permute-done.5.a_in, f32[14,8,128]{2,1,0:T(8,128)S(1)} %collective-permute-done.6.b_in, f32[2,2,64,128]{3,2,1,0:T(8,128)S(1)} %shard_map.83.part_ref), custom_call_target="tpu_custom_call" | custom-call | bytes 1359876 | tf_op jit(solution)/shard_map/pallas_call | solution.py:524
  (2 shorter events, 0.0 us)
Async XLA Ops:
  2.4 7.4 %collective-permute-start = (f32[3,2,64,128]{3,2,1,0:T(8,128)}, f32[3,2,64,128]{3,2,1,0:T(8,128)S(1)}, u32[]{:S(2)}, u32[]{:S(2)}) collective-permute-start(f32[3,2,64,128]{3,2,1,0:T(8,128)} %get-tuple-element.25.own_ref), channel_id=1, source_target_pairs={{0,1},{1,0},{2,3},{3,2},{4,5},{5,4},{6,7},{7,6},{8,9},{9,8},{10,11... | collective-permute-start | bytes 589832 | tf_op jit(solution)/shard_map/ppermute | solution.py:564
  4.4 16.5 %all-to-all-start = ((f32[16,8,128]{2,1,0:T(8,128)}), f32[16,8,128]{2,1,0:T(8,128)S(1)}, u32[]{:S(2)}, u32[]{:S(2)}) async-start(f32[16,8,128]{2,1,0:T(8,128)} %get-tuple-element.31), calls=%async_computation | async-start | bytes 131072 | tf_op jit(solution)/shard_map/all_to_all | solution.py:565
  8.8 0.9 copy-start
  10.1 1.4 %collective-permute-start.1 = (f32[64,128]{1,0:T(8,128)S(1)}, f32[64,128]{1,0:T(8,128)S(1)}, u32[]{:S(2)}, u32[]{:S(2)}) collective-permute-start(f32[64,128]{1,0:T(8,128)S(1)} %get-tuple-element.26), channel_id=1, source_target_pairs={{0,2},{2,0},{4,6},{6,4},{8,10},{10,8},{12,14},{14,12},{1,3},{3,1},... | collective-permute-start | bytes 98312 | tf_op jit(solution)/shard_map/ppermute | solution.py:544
  10.6 0.9 collective-permute-start.2
  11.8 9.2 %collective-permute-start.3 = (f32[14,8,128]{2,1,0:T(8,128)S(1)}, f32[14,8,128]{2,1,0:T(8,128)S(1)}, u32[]{:S(2)}, u32[]{:S(2)}) collective-permute-start(f32[14,8,128]{2,1,0:T(8,128)S(1)} %get-tuple-element.29), channel_id=1, source_target_pairs={{0,16},{16,0},{32,48},{48,32},{64,80},{80,64},{96,112},{112,96},{1... | collective-permute-start | bytes 172040 | tf_op jit(solution)/shard_map/ppermute | solution.py:544
  15.1 9.1 %collective-permute-start.4 = (f32[14,8,128]{2,1,0:T(8,128)S(1)}, f32[14,8,128]{2,1,0:T(8,128)S(1)}, u32[]{:S(2)}, u32[]{:S(2)}) collective-permute-start(f32[14,8,128]{2,1,0:T(8,128)S(1)} %get-tuple-element.30), channel_id=1, source_target_pairs={{16,32},{48,64},{80,96},{112,128},{144,160},{176,192},{208,224},{3... | collective-permute-start | bytes 172040 | tf_op jit(solution)/shard_map/ppermute | solution.py:545
  99.0 6.4 %collective-permute-start.5 = (f32[14,8,128]{2,1,0:T(8,128)S(1)}, f32[14,8,128]{2,1,0:T(8,128)S(1)}, u32[]{:S(2)}, u32[]{:S(2)}) collective-permute-start(f32[14,8,128]{2,1,0:T(8,128)S(1)} %get-tuple-element.42), channel_id=1, source_target_pairs={{0,16},{16,0},{32,48},{48,32},{64,80},{80,64},{96,112},{112,96},{1... | collective-permute-start | bytes 172040 | tf_op jit(solution)/shard_map/ppermute | solution.py:544
  99.9 9.1 %collective-permute-start.6 = (f32[14,8,128]{2,1,0:T(8,128)S(1)}, f32[14,8,128]{2,1,0:T(8,128)S(1)}, u32[]{:S(2)}, u32[]{:S(2)}) collective-permute-start(f32[14,8,128]{2,1,0:T(8,128)S(1)} %get-tuple-element.43), channel_id=1, source_target_pairs={{16,32},{48,64},{80,96},{112,128},{144,160},{176,192},{208,224},{3... | collective-permute-start | bytes 172040 | tf_op jit(solution)/shard_map/ppermute | solution.py:545

commit v9 on v7

--- a/solution.py
+++ b/solution.py
@@ -112,7 +112,7 @@
     write_edges(b_ref, 0, ext_ref, 12, odd)
 
 
-def sweep(now_ref, next_ref, force_ref, weight_ref):
+def sweep(now_ref, next_ref, force_ref, weight_ref, last=False):
     rows, lanes = now_ref.shape[2:]
     line = iota((8, lanes), 0)
 
@@ -121,15 +121,19 @@
         cells = [now_ref[m, z, 8 * i : 8 * i + 8, :] for i in range(tiles)]
         downs = [pltpu.roll(cell, 1, 0) for cell in cells]
         ups = [pltpu.roll(cell, 7, 0) for cell in cells]
-        for i in range(tiles):
+        for i in range(1, 3) if last and rows < 64 else range(tiles):
             beside = jnp.where(line == 0, downs[i - 1], downs[i]) + jnp.where(line == 7, ups[(i + 1) % tiles], ups[i])
             beside = beside + (pltpu.roll(cells[i], 1, 1) + pltpu.roll(cells[i], lanes - 1, 1))
-            at = slice(8 * i, 8 * i + 8)
+            cell = cells[i]
+            at = (slice(8 * i, 8 * i + 8), slice(0, lanes))
+            if last:
+                beside, cell = beside[:, 0:128], cell[:, 0:128]
+                at = (slice(8 * i, 8 * i + 8), slice(0, 128))
             if low is not None:
-                beside = beside + now_ref[m, low, at, :]
+                beside = beside + now_ref[(m, low) + at]
             if high is not None:
-                beside = beside + now_ref[m, high, at, :]
-            next_ref[m, z, at, :] = (1.0 - OMEGA) * cells[i] + (force_ref[m, z, at, :] + weight_ref[z, at, :] * beside)
+                beside = beside + now_ref[(m, high) + at]
+            next_ref[(m, z) + at] = (1.0 - OMEGA) * cell + (force_ref[(m, z) + at] + weight_ref[(z,) + at] * beside)
 
     def image(m, carry):
         for z in range(4):
@@ -236,7 +240,7 @@
     sweep(first_ref, spare, force, weight)
     sweep(spare, other, force, weight)
     sweep(other, spare, force, weight)
-    sweep(spare, other, force, weight)
+    sweep(spare, other, force, weight, True)
     owner = target_ref[2 * col + gz, 5:6, :].astype(jnp.int32)
     for m in range(2):
         for k in range(2):
@@ -410,7 +414,7 @@
             force[m, z] = (-RELAX * second_ref[m, z]) * weight[z]
     sweep(force, other, force, weight)
     sweep(other, spare, force, weight)
-    sweep(spare, other, force, weight)
+    sweep(spare, other, force, weight, True)
     own = heard_ref[row, 5:6, :].astype(jnp.int32)
     above = heard_ref[jnp.maximum(row - 1, 0), 5:6, :].astype(jnp.int32)
     below = heard_ref[jnp.minimum(row + 1, n_row - 1), 5:6, :].astype(jnp.int32)
@@ -459,7 +463,7 @@
     sweep(second_ref, spare, force, weight)
     sweep(spare, other, force, weight)
     sweep(other, spare, force, weight)
-    sweep(spare, other, force, weight)
+    sweep(spare, other, force, weight, True)
     for m in range(2):
         for k in range(2):
             out_ref[m, k] = keep_ref[m, k] + other[m, 2 * gz + k, H : H + 64, 0:128]
@@ -498,7 +502,7 @@
     sweep(spare, other, later, weight)
     sweep(other, spare, later, weight)
     sweep(spare, other, later, weight)
-    sweep(other, spare, later, weight)
+    sweep(other, spare, later, weight, True)
     for m in range(2):
         for k in range(2):
             found = spare.at[m, 2 * gz + k]

time: 110 us -> 110 us (level)
  no operation moved by 1% of the time
where the time goes in v9:
time: 110 us; the launch traced here: 109 us
  blocking collectives  38.4 us (35%)
  starting transfers between devices  29.5 us (27%)
  Pallas kernels  26.1 us (24%)
  waiting for transfers between devices  13.5 us (12%)
    all_to_all x2, blocking collectives, on_device(): partial = lax.all_to_all(partial, ('col', 'gz'), 0, 0)  25.7 us
    all_to_all x1, blocking collectives, on_device(): again = lax.all_to_all(sent, 'row', 0, 0)  12.8 us
    pallas_call x8, Pallas kernels, run(): pl.pallas_call(body, out_shape=[jax.ShapeDtypeStruct(o, F32) for o in out...  12 us
    ppermute x3, starting transfers between devices, swaps(): b = lax.ppermute(b, axis, second)  9.95 us
    all_to_all x1, starting transfers between devices, on_device(): heard = lax.all_to_all(sent, 'row', 0, 0)  8.41 us
    pallas_call x1, Pallas kernels, on_device(): pl.pallas_call(functools.partial(build_apply, n_col, n_row // group), nam...  7.18 us
    ppermute x3, waiting for transfers between devices, swaps(): b = lax.ppermute(b, axis, second)  6.77 us
    all_to_all x1, waiting for transfers between devices, on_device(): heard = lax.all_to_all(sent, 'row', 0, 0)  6.48 us
  transfers between devices with their start and end apart: 9, of which 4 were waited for; matrix products, arithmetic and copies ran while one was open for 0% of the time, Pallas kernels for 5%

profile of v9, /device:TPU:8, one launch (start us, length us, event | category | flops | bytes accessed | tf_op | source)
XLA Modules:
  0.0 109.2 jit_solution(18418982518920145146)
XLA Ops:
  0.6 1.8 %prepare.1 = (f32[3,2,64,128]{3,2,1,0:T(8,128)}, f32[16,8,128]{2,1,0:T(8,128)}) custom-call(f32[8]{0:T(128)} %table_hbm.1, f32[2,2,64,128]{3,2,1,0:T(8,128)} %source_hbm.1, s32[2,64,128]{2,1,0:T(8,128)} %class_hbm.1, s32[1,128]{1,0:T(1,128)} %bitcast.3, f32[3,128]{1,0:T(4,128)} %pos_hbm.1, f32[1,128]{1,0:T(1,128)} %bitcast.4), custom_call_target="tpu_custom_call" | custom-call | tf_op jit(solution)/shard_map/prepare/pallas_call | solution.py:548
  2.4 2.0 %collective-permute-start = (f32[3,2,64,128]{3,2,1,0:T(8,128)}, f32[3,2,64,128]{3,2,1,0:T(8,128)S(1)}, u32[]{:S(2)}, u32[]{:S(2)}) collective-permute-start(f32[3,2,64,128]{3,2,1,0:T(8,128)} %get-tuple-element.24.own_ref), channel_id=1, source_target_pairs={{0,1},{1,0},{2,3},{3,2},{4,5},{5,4},{6,7},{7,6},{8,9},{9,8},{10,11... | collective-permute-start | bytes 589832 | tf_op jit(solution)/shard_map/ppermute | solution.py:564
  4.4 4.4 %all-to-all-start = ((f32[16,8,128]{2,1,0:T(8,128)}), f32[16,8,128]{2,1,0:T(8,128)S(1)}, u32[]{:S(2)}, u32[]{:S(2)}) async-start(f32[16,8,128]{2,1,0:T(8,128)} %get-tuple-element.30), calls=%async_computation | async-start | bytes 131072 | tf_op jit(solution)/shard_map/all_to_all | solution.py:565
  8.9 0.9 copy-done
  9.8 0.0 collective-permute-done.other_ref
  9.8 0.3 shard_map.78
  10.1 0.5 collective-permute-start.1
  10.6 0.7 collective-permute-start.2
  11.2 0.2 collective-permute-done.1.a_in
  11.4 0.0 collective-permute-done.2.b_in
  11.4 0.3 shard_map.79
  11.8 3.4 %collective-permute-start.3 = (f32[14,8,128]{2,1,0:T(8,128)S(1)}, f32[14,8,128]{2,1,0:T(8,128)S(1)}, u32[]{:S(2)}, u32[]{:S(2)}) collective-permute-start(f32[14,8,128]{2,1,0:T(8,128)S(1)} %get-tuple-element.28), channel_id=1, source_target_pairs={{0,16},{16,0},{32,48},{48,32},{64,80},{80,64},{96,112},{112,96},{1... | collective-permute-start | bytes 172040 | tf_op jit(solution)/shard_map/ppermute | solution.py:544
  15.1 5.8 %collective-permute-start.4 = (f32[14,8,128]{2,1,0:T(8,128)S(1)}, f32[14,8,128]{2,1,0:T(8,128)S(1)}, u32[]{:S(2)}, u32[]{:S(2)}) collective-permute-start(f32[14,8,128]{2,1,0:T(8,128)S(1)} %get-tuple-element.29), channel_id=1, source_target_pairs={{16,32},{48,64},{80,96},{112,128},{144,160},{176,192},{208,224},{3... | collective-permute-start | bytes 172040 | tf_op jit(solution)/shard_map/ppermute | solution.py:545
  20.9 0.0 all-to-all-done.target_ref
  21.0 0.0 collective-permute-done.3.a_in
  21.0 3.2 %collective-permute-done.4.b_in = f32[14,8,128]{2,1,0:T(8,128)S(1)} collective-permute-done((f32[14,8,128]{2,1,0:T(8,128)S(1)}, f32[14,8,128]{2,1,0:T(8,128)S(1)}, u32[]{:S(2)}, u32[]{:S(2)}) %collective-permute-start.4) | collective-permute-done | bytes 57376 | tf_op jit(solution)/shard_map/ppermute | solution.py:545
  24.2 2.5 %shard_map.80 = (f32[3,4,80,256]{3,2,1,0:T(8,128)S(1)}, f32[2,4,80,256]{3,2,1,0:T(8,128)S(1)}, f32[16,8,128]{2,1,0:T(8,128)}) custom-call(s32[1]{0:T(128)} %bitcast.me_ref, f32[12,64,256]{2,1,0:T(8,128)S(1)} %get-tuple-element.27.ext_ref, f32[14,8,128]{2,1,0:T(8,128)S(1)} %collective-permute-done.3.a_in, f32[14,8,128]{2,1,0:T(8,128)S(1)} %collective-permute-done.4.b_in, ...), custom_call_target="tpu_custom_call" | custom-call | bytes 2670596 | tf_op jit(solution)/shard_map/pallas_call | solution.py:524
  26.7 8.4 %all-to-all-start.1 = ((f32[16,8,128]{2,1,0:T(8,128)}), f32[16,8,128]{2,1,0:T(8,128)S(1)}, u32[]{:S(2)}, u32[]{:S(2)}) async-start(f32[16,8,128]{2,1,0:T(8,128)} %get-tuple-element.32), calls=%async_computation.1 | async-start | bytes 131072 | tf_op jit(solution)/shard_map/all_to_all | solution.py:581
  35.1 2.3 %carry_relax.1 = (f32[2,2,64,128]{3,2,1,0:T(8,128)S(1)}, f32[2,128]{1,0:T(2,128)S(1)}, bf16[48,2048]{1,0:T(8,128)(2,1)S(1)}) custom-call(s32[1]{0:T(128)} %bitcast.me_ref, f32[3,4,80,256]{3,2,1,0:T(8,128)S(1)} %get-tuple-element.31.full_ref, f32[2,4,80,256]{3,2,1,0:T(8,128)S(1)} %get-tuple-element.33.first_ref, f32[16,8,128]{2,1,0:T(8,128)S(1)} %all-to-all-done.target_ref), custom_call_target="tpu_custom_call" | custom-call | flops 6553600 | bytes 655360 | tf_op jit(solution)/shard_map/carry_relax/pallas_call | solution.py:582
  37.4 6.5 %all-to-all-done.1.heard_ref.info_ref = f32[16,8,128]{2,1,0:T(8,128)S(1)} async-done(((f32[16,8,128]{2,1,0:T(8,128)}), f32[16,8,128]{2,1,0:T(8,128)S(1)}, u32[]{:S(2)}, u32[]{:S(2)}) %all-to-all-start.1) | async-done | bytes 65568 | tf_op jit(solution)/shard_map/all_to_all | solution.py:581
  43.9 7.2 %build_apply.1 = (f32[16,128,2048]{2,1,0:T(8,128)S(1)}, f32[16,2,768]{2,1,0:T(2,128)S(1)}) custom-call(s32[1]{0:T(128)} %bitcast.me_ref, f32[16,8,128]{2,1,0:T(8,128)S(1)} %all-to-all-done.1.heard_ref.info_ref, f32[16,8,128]{2,1,0:T(8,128)S(1)} %all-to-all-done.target_ref, bf16[48,2048]{1,0:T(8,128)(2,1)S(1)} %get-tuple-element.34.goal), custom_call_target="tpu_custom_call" | custom-call | flops 75497472 | bytes 16777216 | tf_op jit(solution)/shard_map/build_apply/pallas_call | solution.py:603
  51.1 16.8 %all_to_all.25.part_ref = f32[16,2,768]{2,1,0:T(2,128)S(1)} all-to-all(f32[16,2,768]{2,1,0:T(2,128)S(1)} %get-tuple-element.35), channel_id=1, replica_groups=mesh['row'=16,'col'=8,'gz'=2] {'col','gz'}, dimensions={0} | all-to-all | bytes 196608 | tf_op jit(solution)/shard_map/all_to_all | solution.py:620
  67.8 4.0 %shard_map.81 = (f32[8,64,256]{2,1,0:T(8,128)S(1)}, f32[16,8,128]{2,1,0:T(8,128)S(1)}, f32[2,4,80,256]{3,2,1,0:T(8,128)S(1)}) custom-call(s32[1]{0:T(128)} %bitcast.me_ref, f32[16,2,768]{2,1,0:T(2,128)S(1)} %all_to_all.25.part_ref, f32[16,8,128]{2,1,0:T(8,128)S(1)} %all-to-all-done.target_ref, f32[3,4,80,256]{3,2,1,0:T(8,128)S(1)} %get-tuple-element.31.full_ref, ...), custom_call_target="tpu_custom_call" | custom-call | bytes 2458628 | tf_op jit(solution)/shard_map/pallas_call | solution.py:524
  71.9 12.8 %all_to_all.26.heard_ref = f32[16,8,128]{2,1,0:T(8,128)S(1)} all-to-all(f32[16,8,128]{2,1,0:T(8,128)S(1)} %get-tuple-element.37), channel_id=1, replica_groups=mesh['row'=16,'col'=8,'gz'=2] {'row'}, dimensions={0} | all-to-all | bytes 131072 | tf_op jit(solution)/shard_map/all_to_all | solution.py:627
  84.6 2.9 %reapply.1 = f32[16,2,768]{2,1,0:T(2,128)S(1)} custom-call(s32[1]{0:T(128)} %bitcast.me_ref, f32[16,8,128]{2,1,0:T(8,128)S(1)} %all_to_all.26.heard_ref, f32[16,8,128]{2,1,0:T(8,128)S(1)} %all-to-all-done.1.heard_ref.info_ref, f32[16,128,2048]{2,1,0:T(8,128)S(1)} %get-tuple-element.38.pair_ref), custom_call_target="tpu_custom_call" | custom-call | flops 16777216 | bytes 16777216 | tf_op jit(solution)/shard_map/reapply/pallas_call | solution.py:628
  87.5 8.9 %all_to_all.27.part_ref = f32[16,2,768]{2,1,0:T(2,128)S(1)} all-to-all(f32[16,2,768]{2,1,0:T(2,128)S(1)} %reapply.1), channel_id=1, replica_groups=mesh['row'=16,'col'=8,'gz'=2] {'col','gz'}, dimensions={0} | all-to-all | bytes 196608 | tf_op jit(solution)/shard_map/all_to_all | solution.py:644
  96.4 1.1 shard_map.82
  97.5 0.9 collective-permute-start.5
  98.4 3.5 %collective-permute-start.6 = (f32[14,8,128]{2,1,0:T(8,128)S(1)}, f32[14,8,128]{2,1,0:T(8,128)S(1)}, u32[]{:S(2)}, u32[]{:S(2)}) collective-permute-start(f32[14,8,128]{2,1,0:T(8,128)S(1)} %get-tuple-element.41), channel_id=1, source_target_pairs={{16,32},{48,64},{80,96},{112,128},{144,160},{176,192},{208,224},{3... | collective-permute-start | bytes 172040 | tf_op jit(solution)/shard_map/ppermute | solution.py:545
  101.9 2.0 %shard_map.83.part_ref = f32[2,2,64,128]{3,2,1,0:T(8,128)S(1)} custom-call(s32[1]{0:T(128)} %bitcast.me_ref, f32[3,4,80,256]{3,2,1,0:T(8,128)S(1)} %get-tuple-element.31.full_ref, f32[2,4,80,256]{3,2,1,0:T(8,128)S(1)} %get-tuple-element.42.second_ref, f32[8,64,256]{2,1,0:T(8,128)S(1)} %get-tuple-element.43.spread_ref, ...), custom_call_target="tpu_custom_call" | custom-call | flops 6553600 | bytes 2424836 | tf_op jit(solution)/shard_map/pallas_call | solution.py:524
  104.0 3.5 %collective-permute-done.6.b_in = f32[14,8,128]{2,1,0:T(8,128)S(1)} collective-permute-done((f32[14,8,128]{2,1,0:T(8,128)S(1)}, f32[14,8,128]{2,1,0:T(8,128)S(1)}, u32[]{:S(2)}, u32[]{:S(2)}) %collective-permute-start.6) | collective-permute-done | bytes 57376 | tf_op jit(solution)/shard_map/ppermute | solution.py:545
  107.5 1.7 %shard_map.84 = f32[2,2,64,128]{3,2,1,0:T(8,128)} custom-call(s32[1]{0:T(128)} %bitcast.me_ref, f32[3,4,80,256]{3,2,1,0:T(8,128)S(1)} %get-tuple-element.31.full_ref, f32[14,8,128]{2,1,0:T(8,128)S(1)} %collective-permute-done.5.a_in, f32[14,8,128]{2,1,0:T(8,128)S(1)} %collective-permute-done.6.b_in, f32[2,2,64,128]{3,2,1,0:T(8,128)S(1)} %shard_map.83.part_ref), custom_call_target="tpu_custom_call" | custom-call | bytes 1359876 | tf_op jit(solution)/shard_map/pallas_call | solution.py:524
  (3 shorter events, 0.0 us)
Async XLA Ops:
  2.4 7.4 %collective-permute-start = (f32[3,2,64,128]{3,2,1,0:T(8,128)}, f32[3,2,64,128]{3,2,1,0:T(8,128)S(1)}, u32[]{:S(2)}, u32[]{:S(2)}) collective-permute-start(f32[3,2,64,128]{3,2,1,0:T(8,128)} %get-tuple-element.24.own_ref), channel_id=1, source_target_pairs={{0,1},{1,0},{2,3},{3,2},{4,5},{5,4},{6,7},{7,6},{8,9},{9,8},{10,11... | collective-permute-start | bytes 589832 | tf_op jit(solution)/shard_map/ppermute | solution.py:564
  4.4 16.5 %all-to-all-start = ((f32[16,8,128]{2,1,0:T(8,128)}), f32[16,8,128]{2,1,0:T(8,128)S(1)}, u32[]{:S(2)}, u32[]{:S(2)}) async-start(f32[16,8,128]{2,1,0:T(8,128)} %get-tuple-element.30), calls=%async_computation | async-start | bytes 131072 | tf_op jit(solution)/shard_map/all_to_all | solution.py:565
  8.8 0.9 copy-start
  10.1 1.4 %collective-permute-start.1 = (f32[64,128]{1,0:T(8,128)S(1)}, f32[64,128]{1,0:T(8,128)S(1)}, u32[]{:S(2)}, u32[]{:S(2)}) collective-permute-start(f32[64,128]{1,0:T(8,128)S(1)} %get-tuple-element.25), channel_id=1, source_target_pairs={{0,2},{2,0},{4,6},{6,4},{8,10},{10,8},{12,14},{14,12},{1,3},{3,1},... | collective-permute-start | bytes 98312 | tf_op jit(solution)/shard_map/ppermute | solution.py:544
  10.6 0.9 collective-permute-start.2
  11.8 9.2 %collective-permute-start.3 = (f32[14,8,128]{2,1,0:T(8,128)S(1)}, f32[14,8,128]{2,1,0:T(8,128)S(1)}, u32[]{:S(2)}, u32[]{:S(2)}) collective-permute-start(f32[14,8,128]{2,1,0:T(8,128)S(1)} %get-tuple-element.28), channel_id=1, source_target_pairs={{0,16},{16,0},{32,48},{48,32},{64,80},{80,64},{96,112},{112,96},{1... | collective-permute-start | bytes 172040 | tf_op jit(solution)/shard_map/ppermute | solution.py:544
  15.1 9.1 %collective-permute-start.4 = (f32[14,8,128]{2,1,0:T(8,128)S(1)}, f32[14,8,128]{2,1,0:T(8,128)S(1)}, u32[]{:S(2)}, u32[]{:S(2)}) collective-permute-start(f32[14,8,128]{2,1,0:T(8,128)S(1)} %get-tuple-element.29), channel_id=1, source_target_pairs={{16,32},{48,64},{80,96},{112,128},{144,160},{176,192},{208,224},{3... | collective-permute-start | bytes 172040 | tf_op jit(solution)/shard_map/ppermute | solution.py:545
  26.7 17.2 %all-to-all-start.1 = ((f32[16,8,128]{2,1,0:T(8,128)}), f32[16,8,128]{2,1,0:T(8,128)S(1)}, u32[]{:S(2)}, u32[]{:S(2)}) async-start(f32[16,8,128]{2,1,0:T(8,128)} %get-tuple-element.32), calls=%async_computation.1 | async-start | bytes 131072 | tf_op jit(solution)/shard_map/all_to_all | solution.py:581
  97.5 6.4 %collective-permute-start.5 = (f32[14,8,128]{2,1,0:T(8,128)S(1)}, f32[14,8,128]{2,1,0:T(8,128)S(1)}, u32[]{:S(2)}, u32[]{:S(2)}) collective-permute-start(f32[14,8,128]{2,1,0:T(8,128)S(1)} %get-tuple-element.40), channel_id=1, source_target_pairs={{0,16},{16,0},{32,48},{48,32},{64,80},{80,64},{96,112},{112,96},{1... | collective-permute-start | bytes 172040 | tf_op jit(solution)/shard_map/ppermute | solution.py:544
  98.4 9.1 %collective-permute-start.6 = (f32[14,8,128]{2,1,0:T(8,128)S(1)}, f32[14,8,128]{2,1,0:T(8,128)S(1)}, u32[]{:S(2)}, u32[]{:S(2)}) collective-permute-start(f32[14,8,128]{2,1,0:T(8,128)S(1)} %get-tuple-element.41), channel_id=1, source_target_pairs={{16,32},{48,64},{80,96},{112,128},{144,160},{176,192},{208,224},{3... | collective-permute-start | bytes 172040 | tf_op jit(solution)/shard_map/ppermute | solution.py:545
